TPU v7x, 32 devices: a whole 2x2x4 slice. The times are simulated.
32 devices in a mesh: dp: 16 (over z, y, core), seq: 2 (over x).
Axes of the slice: x: 2, y: 2, z: 4, core: 2. Of those that a mesh axis runs over, the one named last changes fastest.
Arguments:
- targets: bfloat16 [256, 96, 768], P(('dp', 'seq')), may hold values from -6 to 6
- memory: bfloat16 [256, 1024, 768], P(('dp', 'seq')), may hold values from -6 to 6
- mem_lengths: int32 [256], P(('dp', 'seq')), may hold values from 512 to 1024, as said below
- buckets: int32 [96, 96], replicated, may hold values from 0 to 31
- cotangent: bfloat16 [256, 96, 768], P(('dp', 'seq')), may hold values from -6 to 6
- gain_self: bfloat16 [768], P(('dp', 'seq')), may hold values from 0.5 to 1.5
- gain_cross: bfloat16 [768], P(('dp', 'seq')), may hold values from 0.5 to 1.5
- gain_feed: bfloat16 [768], P(('dp', 'seq')), may hold values from 0.5 to 1.5
- self_query: bfloat16 [768, 768], P(('dp', 'seq')), may hold values from -0.0546875 to 0.0546875
- self_key: bfloat16 [768, 768], P(('dp', 'seq')), may hold values from -0.21875 to 0.21875
- self_value: bfloat16 [768, 768], P(('dp', 'seq')), may hold values from -0.21875 to 0.21875
- self_output: bfloat16 [768, 768], P(('dp', 'seq')), may hold values from -0.625 to 0.625
- cross_query: bfloat16 [768, 768], P(('dp', 'seq')), may hold values from -0.0546875 to 0.0546875
- cross_key: bfloat16 [768, 768], P(('dp', 'seq')), may hold values from -0.21875 to 0.21875
- cross_value: bfloat16 [768, 768], P(('dp', 'seq')), may hold values from -0.21875 to 0.21875
- cross_output: bfloat16 [768, 768], P(('dp', 'seq')), may hold values from -0.875 to 0.875
- gate_weight: bfloat16 [768, 2048], P(('dp', 'seq')), may hold values from -0.21875 to 0.21875
- up_weight: bfloat16 [768, 2048], P(('dp', 'seq')), may hold values from -0.21875 to 0.21875
- down_weight: bfloat16 [2048, 768], P(('dp', 'seq')), may hold values from -0.125 to 0.125
- bias_table: bfloat16 [32, 12], replicated, may hold values from -4 to 4
Outputs:
- outputs: bfloat16 [256, 96, 768], P(('dp', 'seq'))
- target_grad: bfloat16 [256, 96, 768], P(('dp', 'seq'))
- memory_grad: bfloat16 [256, 1024, 768], P(('dp', 'seq'))
- grad_gain_self: float32 [768], P(('dp', 'seq'))
- grad_gain_cross: float32 [768], P(('dp', 'seq'))
- grad_gain_feed: float32 [768], P(('dp', 'seq'))
- grad_self_query: float32 [768, 768], P(('dp', 'seq'))
- grad_self_key: float32 [768, 768], P(('dp', 'seq'))
- grad_self_value: float32 [768, 768], P(('dp', 'seq'))
- grad_self_output: float32 [768, 768], P(('dp', 'seq'))
- grad_cross_query: float32 [768, 768], P(('dp', 'seq'))
- grad_cross_key: float32 [768, 768], P(('dp', 'seq'))
- grad_cross_value: float32 [768, 768], P(('dp', 'seq'))
- grad_cross_output: float32 [768, 768], P(('dp', 'seq'))
- grad_gate_weight: float32 [768, 2048], P(('dp', 'seq'))
- grad_up_weight: float32 [768, 2048], P(('dp', 'seq'))
- grad_down_weight: float32 [2048, 768], P(('dp', 'seq'))
- grad_bias_table: float32 [32, 12], replicated
Inputs may be any that keep to these rules, and one draw needn't show every extreme that they name: `mem_lengths`: each sequence has 512 or 1024 valid memory slots, the first ones; exactly half of all sequences have each.
All inputs are finite; a program needn't handle non-finite values.
Results may differ from a plain program's by a relative error of at most 0.025.
The roundings to bfloat16 on the way count: a program that leaves them out, or rounds other values in their place, can miss the bound.
Values may be sent and summed in bfloat16 or wider, within the bound.
No kernel may reach another device: no remote copies, remote signals or barrier semaphores. Data moves between devices by JAX's collectives and lax.ppermute only.
A program may use at most 320 MiB of HBM per device.

v0:
```python
import jax
import jax.numpy as jnp
from jax import lax
from jax.sharding import PartitionSpec as P

epsilon = 1e-06
masked_out = -1e30
highest = lax.Precision.HIGHEST


def rms_norm(values, gain_row):
    return (
        values * lax.rsqrt(jnp.mean(values * values, axis=-1, keepdims=True) + epsilon) * gain_row
    )


def gelu_tanh(values):
    return jax.nn.gelu(values, approximate=True)


def matmul(left_side, right_side):
    return jnp.dot(left_side, right_side, preferred_element_type=jnp.float32)


def through(grad_in, weight):
    return lax.dot_general(
        grad_in, weight, (((1,), (1,)), ((), ())), preferred_element_type=jnp.float32
    )


def summed(left_side, right_side):
    return lax.dot_general(
        left_side, right_side, (((0,), (0,)), ((), ())), preferred_element_type=jnp.float32
    )


def norm_pullback(values, gain_row, grad_in):
    normed, pullback = jax.vjp(rms_norm, values, gain_row)
    grad_values, grad_gain = pullback(grad_in)
    return (grad_values, grad_gain)


def attend_forward(queries, key_rows, value_rows, extra_bias, keep_mask):
    scores = (
        jnp.einsum("bihe,bjhe->bhij", queries, key_rows, preferred_element_type=jnp.float32)
        + extra_bias
    )
    scores = jnp.where(keep_mask, scores, masked_out)
    row_max = jnp.max(scores, axis=-1, keepdims=True)
    exp_terms = jnp.exp(scores - row_max)
    exp_total = jnp.sum(exp_terms, axis=-1, keepdims=True)
    prob_rows = exp_terms / exp_total
    log_total = row_max + jnp.log(exp_total)
    weights_low = prob_rows.astype(jnp.bfloat16)
    context = jnp.einsum(
        "bhij,bjhe->bihe", weights_low, value_rows, preferred_element_type=jnp.float32
    ).astype(jnp.bfloat16)
    return (prob_rows, log_total, context)


def attend_backward(prob_rows, queries, key_rows, value_rows, grad_context):
    weights_low = prob_rows.astype(jnp.bfloat16)
    grad_probs = jnp.einsum(
        "bihe,bjhe->bhij", grad_context, value_rows, preferred_element_type=jnp.float32
    )
    grad_values = jnp.einsum(
        "bhij,bihe->bjhe", weights_low, grad_context, preferred_element_type=jnp.float32
    ).astype(jnp.bfloat16)
    grad_scores = (
        prob_rows * (grad_probs - jnp.sum(grad_probs * prob_rows, axis=-1, keepdims=True))
    ).astype(jnp.bfloat16)
    grad_queries = jnp.einsum(
        "bhij,bjhe->bihe", grad_scores, key_rows, preferred_element_type=jnp.float32
    ).astype(jnp.bfloat16)
    grad_keys = jnp.einsum(
        "bhij,bihe->bjhe", grad_scores, queries, preferred_element_type=jnp.float32
    ).astype(jnp.bfloat16)
    return (grad_scores, grad_queries, grad_keys, grad_values)


def on_device(
    targets,
    memory,
    mem_lengths,
    buckets,
    cotangent,
    gain_self,
    gain_cross,
    gain_feed,
    self_query,
    self_key,
    self_value,
    self_output,
    cross_query,
    cross_key,
    cross_value,
    cross_output,
    gate_weight,
    up_weight,
    down_weight,
    bias_table,
):
    gathered = (
        lax.all_gather(gain_self, ("dp", "seq"), axis=0, tiled=True),
        lax.all_gather(gain_cross, ("dp", "seq"), axis=0, tiled=True),
        lax.all_gather(gain_feed, ("dp", "seq"), axis=0, tiled=True),
        lax.all_gather(self_query, ("dp", "seq"), axis=0, tiled=True),
        lax.all_gather(self_key, ("dp", "seq"), axis=0, tiled=True),
        lax.all_gather(self_value, ("dp", "seq"), axis=0, tiled=True),
        lax.all_gather(self_output, ("dp", "seq"), axis=0, tiled=True),
        lax.all_gather(cross_query, ("dp", "seq"), axis=0, tiled=True),
        lax.all_gather(cross_key, ("dp", "seq"), axis=0, tiled=True),
        lax.all_gather(cross_value, ("dp", "seq"), axis=0, tiled=True),
        lax.all_gather(cross_output, ("dp", "seq"), axis=0, tiled=True),
        lax.all_gather(gate_weight, ("dp", "seq"), axis=0, tiled=True),
        lax.all_gather(up_weight, ("dp", "seq"), axis=0, tiled=True),
        lax.all_gather(down_weight, ("dp", "seq"), axis=0, tiled=True),
    )
    (
        full_gain_self,
        full_gain_cross,
        full_gain_feed,
        full_query,
        full_key,
        full_value,
        full_output,
        side_query,
        side_key,
        side_value,
        side_output,
        full_gate,
        full_up,
        full_down,
    ) = gathered
    scale_self = full_gain_self.astype(jnp.float32)
    scale_cross = full_gain_cross.astype(jnp.float32)
    scale_feed = full_gain_feed.astype(jnp.float32)
    batch_size, target_len, model_width = targets.shape
    memory_len = memory.shape[1]
    bucket_count, head_count = bias_table.shape
    head_size = model_width // head_count
    row_count = batch_size * target_len

    def to_heads(values):
        return values.reshape(batch_size, values.shape[0] // batch_size, head_count, head_size)

    def from_heads(values):
        return values.reshape(-1, model_width)

    inputs = targets.astype(jnp.float32).reshape(row_count, model_width)
    grad_rows = cotangent.reshape(row_count, model_width)
    normed_one = rms_norm(inputs, scale_self).astype(jnp.bfloat16)
    queries = matmul(normed_one, full_query).astype(jnp.bfloat16)
    key_rows = matmul(normed_one, full_key).astype(jnp.bfloat16)
    value_rows = matmul(normed_one, full_value).astype(jnp.bfloat16)
    bucket_hot = (
        buckets[:, :, None] == lax.broadcasted_iota(jnp.int32, (1, 1, bucket_count), 2)
    ).reshape(target_len * target_len, bucket_count)
    position_bias = (
        matmul(bucket_hot.astype(jnp.bfloat16), bias_table)
        .reshape(target_len, target_len, head_count)
        .transpose(2, 0, 1)
    )
    causal = lax.broadcasted_iota(jnp.int32, (target_len, target_len), 1) <= lax.broadcasted_iota(
        jnp.int32, (target_len, target_len), 0
    )
    self_probs, self_logsum, self_heads = attend_forward(
        to_heads(queries), to_heads(key_rows), to_heads(value_rows), position_bias, causal
    )
    self_context = from_heads(self_heads)
    after_self = inputs + matmul(self_context, full_output)
    normed_two = rms_norm(after_self, scale_cross).astype(jnp.bfloat16)
    side_queries = matmul(normed_two, side_query).astype(jnp.bfloat16)
    memory_flat = memory.reshape(-1, model_width)
    mem_keys = matmul(memory_flat, side_key).astype(jnp.bfloat16)
    mem_values = matmul(memory_flat, side_value).astype(jnp.bfloat16)
    valid_keys = (
        lax.broadcasted_iota(jnp.int32, (batch_size, memory_len), 1) < mem_lengths[:, None]
    )[:, None, None, :]
    mem_key_heads = mem_keys.reshape(batch_size, memory_len, head_count, head_size)
    mem_value_heads = mem_values.reshape(batch_size, memory_len, head_count, head_size)
    cross_probs, cross_logsum, cross_heads = attend_forward(
        to_heads(side_queries), mem_key_heads, mem_value_heads, 0.0, valid_keys
    )
    cross_context = from_heads(cross_heads)
    after_cross = after_self + matmul(cross_context, side_output)
    normed_three = rms_norm(after_cross, scale_feed).astype(jnp.bfloat16)
    gate_out = matmul(normed_three, full_gate)
    up_out = matmul(normed_three, full_up)
    activated, gelu_pull = jax.vjp(gelu_tanh, gate_out)
    hidden = (activated * up_out).astype(jnp.bfloat16)
    result = after_cross + matmul(hidden, full_down)
    outputs = result.astype(jnp.bfloat16).reshape(targets.shape)
    total_down = summed(hidden, grad_rows)
    grad_hidden = through(grad_rows, full_down)
    grad_gate = gelu_pull(grad_hidden * up_out)[0].astype(jnp.bfloat16)
    grad_up = (grad_hidden * activated).astype(jnp.bfloat16)
    total_gate = summed(normed_three, grad_gate)
    total_up = summed(normed_three, grad_up)
    grad_normed_three = through(grad_gate, full_gate) + through(grad_up, full_up)
    grad_feed_in, total_gain_feed = norm_pullback(after_cross, scale_feed, grad_normed_three)
    grad_after_cross = grad_rows.astype(jnp.float32) + grad_feed_in
    low_cross = grad_after_cross.astype(jnp.bfloat16)
    total_cross_output = summed(cross_context, low_cross)
    grad_cross_context = through(low_cross, side_output).astype(jnp.bfloat16)
    cross_scores_grad, grad_side_queries, grad_mem_keys, grad_mem_values = attend_backward(
        cross_probs,
        to_heads(side_queries),
        mem_key_heads,
        mem_value_heads,
        to_heads(grad_cross_context),
    )
    grad_side_flat = from_heads(grad_side_queries)
    total_cross_query = summed(normed_two, grad_side_flat)
    grad_cross_in, total_gain_cross = norm_pullback(
        after_self, scale_cross, through(grad_side_flat, side_query)
    )
    grad_after_self = grad_after_cross + grad_cross_in
    key_flat = grad_mem_keys.reshape(-1, model_width)
    value_flat = grad_mem_values.reshape(-1, model_width)
    total_cross_key = summed(memory_flat, key_flat)
    total_cross_value = summed(memory_flat, value_flat)
    memory_grad = (
        (through(key_flat, side_key) + through(value_flat, side_value))
        .astype(jnp.bfloat16)
        .reshape(memory.shape)
    )
    low_self = grad_after_self.astype(jnp.bfloat16)
    total_self_output = summed(self_context, low_self)
    grad_self_context = through(low_self, full_output).astype(jnp.bfloat16)
    grad_self_scores, grad_queries, grad_keys, grad_values = attend_backward(
        self_probs,
        to_heads(queries),
        to_heads(key_rows),
        to_heads(value_rows),
        to_heads(grad_self_context),
    )
    score_totals = (
        jnp.sum(grad_self_scores.astype(jnp.float32), axis=0)
        .transpose(1, 2, 0)
        .reshape(target_len * target_len, head_count)
    )
    table_part = lax.dot_general(
        bucket_hot.astype(jnp.float32),
        score_totals,
        (((0,), (0,)), ((), ())),
        precision=highest,
        preferred_element_type=jnp.float32,
    )
    query_flat = from_heads(grad_queries)
    keys_flat = from_heads(grad_keys)
    values_flat = from_heads(grad_values)
    total_self_query = summed(normed_one, query_flat)
    total_self_key = summed(normed_one, keys_flat)
    total_self_value = summed(normed_one, values_flat)
    grad_normed_one = (
        through(query_flat, full_query)
        + through(keys_flat, full_key)
        + through(values_flat, full_value)
    )
    grad_target_in, total_gain_self = norm_pullback(inputs, scale_self, grad_normed_one)
    target_grad = (grad_after_self + grad_target_in).astype(jnp.bfloat16).reshape(targets.shape)
    shares = (
        lax.psum_scatter(total_gain_self, ("dp", "seq"), scatter_dimension=0, tiled=True),
        lax.psum_scatter(total_gain_cross, ("dp", "seq"), scatter_dimension=0, tiled=True),
        lax.psum_scatter(total_gain_feed, ("dp", "seq"), scatter_dimension=0, tiled=True),
        lax.psum_scatter(total_self_query, ("dp", "seq"), scatter_dimension=0, tiled=True),
        lax.psum_scatter(total_self_key, ("dp", "seq"), scatter_dimension=0, tiled=True),
        lax.psum_scatter(total_self_value, ("dp", "seq"), scatter_dimension=0, tiled=True),
        lax.psum_scatter(total_self_output, ("dp", "seq"), scatter_dimension=0, tiled=True),
        lax.psum_scatter(total_cross_query, ("dp", "seq"), scatter_dimension=0, tiled=True),
        lax.psum_scatter(total_cross_key, ("dp", "seq"), scatter_dimension=0, tiled=True),
        lax.psum_scatter(total_cross_value, ("dp", "seq"), scatter_dimension=0, tiled=True),
        lax.psum_scatter(total_cross_output, ("dp", "seq"), scatter_dimension=0, tiled=True),
        lax.psum_scatter(total_gate, ("dp", "seq"), scatter_dimension=0, tiled=True),
        lax.psum_scatter(total_up, ("dp", "seq"), scatter_dimension=0, tiled=True),
        lax.psum_scatter(total_down, ("dp", "seq"), scatter_dimension=0, tiled=True),
    )
    (
        share_gain_self,
        share_gain_cross,
        share_gain_feed,
        share_self_query,
        share_self_key,
        share_self_value,
        share_self_output,
        share_cross_query,
        share_cross_key,
        share_cross_value,
        share_cross_output,
        share_gate,
        share_up,
        share_down,
    ) = shares
    table_grad = lax.psum(table_part, ("dp", "seq"))
    return (
        outputs,
        target_grad,
        memory_grad,
        share_gain_self,
        share_gain_cross,
        share_gain_feed,
        share_self_query,
        share_self_key,
        share_self_value,
        share_self_output,
        share_cross_query,
        share_cross_key,
        share_cross_value,
        share_cross_output,
        share_gate,
        share_up,
        share_down,
        table_grad,
    )


def solution(mesh):
    return jax.shard_map(
        on_device,
        mesh=mesh,
        in_specs=(
            P(("dp", "seq"), None, None),
            P(("dp", "seq"), None, None),
            P(("dp", "seq")),
            P(),
            P(("dp", "seq"), None, None),
            P(("dp", "seq")),
            P(("dp", "seq")),
            P(("dp", "seq")),
            P(("dp", "seq"), None),
            P(("dp", "seq"), None),
            P(("dp", "seq"), None),
            P(("dp", "seq"), None),
            P(("dp", "seq"), None),
            P(("dp", "seq"), None),
            P(("dp", "seq"), None),
            P(("dp", "seq"), None),
            P(("dp", "seq"), None),
            P(("dp", "seq"), None),
            P(("dp", "seq"), None),
            P(),
        ),
        out_specs=(
            P(("dp", "seq"), None, None),
            P(("dp", "seq"), None, None),
            P(("dp", "seq"), None, None),
            P(("dp", "seq")),
            P(("dp", "seq")),
            P(("dp", "seq")),
            P(("dp", "seq"), None),
            P(("dp", "seq"), None),
            P(("dp", "seq"), None),
            P(("dp", "seq"), None),
            P(("dp", "seq"), None),
            P(("dp", "seq"), None),
            P(("dp", "seq"), None),
            P(("dp", "seq"), None),
            P(("dp", "seq"), None),
            P(("dp", "seq"), None),
            P(("dp", "seq"), None),
            P(),
        ),
        check_vma=False,
    )
```

profile of v0, /device:TPU:8, one launch (start us, length us, event | category | flops | bytes accessed | tf_op | source)
XLA Modules:
  0.0 1995.0 jit_solution(7241529144287481477)
XLA Ops:
  17.9 40.6 %all-reduce.7 = (bf16[768]{0:T(1024)(128)(2,1)S(1)}, bf16[768]{0:T(1024)(128)(2,1)S(1)}, bf16[768]{0:T(1024)(128)(2,1)S(1)}) all-reduce(bf16[768]{0:T(1024)(128)(2,1)S(1)} %dynamic-update-slice, bf16[768]{0:T(1024)(128)(2,1)S(1)} %dynamic-update-slice.1, ...), channel_id=1, replica_groups=mesh['dp'=16,'seq'=2] {'dp','seq'}, use_global_device_ids=true, to_apply=%add | all-reduce | flops 2304 | bytes 9216
  76.0 45.6 %all-gather.14.cloned.1.call-done = bf16[768,768]{1,0:T(8,128)(2,1)} async-done(((bf16[24,768]{1,0:T(8,128)(2,1)}), bf16[768,768]{1,0:T(8,128)(2,1)}) %all-gather.14.cloned.1.call-update) | async-done | bytes 1179664 | tf_op jit(solution)/shard_map/all_gather | solution.py:107
  131.0 46.5 %all-gather.16.cloned.1.call-done = bf16[768,768]{1,0:T(8,128)(2,1)} async-done(((bf16[24,768]{1,0:T(8,128)(2,1)}), bf16[768,768]{1,0:T(8,128)(2,1)}) %all-gather.16.cloned.1.call-update) | async-done | bytes 1179664 | tf_op jit(solution)/shard_map/all_gather | solution.py:108
  203.5 29.8 %all-gather.20.cloned.1.call-done = bf16[768,768]{1,0:T(8,128)(2,1)} async-done(((bf16[24,768]{1,0:T(8,128)(2,1)}), bf16[768,768]{1,0:T(8,128)(2,1)}) %all-gather.20.cloned.1.call-update) | async-done | bytes 1179664 | tf_op jit(solution)/shard_map/all_gather | solution.py:113
  233.2 16.0 convolution_convert_fusion.1
  249.2 15.6 copy.109
  292.5 52.3 %all-gather.22.cloned.1.call-done = bf16[768,768]{1,0:T(8,128)(2,1)} async-done(((bf16[24,768]{1,0:T(8,128)(2,1)}), bf16[768,768]{1,0:T(8,128)(2,1)}) %all-gather.22.cloned.1.call-update) | async-done | bytes 1179664 | tf_op jit(solution)/shard_map/all_gather | solution.py:111
  354.4 46.3 %all-gather.24.cloned.1.call-done = bf16[768,768]{1,0:T(8,128)(2,1)} async-done(((bf16[24,768]{1,0:T(8,128)(2,1)}), bf16[768,768]{1,0:T(8,128)(2,1)}) %all-gather.24.cloned.1.call-update) | async-done | bytes 1179664 | tf_op jit(solution)/shard_map/all_gather | solution.py:112
  400.7 16.3 convolution_convert_fusion
  417.0 15.6 copy.111
  447.2 30.2 %fusion.13 = f32[8,12,96,1024]{3,2,1,0:T(8,128)} fusion(bf16[8,96,12,64]{1,3,2,0:T(8,128)(2,1)S(1)} %copy.112, bf16[8,1024,12,64]{1,0,3,2:T(8,128)(2,1)} %bitcast.181), kind=kOutput, calls=%fused_computation.21 | convolution fusion | flops 1207959552 | bytes 51511296 | tf_op jit(solution)/shard_map/bihe,bjhe->bhij/dot_general | solution.py:45
  477.4 42.7 %fusion.87 = (f32[8,12,96]{2,1,0:T(8,128)S(1)}, f32[8,12,96,1024]{3,2,1,0:T(8,128)}) fusion(f32[8,12,96,1024]{3,2,1,0:T(8,128)} %fusion.13, pred[8,1024]{1,0:T(8,128)(4,1)S(1)} %iota_compare_fusion.8), kind=kOutput, calls=%fused_computation.133 | output fusion | flops 37749760 | bytes 75542528 | tf_op jit(solution)/shard_map/sub | solution.py:50
  520.7 26.6 %fusion.60 = bf16[8,96,12,64]{1,3,2,0:T(8,128)(2,1)} fusion(bf16[8,1024,12,64]{1,0,3,2:T(8,128)(2,1)} %bitcast.189, f32[8,12,96,1024]{3,2,1,0:T(8,128)} %get-tuple-element.97, f32[8,12,96]{2,1,0:T(8,128)S(1)} %get-tuple-element.96), kind=kOutput, calls=%fused_computation.103 | convolution fusion | flops 1227423744 | bytes 51548160 | tf_op jit(solution)/shard_map/bhij,bjhe->bihe/dot_general | solution.py:55
  584.5 54.5 %all-gather.32.cloned.1.call-done = bf16[2048,768]{1,0:T(8,128)(2,1)} async-done(((bf16[64,768]{1,0:T(8,128)(2,1)}), bf16[2048,768]{1,0:T(8,128)(2,1)}) %all-gather.32.cloned.1.call-update) | async-done | bytes 3145744 | tf_op jit(solution)/shard_map/all_gather | solution.py:117
  669.5 34.6 %multiply_reduce_fusion = (f32[8,12,96]{2,1,0:T(8,128)S(1)}, f32[8,12,96,1024]{3,2,1,0:T(8,128)}) fusion(f32[8,12,96,1024]{3,2,1,0:T(8,128)} %get-tuple-element.97, f32[8,12,96]{2,1,0:T(8,128)S(1)} %copy-done.39, bf16[8,96,12,64]{1,3,2,0:T(8,128)(2,1)} %copy.117, bf16[8,1024,12,64]{1,0,3,2:T(8,128)(2,1)} %bitcast.190), kind=kOutput, calls=%fused_computation.3 | convolution fusion | flops 1236261888 | bytes 89333760 | tf_op jit(solution)/shard_map/bihe,bjhe->bhij/dot_general | solution.py:63
  704.2 30.9 %multiply_convert_fusion = bf16[8,12,96,1024]{3,2,1,0:T(8,128)(2,1)} fusion(f32[8,12,96,1024]{3,2,1,0:T(8,128)} %get-tuple-element.102, f32[8,12,96]{2,1,0:T(8,128)S(1)} %get-tuple-element.101, f32[8,12,96,1024]{3,2,1,0:T(8,128)} %get-tuple-element.97, f32[8,12,96]{2,1,0:T(8,128)S(1)} %copy-done.39), kind=kLoop, calls=%fused_computation.2 | loop fusion | flops 37748736 | bytes 94445568 | tf_op jit(solution)/shard_map/convert_element_type | solution.py:71
  735.1 19.5 fusion.53
  858.4 18.9 convert_bitcast_fusion
  903.0 16.2 convolution_bitcast_fusion.1
  922.5 16.3 convolution_bitcast_fusion
  982.3 40.6 %all-reduce.6 = (f32[768]{0:T(1024)}, f32[768]{0:T(1024)}, f32[768]{0:T(1024)}, f32[32,12]{0,1:T(8,128)}) all-reduce(f32[768]{0:T(1024)} %get-tuple-element.76, f32[768]{0:T(1024)} %get-tuple-element.74, f32[768]{0:T(1024)} %get-tuple-element.72, f32[32,12]{0,1:T(8,128)} %fusion.68), channel_id=2, replica_groups=mesh['dp'=16,'seq'=2] {'dp','seq'}, use_global_device_ids=true, to_apply=%region_13.14.clone | all-reduce | flops 2688 | bytes 21504
  1036.9 15.0 fusion.93
  1051.9 22.9 %add_convert_fusion = bf16[8192,768]{1,0:T(8,128)(2,1)} fusion(f32[8192,768]{1,0:T(8,128)} %fusion.93, bf16[8192,768]{0,1:T(8,128)(2,1)} %bitcast.188, bf16[768,768]{1,0:T(8,128)(2,1)} %all-gather.20.cloned.1.call-done), kind=kOutput, calls=%fused_computation.7 | convolution fusion | flops 9676259328 | bytes 51511296 | tf_op jit(solution)/shard_map/dot_general | solution.py:26
  1074.8 30.5 %reduce-scatter.20.cloned.1.call-done = f32[24,768]{1,0:T(8,128)} async-done(((f32[768,768]{1,0:T(8,128)}), f32[24,768]{1,0:T(8,128)}) %reduce-scatter.20.cloned.1.call-update) | async-done | bytes 73744 | tf_op jit(solution)/shard_map/reduce_scatter | solution.py:269
  1105.3 104.4 %reduce-scatter.22.cloned.1.call-done = f32[24,768]{1,0:T(8,128)} async-done(((f32[768,768]{1,0:T(8,128)}), f32[24,768]{1,0:T(8,128)}) %reduce-scatter.22.cloned.1.call-update) | async-done | bytes 73744 | tf_op jit(solution)/shard_map/reduce_scatter | solution.py:270
  1209.7 104.3 %reduce-scatter.24.cloned.1.call-done = f32[24,768]{1,0:T(8,128)} async-done(((f32[768,768]{1,0:T(8,128)}), f32[24,768]{1,0:T(8,128)}) %reduce-scatter.24.cloned.1.call-update) | async-done | bytes 73744 | tf_op jit(solution)/shard_map/reduce_scatter | solution.py:271
  1314.0 104.4 %reduce-scatter.34.cloned.1.call-done = f32[24,768]{1,0:T(8,128)} async-done(((f32[768,768]{1,0:T(8,128)}), f32[24,768]{1,0:T(8,128)}) %reduce-scatter.34.cloned.1.call-update) | async-done | bytes 73744
  1418.4 104.4 %reduce-scatter.36.cloned.1.call-done = f32[24,768]{1,0:T(8,128)} async-done(((f32[768,768]{1,0:T(8,128)}), f32[24,768]{1,0:T(8,128)}) %reduce-scatter.36.cloned.1.call-update) | async-done | bytes 73744
  1522.8 104.5 %reduce-scatter.26.cloned.1.call-done = f32[24,768]{1,0:T(8,128)} async-done(((f32[768,768]{1,0:T(8,128)}), f32[24,768]{1,0:T(8,128)}) %reduce-scatter.26.cloned.1.call-update) | async-done | bytes 73744 | tf_op jit(solution)/shard_map/reduce_scatter | solution.py:274
  1627.3 120.0 %reduce-scatter.28.cloned.1.call-done = f32[24,2048]{1,0:T(8,128)} async-done(((f32[768,2048]{1,0:T(8,128)}), f32[24,2048]{1,0:T(8,128)}) %reduce-scatter.28.cloned.1.call-update) | async-done | bytes 196624 | tf_op jit(solution)/shard_map/reduce_scatter | solution.py:275
  1747.3 120.2 %reduce-scatter.30.cloned.1.call-done = f32[24,2048]{1,0:T(8,128)} async-done(((f32[768,2048]{1,0:T(8,128)}), f32[24,2048]{1,0:T(8,128)}) %reduce-scatter.30.cloned.1.call-update) | async-done | bytes 196624 | tf_op jit(solution)/shard_map/reduce_scatter | solution.py:276
  1867.5 120.2 %reduce-scatter.32.cloned.1.call-done = f32[64,768]{1,0:T(8,128)} async-done(((f32[2048,768]{1,0:T(8,128)}), f32[64,768]{1,0:T(8,128)}) %reduce-scatter.32.cloned.1.call-update) | async-done | bytes 196624 | tf_op jit(solution)/shard_map/reduce_scatter | solution.py:277
  (288 shorter events, 373.1 us)
Async XLA Ops:
  7.2 56.6 %copy-start.2 = (bf16[8,96,768]{2,1,0:T(8,128)(2,1)S(1)}, bf16[8,96,768]{2,1,0:T(8,128)(2,1)}, u32[]{:S(2)}) copy-start(bf16[8,96,768]{2,1,0:T(8,128)(2,1)} %param.20) | copy-start | bytes 3538948
  7.2 55.9 %copy-start.59 = (s32[8]{0:T(128)S(1)}, s32[8]{0:T(128)}, u32[]{:S(2)}) copy-start(s32[8]{0:T(128)} %param.22) | copy-start | bytes 100
  7.2 58.4 %all-gather.12.cloned.1.call-start = ((), (), s32[]{:S(2)}) async-start(), calls=%async_computation.11 | async-start | bytes 1216512 | tf_op jit(solution)/shard_map/all_gather | solution.py:109
  8.0 113.6 %all-gather.14.cloned.1.call-start = ((), (), s32[]{:S(2)}) async-start(), calls=%async_computation.12 | async-start | bytes 1216512 | tf_op jit(solution)/shard_map/all_gather | solution.py:107
  8.7 168.7 %all-gather.16.cloned.1.call-start = ((), (), s32[]{:S(2)}) async-start(), calls=%async_computation.13 | async-start | bytes 1216512 | tf_op jit(solution)/shard_map/all_gather | solution.py:108
  9.4 223.8 %all-gather.20.cloned.1.call-start = ((), (), s32[]{:S(2)}) async-start(), calls=%async_computation.15 | async-start | bytes 1216512 | tf_op jit(solution)/shard_map/all_gather | solution.py:113
  10.0 278.9 %all-gather.18.cloned.1.call-start = ((), (), s32[]{:S(2)}) async-start(), calls=%async_computation.14 | async-start | bytes 1216512 | tf_op jit(solution)/shard_map/all_gather | solution.py:110
  10.6 334.1 %all-gather.22.cloned.1.call-start = ((), (), s32[]{:S(2)}) async-start(), calls=%async_computation.16 | async-start | bytes 1216512 | tf_op jit(solution)/shard_map/all_gather | solution.py:111
  11.2 389.5 %all-gather.24.cloned.1.call-start = ((), (), s32[]{:S(2)}) async-start(), calls=%async_computation.17 | async-start | bytes 1216512 | tf_op jit(solution)/shard_map/all_gather | solution.py:112
  11.9 542.5 %all-gather.26.cloned.1.call-start = ((), (), s32[]{:S(2)}) async-start(), calls=%async_computation.18 | async-start | bytes 1216512 | tf_op jit(solution)/shard_map/all_gather | solution.py:114
  12.7 546.4 %all-gather.28.cloned.1.call-start = ((), (), s32[]{:S(2)}) async-start(), calls=%async_computation.19 | async-start | bytes 3244032 | tf_op jit(solution)/shard_map/all_gather | solution.py:115
  13.4 564.7 %all-gather.30.cloned.1.call-start = ((), (), s32[]{:S(2)}) async-start(), calls=%async_computation.20 | async-start | bytes 3244032 | tf_op jit(solution)/shard_map/all_gather | solution.py:116
  14.0 625.0 %all-gather.32.cloned.1.call-start = ((), (), s32[]{:S(2)}) async-start(), calls=%async_computation.21 | async-start | bytes 3244032 | tf_op jit(solution)/shard_map/all_gather | solution.py:117
  14.7 1060.1 %reduce-scatter.16.cloned.1.call-start = ((), (), s32[]{:S(2)}) async-start(), calls=%async_computation.22 | async-start | bytes 2433024 | tf_op jit(solution)/shard_map/reduce_scatter | solution.py:267
  63.1 281.6 %copy-start.49 = (f32[768]{0:T(1024)}, f32[768]{0:T(1024)S(1)}, u32[]{:S(2)}) copy-start(f32[768]{0:T(1024)S(1)} %convert_element_type.156) | copy-start | bytes 9220
  64.1 57.4 %copy-start.31 = (bf16[768,768]{1,0:T(8,128)(2,1)}, bf16[768,768]{1,0:T(8,128)(2,1)S(1)}, u32[]{:S(2)}) copy-start(bf16[768,768]{1,0:T(8,128)(2,1)S(1)} %fusion.34) | copy-start | bytes 3538948
  131.0 59.7 %copy-start.19 = (bf16[8,96,12,64]{1,3,2,0:T(8,128)(2,1)}, bf16[8,96,12,64]{1,3,2,0:T(8,128)(2,1)S(1)}, u32[]{:S(2)}) copy-start(bf16[8,96,12,64]{1,3,2,0:T(8,128)(2,1)S(1)} %copy.103) | copy-start | bytes 3538948
  291.9 55.3 %copy-start.8 = (f32[768,768]{1,0:T(8,128)}, f32[768,768]{1,0:T(8,128)S(1)}, u32[]{:S(2)}) copy-start(f32[768,768]{1,0:T(8,128)S(1)} %get-tuple-element.95) | copy-start | bytes 7077892
  292.5 54.7 %copy-start.51 = (f32[768]{0:T(1024)}, f32[768]{0:T(1024)S(1)}, u32[]{:S(2)}) copy-start(f32[768]{0:T(1024)S(1)} %fusion.80) | copy-start | bytes 9220
  354.4 92.8 %copy-start.4 = (bf16[8,96,12,64]{1,3,2,0:T(8,128)(2,1)}, bf16[8,96,12,64]{1,3,2,0:T(8,128)(2,1)S(1)}, u32[]{:S(2)}) copy-start(bf16[8,96,12,64]{1,3,2,0:T(8,128)(2,1)S(1)} %copy.112) | copy-start | bytes 3538948
  565.9 73.1 %copy-start.28 = (bf16[8,96,768]{2,1,0:T(8,128)(2,1)S(1)}, bf16[8,96,768]{2,1,0:T(8,128)(2,1)}, u32[]{:S(2)}) copy-start(bf16[8,96,768]{2,1,0:T(8,128)(2,1)} %param.24) | copy-start | bytes 3538948
  796.9 277.9 %reduce-scatter.18.cloned.1.call-start = ((), (), s32[]{:S(2)}) async-start(), calls=%async_computation.23 | async-start | bytes 2433024 | tf_op jit(solution)/shard_map/reduce_scatter | solution.py:268
  807.1 298.2 %reduce-scatter.20.cloned.1.call-start = ((), (), s32[]{:S(2)}) async-start(), calls=%async_computation.24 | async-start | bytes 2433024 | tf_op jit(solution)/shard_map/reduce_scatter | solution.py:269
  819.6 390.1 %reduce-scatter.22.cloned.1.call-start = ((), (), s32[]{:S(2)}) async-start(), calls=%async_computation.25 | async-start | bytes 2433024 | tf_op jit(solution)/shard_map/reduce_scatter | solution.py:270
  857.6 456.5 %reduce-scatter.24.cloned.1.call-start = ((), (), s32[]{:S(2)}) async-start(), calls=%async_computation.26 | async-start | bytes 2433024 | tf_op jit(solution)/shard_map/reduce_scatter | solution.py:271
  903.0 515.4 %reduce-scatter.34.cloned.1.call-start = ((), (), s32[]{:S(2)}) async-start(), calls=%async_computation.31 | async-start | bytes 2433024
  922.3 600.5 %reduce-scatter.36.cloned.1.call-start = ((), (), s32[]{:S(2)}) async-start(), calls=%async_computation.32 | async-start | bytes 2433024
  942.0 685.3 %reduce-scatter.26.cloned.1.call-start = ((), (), s32[]{:S(2)}) async-start(), calls=%async_computation.27 | async-start | bytes 2433024 | tf_op jit(solution)/shard_map/reduce_scatter | solution.py:274
  947.5 799.9 %reduce-scatter.28.cloned.1.call-start = ((), (), s32[]{:S(2)}) async-start(), calls=%async_computation.28 | async-start | bytes 6488064 | tf_op jit(solution)/shard_map/reduce_scatter | solution.py:275
  955.5 912.1 %reduce-scatter.30.cloned.1.call-start = ((), (), s32[]{:S(2)}) async-start(), calls=%async_computation.29 | async-start | bytes 6488064 | tf_op jit(solution)/shard_map/reduce_scatter | solution.py:276
  962.0 1025.8 %reduce-scatter.32.cloned.1.call-start = ((), (), s32[]{:S(2)}) async-start(), calls=%async_computation.30 | async-start | bytes 6488064 | tf_op jit(solution)/shard_map/reduce_scatter | solution.py:277
  1051.9 935.8 %copy-start.1 = (bf16[32,12]{0,1:T(8,128)(2,1)S(1)}, bf16[32,12]{0,1:T(8,128)(2,1)}, u32[]{:S(2)}) copy-start(bf16[32,12]{0,1:T(8,128)(2,1)} %param.39) | copy-start | bytes 2308
  (58 other events, 344.7 us)
Sparse Core Ops, SparseCore 0:
  11.0 54.2 all-gather.11
  68.2 53.2 all-gather.13
  124.4 52.9 all-gather.15
  180.2 52.9 all-gather.19
  236.0 52.9 all-gather.17
  291.7 52.9 all-gather.21
  347.7 52.9 all-gather.23
  403.6 52.9 all-gather.25
  459.5 57.9 all-gather.27
  520.2 57.9 all-gather.29
  581.0 57.9 all-gather.31
  797.1 99.3 reduce-scatter.15
  902.3 98.6 reduce-scatter.17
  1006.7 98.5 reduce-scatter.19
  1111.0 98.6 reduce-scatter.21
  1215.4 98.5 reduce-scatter.23
  1319.7 98.6 reduce-scatter.33
  1424.1 98.6 reduce-scatter.35
  1528.6 98.6 reduce-scatter.25
  1633.3 113.9 reduce-scatter.27
  1753.6 113.9 reduce-scatter.29
  1873.8 113.9 reduce-scatter.31
where the time goes:
time: 2010 us; the launch traced here: 2000 us
  waiting for transfers between devices  1220 us (61%)
  matrix products  380 us (19%)
  local copies, waits for them, and re-layouts  212 us (11%)
  other arithmetic  88.3 us (4%)
  blocking collectives  81.2 us (4%)
    unnamed x24, waiting for transfers between devices  216 us
    reduce_scatter x1, waiting for transfers between devices, on_device(): lax.psum_scatter(total_up, ('dp', 'seq'), scatter_dimension=0, tiled=True)  120 us
    reduce_scatter x1, waiting for transfers between devices, on_device(): lax.psum_scatter(total_down, ('dp', 'seq'), scatter_dimension=0, tiled=True)  120 us
    reduce_scatter x1, waiting for transfers between devices, on_device(): lax.psum_scatter(total_gate, ('dp', 'seq'), scatter_dimension=0, tiled=True)  120 us
    reduce_scatter x1, waiting for transfers between devices, on_device(): lax.psum_scatter(total_cross_output, ('dp', 'seq'), scatter_dimension=0,...  105 us
    reduce_scatter x1, waiting for transfers between devices, on_device(): lax.psum_scatter(total_self_output, ('dp', 'seq'), scatter_dimension=0, t...  104 us
    reduce_scatter x1, waiting for transfers between devices, on_device(): lax.psum_scatter(total_cross_query, ('dp', 'seq'), scatter_dimension=0, t...  104 us
    unnamed x2, blocking collectives  81.2 us
  transfers between devices with their start and end apart: 22, of which 17 were waited for; matrix products, arithmetic and copies ran while one was open for 26% of the time, Pallas kernels for 0%

commit v1 on v0

v1 whole, which is shorter than its diff:
```python
import math

import jax
import jax.numpy as jnp
from jax import lax
from jax.experimental import pallas as pl
from jax.experimental.pallas import tpu as pltpu
from jax.sharding import PartitionSpec as P

epsilon = 1e-06
masked_out = -1e30
bf16 = jnp.bfloat16
f32 = jnp.float32
axes = ("dp", "seq")
lane_tile = 256
group_rows = 24
pair_width = 128
NN = (((1,), (0,)), ((), ()))
NT = (((1,), (1,)), ((), ()))
TN = (((0,), (0,)), ((), ()))
gelu_scale = math.sqrt(2.0 / math.pi)
gelu_cubic = 0.044715


def dot(left_side, right_side, dims=NN):
    return lax.dot_general(left_side, right_side, dims, preferred_element_type=f32)


def params():
    return pltpu.CompilerParams(vmem_limit_bytes=60 * 1024 * 1024)


def column_tile(packed_ref, index):
    tile = packed_ref[:, index * group_rows : (index + 1) * group_rows, :]
    return tile.reshape(tile.shape[0] * group_rows, lane_tile)


def put_column_tile(packed_ref, index, values):
    groups = packed_ref.shape[0]
    packed_ref[:, index * group_rows : (index + 1) * group_rows, :] = values.reshape(
        groups, group_rows, lane_tile
    ).astype(bf16)


def lane_halves(rows):
    lanes = lax.broadcasted_iota(jnp.int32, (rows, pair_width), 1)
    return lanes < pair_width // 2


def project(rows, packed_ref, base, tiles):
    return [dot(rows, column_tile(packed_ref, base + t)) for t in range(tiles)]


def through(rows, packed_ref, base, tiles):
    total = None
    for t in range(tiles):
        part = dot(
            rows[:, t * lane_tile : (t + 1) * lane_tile], column_tile(packed_ref, base + t), NT
        )
        total = part if total is None else total + part
    return total


def put_weight_grad(packed_ref, base, rows, grads):
    for t in range(grads.shape[1] // lane_tile):
        part = dot(rows, grads[:, t * lane_tile : (t + 1) * lane_tile], TN)
        put_column_tile(packed_ref, base + t, part)


def norm_scale(values):
    return lax.rsqrt(jnp.mean(values * values, axis=-1, keepdims=True) + epsilon)


def norm_pullback(values, gain_row, grad_in):
    inverse = norm_scale(values)
    weighted = grad_in * gain_row
    inner = jnp.mean(weighted * values, axis=-1, keepdims=True)
    grad_values = inverse * weighted - values * (inverse * inverse * inverse * inner)
    grad_gain = jnp.sum(grad_in * values * inverse, axis=0, keepdims=True)
    return grad_values, grad_gain


def memory_kernel(lengths, memory_ref, packed_ref, keys_ref, values_ref):
    seq = pl.program_id(0)
    memory_len = memory_ref.shape[1]

    def fill(count):
        rows = memory_ref[0, :count, :]
        for base, out_ref in ((0, keys_ref), (3, values_ref)):
            for t in range(3):
                out_ref[0, :count, t * lane_tile : (t + 1) * lane_tile] = dot(
                    rows, column_tile(packed_ref, base + t)
                ).astype(bf16)

    @pl.when(lengths[seq] > memory_len // 2)
    def _():
        fill(memory_len)

    @pl.when(lengths[seq] <= memory_len // 2)
    def _():
        fill(memory_len // 2)


def project_memory(mem_lengths, memory, packed):
    batch, memory_len, width = memory.shape
    block = pl.BlockSpec((1, memory_len, width), lambda b, n: (b, 0, 0))
    return pl.pallas_call(
        memory_kernel,
        out_shape=[jax.ShapeDtypeStruct(memory.shape, bf16)] * 2,
        grid_spec=pltpu.PrefetchScalarGridSpec(
            num_scalar_prefetch=1,
            grid=(batch,),
            in_specs=[block, pl.BlockSpec(packed.shape, lambda b, n: (0, 0, 0))],
            out_specs=[block, block],
        ),
        compiler_params=params(),
        name="memory_project",
    )(mem_lengths, memory, packed)


def stacked_pair(rows, half, pad):
    zero = jnp.zeros_like(rows)
    gap = jnp.zeros((pad, pair_width), rows.dtype)
    return jnp.concatenate(
        [jnp.where(half, rows, zero), gap, jnp.where(half, zero, rows), gap], axis=0
    )


def pair_softmax(scores):
    parts = []
    for h in range(2):
        one = scores[:, h * pair_width : (h + 1) * pair_width]
        terms = jnp.exp(one - jnp.max(one, axis=-1, keepdims=True))
        parts.append(terms * (1.0 / jnp.sum(terms, axis=-1, keepdims=True)))
    return parts


def self_forward_kernel(
    target_len,
    targets_ref,
    packed_ref,
    bias_ref,
    gain_self_ref,
    gain_cross_ref,
    normed_one_ref,
    queries_ref,
    keys_ref,
    values_ref,
    context_ref,
    after_ref,
    normed_two_ref,
    side_ref,
):
    inputs = targets_ref[...].astype(f32)
    normed_one = (inputs * norm_scale(inputs) * gain_self_ref[...]).astype(bf16)
    normed_one_ref[...] = normed_one
    for base, out_ref in ((0, queries_ref), (3, keys_ref), (6, values_ref)):
        for t in range(3):
            out_ref[:, t * lane_tile : (t + 1) * lane_tile] = dot(
                normed_one, column_tile(packed_ref, base + t)
            ).astype(bf16)
    half = lane_halves(target_len)
    pad = pair_width - target_len
    pairs = bias_ref.shape[0]

    def attend(seq, carry):
        rows = pl.ds(pl.multiple_of(seq * target_len, 32), target_len)
        for p in range(pairs):
            cols = slice(p * pair_width, (p + 1) * pair_width)
            key_stack = stacked_pair(keys_ref[rows, cols], half, pad)
            value_stack = stacked_pair(values_ref[rows, cols], half, pad)
            scores = dot(queries_ref[rows, cols], key_stack, NT) + bias_ref[p]
            probs = jnp.concatenate(pair_softmax(scores), axis=1)
            context_ref[rows, cols] = dot(probs.astype(bf16), value_stack).astype(bf16)
        return carry

    lax.fori_loop(0, targets_ref.shape[0] // target_len, attend, 0)
    after = inputs + jnp.concatenate(project(context_ref[...], packed_ref, 9, 3), axis=1)
    after_ref[...] = after
    normed_two = (after * norm_scale(after) * gain_cross_ref[...]).astype(bf16)
    normed_two_ref[...] = normed_two
    for t in range(3):
        side_ref[:, t * lane_tile : (t + 1) * lane_tile] = dot(
            normed_two, column_tile(packed_ref, 12 + t)
        ).astype(bf16)


def self_forward(target_len, targets, packed, bias, gain_self, gain_cross):
    low = jax.ShapeDtypeStruct(targets.shape, bf16)
    wide = jax.ShapeDtypeStruct(targets.shape, f32)

    def body(*refs):
        self_forward_kernel(target_len, *refs)

    return pl.pallas_call(
        body,
        out_shape=[low, low, low, low, low, wide, low, low],
        compiler_params=params(),
        name="self_forward",
    )(targets, packed, bias, gain_self, gain_cross)


def masked_stack(rows, half):
    zero = jnp.zeros_like(rows)
    return jnp.concatenate([jnp.where(half, rows, zero), jnp.where(half, zero, rows)], axis=0)


def cross_forward_kernel(lengths, side_ref, keys_ref, values_ref, context_ref, weights_ref):
    seq = pl.program_id(0)
    target_len, width = side_ref.shape
    memory_len = keys_ref.shape[1]
    half = lane_halves(target_len)

    def attend(count):
        for p in range(width // pair_width):
            cols = slice(p * pair_width, (p + 1) * pair_width)
            stack = masked_stack(side_ref[:, cols], half)
            scores = dot(stack, keys_ref[0, :count, cols], NT)
            terms = jnp.exp(scores - jnp.max(scores, axis=-1, keepdims=True))
            scale = 1.0 / jnp.sum(terms, axis=-1, keepdims=True)
            weights = (terms * scale).astype(bf16)
            weights_ref[0, 2 * target_len * p : 2 * target_len * (p + 1), :count] = weights
            both = dot(weights, values_ref[0, :count, cols])
            context_ref[:, cols] = jnp.where(half, both[:target_len], both[target_len:]).astype(
                bf16
            )

    @pl.when(lengths[seq] > memory_len // 2)
    def _():
        attend(memory_len)

    @pl.when(lengths[seq] <= memory_len // 2)
    def _():
        attend(memory_len // 2)


def cross_forward(mem_lengths, side, mem_keys, mem_values, head_count):
    batch, memory_len, width = mem_keys.shape
    target_len = side.shape[0] // batch
    rows = pl.BlockSpec((target_len, width), lambda b, n: (b, 0))
    memory = pl.BlockSpec((1, memory_len, width), lambda b, n: (b, 0, 0))
    weights = pl.BlockSpec((1, head_count * target_len, memory_len), lambda b, n: (b, 0, 0))
    return pl.pallas_call(
        cross_forward_kernel,
        out_shape=[
            jax.ShapeDtypeStruct(side.shape, bf16),
            jax.ShapeDtypeStruct((batch, head_count * target_len, memory_len), bf16),
        ],
        grid_spec=pltpu.PrefetchScalarGridSpec(
            num_scalar_prefetch=1,
            grid=(batch,),
            in_specs=[rows, memory, memory],
            out_specs=[rows, weights],
        ),
        compiler_params=params(),
        name="cross_forward",
    )(mem_lengths, side, mem_keys, mem_values)


def feed_kernel(
    after_ref,
    context_ref,
    cot_ref,
    gain_ref,
    side_output_ref,
    gate_ref,
    up_ref,
    down_ref,
    outputs_ref,
    grad_after_ref,
    grad_context_ref,
    grad_gain_ref,
    packed_ref,
    after_cross_ref,
    normed_ref,
    out_total_ref,
    grad_normed_ref,
):
    step = pl.program_id(0)
    steps = pl.num_programs(0)

    @pl.when(step == 0)
    def _():
        after_cross = after_ref[...] + jnp.concatenate(
            project(context_ref[...], side_output_ref, 0, 3), axis=1
        )
        after_cross_ref[...] = after_cross
        normed_ref[...] = (after_cross * norm_scale(after_cross) * gain_ref[...]).astype(bf16)
        out_total_ref[...] = after_cross
        grad_normed_ref[...] = jnp.zeros_like(grad_normed_ref)

    normed = normed_ref[...]
    cot = cot_ref[...]
    gate_weight = column_tile(gate_ref, 0)
    up_weight = column_tile(up_ref, 0)
    share = down_ref.shape[1] // 3
    owners = down_ref.shape[0]
    down_weight = jnp.concatenate(
        [
            down_ref[:, c * share : (c + 1) * share, :].reshape(owners * share, lane_tile)
            for c in range(3)
        ],
        axis=1,
    )
    gate = dot(normed, gate_weight)
    up = dot(normed, up_weight)
    grad_hidden = dot(cot, down_weight, NT)
    square = gate * gate
    tanh = jnp.tanh(gelu_scale * (gate + gelu_cubic * (square * gate)))
    half_sum = 0.5 * (1.0 + tanh)
    active = gate * half_sum
    slope = half_sum + 0.5 * gate * (1.0 - tanh * tanh) * (
        gelu_scale * (1.0 + 3.0 * gelu_cubic * square)
    )
    hidden = (active * up).astype(bf16)
    grad_gate = (grad_hidden * up * slope).astype(bf16)
    grad_up = (grad_hidden * active).astype(bf16)
    out_total_ref[...] += dot(hidden, down_weight)
    grad_normed_ref[...] += dot(grad_gate, gate_weight, NT) + dot(grad_up, up_weight, NT)
    groups = packed_ref.shape[0]

    def put(base, value):
        packed_ref[:, pl.ds(base + step * group_rows, group_rows), :] = value.reshape(
            groups, group_rows, lane_tile
        ).astype(bf16)

    put(0, dot(normed, grad_gate, TN))
    put(steps * group_rows, dot(normed, grad_up, TN))
    down_base = 2 * steps * group_rows
    for c in range(3):
        part = dot(hidden, cot[:, c * lane_tile : (c + 1) * lane_tile], TN)
        packed_ref[
            pl.ds(step * owners, owners), down_base + c * share : down_base + (c + 1) * share, :
        ] = part.reshape(owners, share, lane_tile).astype(bf16)

    @pl.when(step == steps - 1)
    def _():
        outputs_ref[...] = out_total_ref[...].astype(bf16)
        grad_in, grad_gain = norm_pullback(
            after_cross_ref[...], gain_ref[...], grad_normed_ref[...]
        )
        grad_gain_ref[...] = grad_gain
        grad_after = cot_ref[...].astype(f32) + grad_in
        grad_after_ref[...] = grad_after
        low = grad_after.astype(bf16)
        put_weight_grad(packed_ref, 3 * down_base // (2 * group_rows), context_ref[...], low)
        grad_context_ref[...] = through(low, side_output_ref, 0, 3).astype(bf16)


def feed_both(after_self, context, cotangent, gain, packed_self, packed_feed):
    rows, width = context.shape
    groups, feed_rows, _ = packed_feed.shape
    steps = feed_rows // (3 * group_rows)
    owners = groups // steps
    whole = lambda f: (0, 0)
    full = pl.BlockSpec((rows, width), whole)
    tile = (groups, group_rows, lane_tile)
    out_rows = feed_rows + 3 * group_rows
    return pl.pallas_call(
        feed_kernel,
        out_shape=[
            jax.ShapeDtypeStruct((rows, width), bf16),
            jax.ShapeDtypeStruct((rows, width), f32),
            jax.ShapeDtypeStruct((rows, width), bf16),
            jax.ShapeDtypeStruct((1, width), f32),
            jax.ShapeDtypeStruct((groups, out_rows, lane_tile), bf16),
        ],
        grid=(steps,),
        in_specs=[
            full,
            full,
            full,
            pl.BlockSpec((1, width), whole),
            pl.BlockSpec((groups, 3 * group_rows, lane_tile), lambda f: (0, 5, 0)),
            pl.BlockSpec(tile, lambda f: (0, f, 0)),
            pl.BlockSpec(tile, lambda f: (0, steps + f, 0)),
            pl.BlockSpec((owners, steps * group_rows, lane_tile), lambda f: (f, 2, 0)),
        ],
        out_specs=[
            full,
            full,
            full,
            pl.BlockSpec((1, width), whole),
            pl.BlockSpec((groups, out_rows, lane_tile), lambda f: (0, 0, 0)),
        ],
        scratch_shapes=[
            pltpu.VMEM((rows, width), f32),
            pltpu.VMEM((rows, width), bf16),
            pltpu.VMEM((rows, width), f32),
            pltpu.VMEM((rows, width), f32),
        ],
        compiler_params=params(),
        name="feed_both",
    )(after_self, context, cotangent, gain, packed_self, packed_feed, packed_feed, packed_feed)


def cross_backward_kernel(
    lengths,
    grad_ref,
    context_ref,
    side_ref,
    keys_ref,
    values_ref,
    weights_ref,
    grad_side_ref,
    grad_keys_ref,
    grad_values_ref,
):
    seq = pl.program_id(0)
    target_len, width = side_ref.shape
    memory_len = keys_ref.shape[1]
    half = lane_halves(target_len)

    def attend(count):
        for p in range(width // pair_width):
            cols = slice(p * pair_width, (p + 1) * pair_width)
            grad_rows = grad_ref[:, cols]
            grad_stack = masked_stack(grad_rows, half)
            query_stack = masked_stack(side_ref[:, cols], half)
            product = grad_rows.astype(f32) * context_ref[:, cols].astype(f32)
            inner = jnp.sum(masked_stack(product, half), axis=-1, keepdims=True)
            weights = weights_ref[0, 2 * target_len * p : 2 * target_len * (p + 1), :count]
            grad_probs = dot(grad_stack, values_ref[0, :count, cols], NT)
            grad_scores = (weights.astype(f32) * (grad_probs - inner)).astype(bf16)
            both = dot(grad_scores, keys_ref[0, :count, cols])
            grad_side_ref[:, cols] = jnp.where(half, both[:target_len], both[target_len:]).astype(
                bf16
            )
            grad_keys_ref[0, cols, :count] = dot(query_stack, grad_scores, TN).astype(bf16)
            grad_values_ref[0, cols, :count] = dot(grad_stack, weights, TN).astype(bf16)

    @pl.when(lengths[seq] > memory_len // 2)
    def _():
        attend(memory_len)

    @pl.when(lengths[seq] <= memory_len // 2)
    def _():
        attend(memory_len // 2)


def cross_backward(mem_lengths, grad_context, context, side, mem_keys, mem_values, weights):
    batch, memory_len, width = mem_keys.shape
    target_len = side.shape[0] // batch
    rows = pl.BlockSpec((target_len, width), lambda b, n: (b, 0))
    memory = pl.BlockSpec((1, memory_len, width), lambda b, n: (b, 0, 0))
    turned = pl.BlockSpec((1, width, memory_len), lambda b, n: (b, 0, 0))
    return pl.pallas_call(
        cross_backward_kernel,
        out_shape=[jax.ShapeDtypeStruct(side.shape, bf16)]
        + [jax.ShapeDtypeStruct((batch, width, memory_len), bf16)] * 2,
        grid_spec=pltpu.PrefetchScalarGridSpec(
            num_scalar_prefetch=1,
            grid=(batch,),
            in_specs=[
                rows,
                rows,
                rows,
                memory,
                memory,
                pl.BlockSpec((1,) + weights.shape[1:], lambda b, n: (b, 0, 0)),
            ],
            out_specs=[rows, turned, turned],
        ),
        compiler_params=params(),
        name="cross_backward",
    )(mem_lengths, grad_context, context, side, mem_keys, mem_values, weights)


def memory_weight_kernel(
    lengths, memory_ref, grad_keys_ref, grad_values_ref, packed_ref, key_total_ref, value_total_ref
):
    seq = pl.program_id(0)
    memory_len = memory_ref.shape[1]

    @pl.when(seq == 0)
    def _():
        key_total_ref[...] = jnp.zeros_like(key_total_ref)
        value_total_ref[...] = jnp.zeros_like(value_total_ref)

    def add(count):
        rows = memory_ref[0, :count, :]
        key_total_ref[...] += dot(grad_keys_ref[0, :, :count], rows)
        value_total_ref[...] += dot(grad_values_ref[0, :, :count], rows)

    @pl.when(lengths[seq] > memory_len // 2)
    def _():
        add(memory_len)

    @pl.when(lengths[seq] <= memory_len // 2)
    def _():
        add(memory_len // 2)

    @pl.when(seq == pl.num_programs(0) - 1)
    def _():
        for base, total_ref in ((0, key_total_ref), (3, value_total_ref)):
            for t in range(3):
                put_column_tile(
                    packed_ref,
                    base + t,
                    jnp.transpose(total_ref[t * lane_tile : (t + 1) * lane_tile, :]),
                )


def memory_weight_grads(mem_lengths, memory, grad_keys, grad_values, packed_shape):
    batch, memory_len, width = memory.shape
    block = pl.BlockSpec((1, memory_len, width), lambda b, n: (b, 0, 0))
    turned = pl.BlockSpec((1, width, memory_len), lambda b, n: (b, 0, 0))
    return pl.pallas_call(
        memory_weight_kernel,
        out_shape=jax.ShapeDtypeStruct(packed_shape, bf16),
        grid_spec=pltpu.PrefetchScalarGridSpec(
            num_scalar_prefetch=1,
            grid=(batch,),
            in_specs=[block, turned, turned],
            out_specs=pl.BlockSpec(packed_shape, lambda b, n: (0, 0, 0)),
            scratch_shapes=[pltpu.VMEM((width, width), f32)] * 2,
        ),
        compiler_params=params(),
        name="memory_weight_grads",
    )(mem_lengths, memory, grad_keys, grad_values)


def memory_grad_kernel(
    lengths, grad_keys_ref, grad_values_ref, packed_ref, out_ref, key_turned_ref, value_turned_ref
):
    seq = pl.program_id(0)
    memory_len = out_ref.shape[1]

    @pl.when(seq == 0)
    def _():
        for base, turned_ref in ((0, key_turned_ref), (3, value_turned_ref)):
            for t in range(3):
                turned_ref[t * lane_tile : (t + 1) * lane_tile, :] = jnp.transpose(
                    column_tile(packed_ref, base + t)
                )

    def fill(count):
        out_ref[0, :count, :] = (
            dot(grad_keys_ref[0, :, :count], key_turned_ref[...], TN)
            + dot(grad_values_ref[0, :, :count], value_turned_ref[...], TN)
        ).astype(bf16)

    @pl.when(lengths[seq] > memory_len // 2)
    def _():
        fill(memory_len)

    @pl.when(lengths[seq] <= memory_len // 2)
    def _():
        fill(memory_len // 2)
        out_ref[0, memory_len // 2 :, :] = jnp.zeros_like(out_ref[0, memory_len // 2 :, :])


def memory_gradient(mem_lengths, grad_keys, grad_values, packed):
    batch, width, memory_len = grad_keys.shape
    turned = pl.BlockSpec((1, width, memory_len), lambda b, n: (b, 0, 0))
    return pl.pallas_call(
        memory_grad_kernel,
        out_shape=jax.ShapeDtypeStruct((batch, memory_len, width), bf16),
        grid_spec=pltpu.PrefetchScalarGridSpec(
            num_scalar_prefetch=1,
            grid=(batch,),
            in_specs=[turned, turned, pl.BlockSpec(packed.shape, lambda b, n: (0, 0, 0))],
            out_specs=pl.BlockSpec((1, memory_len, width), lambda b, n: (b, 0, 0)),
            scratch_shapes=[pltpu.VMEM((width, width), bf16)] * 2,
        ),
        compiler_params=params(),
        name="memory_grad",
    )(mem_lengths, grad_keys, grad_values, packed)


def self_backward_kernel(
    target_len,
    grad_side_ref,
    after_ref,
    grad_after_ref,
    normed_two_ref,
    normed_one_ref,
    queries_ref,
    keys_ref,
    values_ref,
    context_ref,
    targets_ref,
    packed_ref,
    bias_ref,
    buckets_ref,
    gain_self_ref,
    gain_cross_ref,
    target_grad_ref,
    grads_ref,
    grad_gains_ref,
    table_ref,
    grad_queries_ref,
    grad_keys_ref,
    grad_values_ref,
    grad_context_ref,
    total_ref,
    score_total_ref,
):
    grad_side = grad_side_ref[...]
    grad_in, grad_gain_cross = norm_pullback(
        after_ref[...], gain_cross_ref[...], through(grad_side, packed_ref, 12, 3)
    )
    put_weight_grad(grads_ref, 12, normed_two_ref[...], grad_side)
    grad_after = grad_after_ref[...] + grad_in
    total_ref[...] = grad_after
    low = grad_after.astype(bf16)
    put_weight_grad(grads_ref, 9, context_ref[...], low)
    grad_context_ref[...] = through(low, packed_ref, 9, 3).astype(bf16)
    half = lane_halves(target_len)
    pad = pair_width - target_len
    pairs = bias_ref.shape[0]
    score_total_ref[...] = jnp.zeros_like(score_total_ref)

    def pick(values):
        return jnp.where(
            half, values[:target_len], values[pair_width : pair_width + target_len]
        ).astype(bf16)

    def attend(seq, carry):
        rows = pl.ds(pl.multiple_of(seq * target_len, 32), target_len)
        for p in range(pairs):
            cols = slice(p * pair_width, (p + 1) * pair_width)
            queries = queries_ref[rows, cols]
            grad_rows = grad_context_ref[rows, cols]
            key_stack = stacked_pair(keys_ref[rows, cols], half, pad)
            value_stack = stacked_pair(values_ref[rows, cols], half, pad)
            scores = dot(queries, key_stack, NT) + bias_ref[p]
            probs = pair_softmax(scores)
            grad_probs = dot(grad_rows, value_stack, NT)
            parts = []
            for h in range(2):
                one = grad_probs[:, h * pair_width : (h + 1) * pair_width]
                inner = jnp.sum(one * probs[h], axis=-1, keepdims=True)
                parts.append(probs[h] * (one - inner))
            grad_scores = jnp.concatenate(parts, axis=1).astype(bf16)
            weights = jnp.concatenate(probs, axis=1).astype(bf16)
            score_total_ref[p] += grad_scores.astype(f32)
            grad_queries_ref[rows, cols] = dot(grad_scores, key_stack).astype(bf16)
            grad_keys_ref[rows, cols] = pick(dot(grad_scores, queries, TN))
            grad_values_ref[rows, cols] = pick(dot(weights, grad_rows, TN))
        return carry

    lax.fori_loop(0, targets_ref.shape[0] // target_len, attend, 0)
    buckets = buckets_ref[...]
    both = jnp.concatenate([buckets, buckets], axis=1)

    def count(bucket, carry):
        chosen = both == bucket
        for p in range(pairs):
            table_ref[bucket, p : p + 1, :] = jnp.sum(
                jnp.where(chosen, score_total_ref[p], 0.0), axis=0, keepdims=True
            )
        return carry

    lax.fori_loop(0, table_ref.shape[0], count, 0)
    normed_one = normed_one_ref[...]
    total = None
    for base, grad_ref in ((0, grad_queries_ref), (3, grad_keys_ref), (6, grad_values_ref)):
        grads = grad_ref[...]
        put_weight_grad(grads_ref, base, normed_one, grads)
        part = through(grads, packed_ref, base, 3)
        total = part if total is None else total + part
    grad_in, grad_gain_self = norm_pullback(
        targets_ref[...].astype(f32), gain_self_ref[...], total
    )
    target_grad_ref[...] = (total_ref[...] + grad_in).astype(bf16)
    grad_gains_ref[0:1, :] = grad_gain_self
    grad_gains_ref[1:2, :] = grad_gain_cross


def self_backward(target_len, bucket_count, operands):
    targets = operands[9]
    packed = operands[10]
    bias = operands[11]
    rows, width = targets.shape

    def body(*refs):
        self_backward_kernel(target_len, *refs)

    return pl.pallas_call(
        body,
        out_shape=[
            jax.ShapeDtypeStruct((rows, width), bf16),
            jax.ShapeDtypeStruct((packed.shape[0], 15 * group_rows, lane_tile), bf16),
            jax.ShapeDtypeStruct((2, width), f32),
            jax.ShapeDtypeStruct((bucket_count, bias.shape[0], bias.shape[2]), f32),
        ],
        scratch_shapes=[pltpu.VMEM((rows, width), bf16)] * 4
        + [pltpu.VMEM((rows, width), f32), pltpu.VMEM(bias.shape, f32)],
        compiler_params=params(),
        name="self_backward",
    )(*operands)


def pack(shard):
    rows, columns = shard.shape
    tiles = columns // lane_tile
    return (
        shard.reshape(rows, tiles, lane_tile)
        .transpose(1, 0, 2)
        .reshape(rows * tiles, lane_tile)
    )


def unpack(packed, rows, columns):
    tiles = columns // lane_tile
    return packed.reshape(tiles, rows, lane_tile).transpose(1, 0, 2).reshape(rows, columns)


def regroup(packed, from_groups, to_groups, shapes):
    if from_groups == to_groups:
        return packed
    parts = []
    offset = 0
    for rows, columns in shapes:
        tiles = columns // lane_tile
        size = rows // from_groups * tiles
        part = packed[:, offset : offset + size, :]
        offset += size
        part = part.reshape(from_groups, tiles, rows // from_groups, lane_tile)
        part = part.transpose(0, 2, 1, 3).reshape(to_groups, rows // to_groups, tiles, lane_tile)
        parts.append(
            part.transpose(0, 2, 1, 3).reshape(to_groups, rows // to_groups * tiles, lane_tile)
        )
    return jnp.concatenate(parts, axis=1)


def gather(shards, shapes, groups, devices):
    packed = jnp.concatenate([pack(shard) for shard in shards], axis=0)
    whole = lax.all_gather(packed, axes, axis=0, tiled=False)
    return regroup(whole, devices, groups, shapes)


def scatter(packed, shapes, groups, devices):
    packed = regroup(packed, groups, devices, shapes)
    share = lax.psum_scatter(packed, axes, scatter_dimension=0, tiled=False)
    parts = []
    offset = 0
    for rows, columns in shapes:
        size = rows // devices * (columns // lane_tile)
        parts.append(
            unpack(share[offset : offset + size], rows // devices, columns).astype(f32)
        )
        offset += size
    return parts


def on_device(
    devices,
    targets,
    memory,
    mem_lengths,
    buckets,
    cotangent,
    gain_self,
    gain_cross,
    gain_feed,
    self_query,
    self_key,
    self_value,
    self_output,
    cross_query,
    cross_key,
    cross_value,
    cross_output,
    gate_weight,
    up_weight,
    down_weight,
    bias_table,
):
    batch, target_len, width = targets.shape
    bucket_count, head_count = bias_table.shape
    row_count = batch * target_len
    groups = width // group_rows
    square = (width, width)
    feed_width = gate_weight.shape[1]
    feed_shapes = [(width, feed_width), (width, feed_width), (feed_width, width)]

    packed_memory = gather([cross_key, cross_value], [square] * 2, groups, devices)
    packed_self = gather(
        [self_query, self_key, self_value, self_output, cross_query, cross_output],
        [square] * 6,
        groups,
        devices,
    )
    gains = lax.all_gather(
        jnp.stack([gain_self, gain_cross, gain_feed]), axes, axis=1, tiled=True
    ).astype(f32)
    packed_feed = gather([gate_weight, up_weight, down_weight], feed_shapes, groups, devices)

    pad = pair_width - target_len
    bucket_hot = (
        buckets[:, :, None] == lax.broadcasted_iota(jnp.int32, (1, 1, bucket_count), 2)
    ).reshape(target_len * target_len, bucket_count)
    bias = (
        dot(bucket_hot.astype(bf16), bias_table)
        .reshape(target_len, target_len, head_count)
        .transpose(2, 0, 1)
    )
    causal = lax.broadcasted_iota(jnp.int32, (target_len, target_len), 1) <= lax.broadcasted_iota(
        jnp.int32, (target_len, target_len), 0
    )
    bias = jnp.where(causal, bias, masked_out)
    bias = jnp.pad(bias, ((0, 0), (0, 0), (0, pad)), constant_values=masked_out)
    bias = (
        bias.reshape(head_count // 2, 2, target_len, pair_width)
        .transpose(0, 2, 1, 3)
        .reshape(head_count // 2, target_len, 2 * pair_width)
    )
    wide_buckets = jnp.pad(buckets, ((0, 0), (0, pad)), constant_values=-1)
    target_rows = targets.reshape(row_count, width)
    cot_rows = cotangent.reshape(row_count, width)

    mem_keys, mem_values = project_memory(mem_lengths, memory, packed_memory)
    normed_one, queries, key_rows, value_rows, self_context, after_self, normed_two, side = (
        self_forward(target_len, target_rows, packed_self, bias, gains[0:1], gains[1:2])
    )
    cross_context, weights = cross_forward(mem_lengths, side, mem_keys, mem_values, head_count)
    outputs, grad_after_cross, grad_context, grad_gain_feed, feed_grads = feed_both(
        after_self, cross_context, cot_rows, gains[2:3], packed_self, packed_feed
    )
    share_gate, share_up, share_down, share_cross_output = scatter(
        feed_grads, feed_shapes + [square], groups, devices
    )
    grad_side, grad_mem_keys, grad_mem_values = cross_backward(
        mem_lengths, grad_context, cross_context, side, mem_keys, mem_values, weights
    )
    target_grad, self_grads, grad_gains, table_parts = self_backward(
        target_len,
        bucket_count,
        (
            grad_side,
            after_self,
            grad_after_cross,
            normed_two,
            normed_one,
            queries,
            key_rows,
            value_rows,
            self_context,
            target_rows,
            packed_self,
            bias,
            wide_buckets,
            gains[0:1],
            gains[1:2],
        ),
    )
    share_query, share_key, share_value, share_output, share_cross_query = scatter(
        self_grads, [square] * 5, groups, devices
    )
    memory_grads = memory_weight_grads(
        mem_lengths, memory, grad_mem_keys, grad_mem_values, packed_memory.shape
    )
    share_cross_key, share_cross_value = scatter(memory_grads, [square] * 2, groups, devices)
    memory_grad = memory_gradient(mem_lengths, grad_mem_keys, grad_mem_values, packed_memory)

    table_part = (
        table_parts.reshape(bucket_count, head_count, pair_width).sum(axis=-1).reshape(-1)
    )
    small = jnp.concatenate(
        [grad_gains[0], grad_gains[1], grad_gain_feed[0], table_part], axis=0
    )
    small = jnp.sum(lax.all_gather(small, axes, axis=0, tiled=False), axis=0)
    table_grad = small[3 * width :].reshape(bucket_count, head_count)
    own = width // devices
    place = lax.axis_index(axes) * own

    def own_gain(index):
        return lax.dynamic_slice(small, (index * width + place,), (own,))

    return (
        outputs.reshape(targets.shape),
        target_grad.reshape(targets.shape),
        memory_grad,
        own_gain(0),
        own_gain(1),
        own_gain(2),
        share_query,
        share_key,
        share_value,
        share_output,
        share_cross_query,
        share_cross_key,
        share_cross_value,
        share_cross_output,
        share_gate,
        share_up,
        share_down,
        table_grad,
    )


def solution(mesh):
    devices = mesh.shape["dp"] * mesh.shape["seq"]
    rows = P(axes, None, None)
    flat = P(axes)
    weight = P(axes, None)

    def body(*arguments):
        return on_device(devices, *arguments)

    return jax.shard_map(
        body,
        mesh=mesh,
        in_specs=(rows, rows, flat, P(), rows, flat, flat, flat) + (weight,) * 11 + (P(),),
        out_specs=(rows, rows, rows, flat, flat, flat) + (weight,) * 11 + (P(),),
        check_vma=False,
    )
```

time: 2010 us -> 708 us (0.35)
  waiting for transfers between devices: 1220 us -> 297 us
  matrix products: 380 us -> 0.36 us
  Pallas kernels: 0 us -> 251 us
  local copies, waits for them, and re-layouts: 212 us -> 21.7 us
  other arithmetic: 88.3 us -> 1.8 us
  blocking collectives: 81.2 us -> 112 us
    reduce_scatter x9 -> x3, waiting for transfers between devices: 704 us -> 226 us  [scatter(): share = lax.psum_scatter(packed, axes, scatter_dimension=0, tiled=False)]
    dot_general x46 -> x1, matrix products: 374 us -> 0.36 us  [dot(): lax.dot_general(left_side, right_side, dims, preferred_element_type=f32)]
    pallas_call x0 -> x8, Pallas kernels: none -> 251 us  [the longest x1 48.7 us: self_backward(): pl.pallas_call(body, out_shape=[jax.ShapeDtypeStruct((rows, width), bf16)...]
    all_gather x11 -> x3, waiting for transfers between devices: 297 us -> 69.8 us  [gather(): whole = lax.all_gather(packed, axes, axis=0, tiled=False)]
    unnamed x24 -> x6, waiting for transfers between devices: 216 us -> 0.6 us
    all_gather x0 -> x2, blocking collectives: none -> 112 us  [the longest x1 56.1 us: on_device(): lax.all_gather(jnp.stack([gain_self, gain_cross, gain_feed]), axes, axis=...]
    unnamed x2 -> x0, blocking collectives: 81.2 us -> none
    unnamed x151 -> x43, local copies, waits for them, and re-layouts: 78.7 us -> 7.56 us
  transfers between devices with their start and end apart: 22 -> 6, of which waited for: 17 -> 4; matrix products, arithmetic and copies ran while one was open for 26% -> 2% of each run, Pallas kernels for 0% -> 23%
where the time goes in v1:
time: 708 us; the launch traced here: 699 us
  waiting for transfers between devices  297 us (42%)
  Pallas kernels  251 us (35%)
  blocking collectives  112 us (16%)
  local copies, waits for them, and re-layouts  21.7 us (3%)
  between operations  14.8 us (2%)
    reduce_scatter x3, waiting for transfers between devices, scatter(): share = lax.psum_scatter(packed, axes, scatter_dimension=0, tiled=False)  226 us
    all_gather x3, waiting for transfers between devices, gather(): whole = lax.all_gather(packed, axes, axis=0, tiled=False)  69.8 us
    all_gather x1, blocking collectives, on_device(): lax.all_gather(jnp.stack([gain_self, gain_cross, gain_feed]), axes, axis=...  56.1 us
    all_gather x1, blocking collectives, on_device(): small = jnp.sum(lax.all_gather(small, axes, axis=0, tiled=False), axis=0)  56 us
    pallas_call x1, Pallas kernels, self_backward(): pl.pallas_call(body, out_shape=[jax.ShapeDtypeStruct((rows, width), bf16)...  48.7 us
    pallas_call x1, Pallas kernels, feed_both(): pl.pallas_call(feed_kernel, out_shape=[jax.ShapeDtypeStruct((rows, width)...  37.9 us
    pallas_call x1, Pallas kernels, cross_backward(): pl.pallas_call(cross_backward_kernel, out_shape=[jax.ShapeDtypeStruct(sid...  31.3 us
    pallas_call x1, Pallas kernels, cross_forward(): pl.pallas_call(cross_forward_kernel, out_shape=[jax.ShapeDtypeStruct(side...  29.5 us
  transfers between devices with their start and end apart: 6, of which 4 were waited for; matrix products, arithmetic and copies ran while one was open for 2% of the time, Pallas kernels for 23%

profile of v1, /device:TPU:8, one launch (start us, length us, event | category | flops | bytes accessed | tf_op | source)
XLA Modules:
  0.0 699.0 jit_solution(14680887841782782586)
XLA Ops:
  7.3 0.9 reshape.254
  8.2 0.8 reshape.256
  9.7 0.8 reshape.240
  10.5 0.8 reshape.242
  11.3 0.8 reshape.244
  12.1 0.8 reshape.246
  13.0 0.8 reshape.248
  13.8 0.8 reshape.250
  14.7 0.7 copy-done.2
  15.6 0.7 pad_maximum_fusion
  16.4 56.1 %all-gather.4 = bf16[32,24,3]{1,2,0:T(4,128)(2,1)S(1)} all-gather(bf16[1,24,3]{1,2,0:T(4,128)(2,1)S(1)} %maximum_bitcast_fusion), channel_id=1, replica_groups=mesh['dp'=16,'seq'=2] {'dp','seq'}, dimensions={0}, use_global_device_ids=true | all-gather | bytes 4752 | tf_op jit(solution)/shard_map/all_gather | solution.py:786
  73.5 0.9 copy.176
  75.0 24.2 %memory_project.1 = (bf16[8,1024,768]{2,1,0:T(8,128)(2,1)}, bf16[8,1024,768]{2,1,0:T(8,128)(2,1)}) custom-call(s32[8]{0:T(128)} %lengths.9, bf16[8,1024,768]{2,1,0:T(8,128)(2,1)} %memory_ref.3, bf16[32,144,256]{2,1,0:T(8,128)(2,1)} %bitcast.124), custom_call_target="tpu_custom_call" | custom-call | tf_op jit(solution)/shard_map/memory_project/pallas_call | solution.py:107
  99.2 45.0 %all-gather.10.cloned.1.call-done = bf16[13824,256]{1,0:T(8,128)(2,1)} async-done(((bf16[432,256]{1,0:T(8,128)(2,1)}), bf16[13824,256]{1,0:T(8,128)(2,1)}) %all-gather.10.cloned.1.call-update) | async-done | bytes 7077904 | tf_op jit(solution)/shard_map/all_gather | solution.py:730
  144.2 29.4 %self_forward.1 = (bf16[768,768]{1,0:T(8,128)(2,1)}, bf16[768,768]{1,0:T(8,128)(2,1)}, bf16[768,768]{1,0:T(8,128)(2,1)}, bf16[768,768]{1,0:T(8,128)(2,1)}, bf16[...) custom-call(bf16[768,768]{1,0:T(8,128)(2,1)} %bitcast.128, ...), custom_call_target="tpu_custom_call" | custom-call | tf_op jit(solution)/shard_map/self_forward/pallas_call | solution.py:195
  173.6 29.5 %cross_forward.1 = (bf16[768,768]{1,0:T(8,128)(2,1)}, bf16[8,1152,1024]{2,1,0:T(8,128)(2,1)}) custom-call(s32[8]{0:T(128)} %lengths.9, bf16[768,768]{1,0:T(8,128)(2,1)} %get-tuple-element.43.side_ref, bf16[8,1024,768]{2,1,0:T(8,128)(2,1)} %get-tuple-element.44.keys_ref, bf16[8,1024,768]{2,1,0:T(8,128)(2,1)} %get-tuple-element.45.values_ref), custom_call_target="tpu_custom_call" | custom-call | tf_op jit(solution)/shard_map/cross_forward/pallas_call | solution.py:243
  203.0 24.8 %all-gather.14.cloned.1.call-done = bf16[18432,256]{1,0:T(8,128)(2,1)} async-done(((bf16[576,256]{1,0:T(8,128)(2,1)}), bf16[18432,256]{1,0:T(8,128)(2,1)}) %all-gather.14.cloned.1.call-update) | async-done | bytes 9437200 | tf_op jit(solution)/shard_map/all_gather | solution.py:730
  227.8 37.9 %feed_both.1 = (bf16[768,768]{1,0:T(8,128)(2,1)}, f32[768,768]{1,0:T(8,128)}, bf16[768,768]{1,0:T(8,128)(2,1)}, f32[1,768]{1,0:T(1,128)}, bf16[32,648,256]{2,1,0:T(8,128)(2,1)}) custom-call(f32[768,768]{1,0:T(8,128)} %get-tuple-element.42.after_ref.refs_1_, bf16[768,768]{1,0:T(8,128)(2,1)} %get-tuple-element.46.context_ref, bf16[768,768]{1,0:T(8,128)(2,1)} %bitcast.131, ...), custom_call_target="tpu_custom_call" | custom-call | tf_op jit(solution)/shard_map/feed_both/pallas_call | solution.py:359
  265.7 31.3 %cross_backward.1 = (bf16[768,768]{1,0:T(8,128)(2,1)}, bf16[8,768,1024]{2,1,0:T(8,128)(2,1)}, bf16[8,768,1024]{2,1,0:T(8,128)(2,1)}) custom-call(s32[8]{0:T(128)} %lengths.9, bf16[768,768]{1,0:T(8,128)(2,1)} %get-tuple-element.48.grad_ref, bf16[768,768]{1,0:T(8,128)(2,1)} %get-tuple-element.46.context_ref, bf16[768,768]{1,0:T(8,128)(2,1)} %get-tuple-element.43.side_ref, ...), custom_call_target="tpu_custom_call" | custom-call | tf_op jit(solution)/shard_map/cross_backward/pallas_call | solution.py:447
  297.0 24.7 %memory_weight_grads.1 = bf16[32,144,256]{2,1,0:T(8,128)(2,1)} custom-call(s32[8]{0:T(128)} %lengths.9, bf16[8,1024,768]{2,1,0:T(8,128)(2,1)} %memory_ref.3, bf16[8,768,1024]{2,1,0:T(8,128)(2,1)} %get-tuple-element.59.grad_keys_ref, bf16[8,768,1024]{2,1,0:T(8,128)(2,1)} %get-tuple-element.60.grad_values_ref), custom_call_target="tpu_custom_call" | custom-call | tf_op jit(solution)/shard_map/memory_weight_grads/pallas_call | solution.py:508
  322.4 48.7 %self_backward.1 = (bf16[768,768]{1,0:T(8,128)(2,1)}, bf16[32,360,256]{2,1,0:T(8,128)(2,1)}, f32[2,768]{1,0:T(2,128)}, f32[32,6,256]{2,1,0:T(8,128)}) custom-call(bf16[768,768]{1,0:T(8,128)(2,1)} %get-tuple-element.50.refs_0_, f32[768,768]{1,0:T(8,128)} %get-tuple-element.42.after_ref.refs_1_, f32[768,768]{1,0:T(8,128)} %get-tuple-element.51.refs_2_, ...), custom_call_target="tpu_custom_call" | custom-call | tf_op jit(solution)/shard_map/self_backward/pallas_call | solution.py:680
  371.7 25.6 %memory_grad.1 = bf16[8,1024,768]{2,1,0:T(8,128)(2,1)} custom-call(s32[8]{0:T(128)} %lengths.9, bf16[8,768,1024]{2,1,0:T(8,128)(2,1)} %get-tuple-element.59.grad_keys_ref, bf16[8,768,1024]{2,1,0:T(8,128)(2,1)} %get-tuple-element.60.grad_values_ref, bf16[32,144,256]{2,1,0:T(8,128)(2,1)} %bitcast.125), custom_call_target="tpu_custom_call" | custom-call | tf_op jit(solution)/shard_map/memory_grad/pallas_call | solution.py:556
  397.7 56.0 %all-gather.5 = f32[32,1,2688]{2,1,0:T(1,128)S(1)} all-gather(f32[1,1,2688]{2,1,0:T(1,128)S(1)} %reshape.298), channel_id=5, replica_groups=mesh['dp'=16,'seq'=2] {'dp','seq'}, dimensions={0}, use_global_device_ids=true | all-gather | bytes 354816 | tf_op jit(solution)/shard_map/all_gather | solution.py:864
  454.0 0.7 copy.157
  455.3 0.8 fusion.7
  457.4 83.6 %reduce-scatter.4.cloned.1.call-done = bf16[1,360,256]{2,1,0:T(8,128)(2,1)} async-done(((bf16[32,360,256]{2,1,0:T(8,128)(2,1)}), bf16[1,360,256]{2,1,0:T(8,128)(2,1)}) %reduce-scatter.4.cloned.1.call-update) | async-done | bytes 184336 | tf_op jit(solution)/shard_map/reduce_scatter | solution.py:736
  541.0 0.9 fusion.6
  545.3 142.8 %reduce-scatter.8.cloned.1.call-done = bf16[1,648,256]{2,1,0:T(8,128)(2,1)} async-done(((bf16[32,648,256]{2,1,0:T(8,128)(2,1)}), bf16[1,648,256]{2,1,0:T(8,128)(2,1)}) %reduce-scatter.8.cloned.1.call-update) | async-done | bytes 331792 | tf_op jit(solution)/shard_map/reduce_scatter | solution.py:736
  688.0 1.0 fusion.5
  689.1 0.7 copy.172
  689.9 0.7 copy.162
  690.6 0.7 copy.163
  (100 shorter events, 10.6 us)
Async XLA Ops:
  7.2 65.7 %copy-start = (bf16[32,12]{0,1:T(8,128)(2,1)S(1)}, bf16[32,12]{0,1:T(8,128)(2,1)}, u32[]{:S(2)}) copy-start(bf16[32,12]{0,1:T(8,128)(2,1)} %param.39) | copy-start | bytes 2308
  7.2 8.2 %copy-start.5 = (bf16[64,768]{1,0:T(8,128)(2,1)S(1)}, bf16[64,768]{1,0:T(8,128)(2,1)}, u32[]{:S(2)}) copy-start(bf16[64,768]{1,0:T(8,128)(2,1)} %param.38) | copy-start | bytes 294916
  7.2 8.3 %copy-start.6 = (bf16[24,2048]{1,0:T(8,128)(2,1)S(1)}, bf16[24,2048]{1,0:T(8,128)(2,1)}, u32[]{:S(2)}) copy-start(bf16[24,2048]{1,0:T(8,128)(2,1)} %param.36) | copy-start | bytes 294916
  7.2 8.3 %copy-start.7 = (bf16[24,2048]{1,0:T(8,128)(2,1)S(1)}, bf16[24,2048]{1,0:T(8,128)(2,1)}, u32[]{:S(2)}) copy-start(bf16[24,2048]{1,0:T(8,128)(2,1)} %param.37) | copy-start | bytes 294916
  7.2 67.7 %all-gather.12.cloned.1.call-start = ((), (), s32[]{:S(2)}) async-start(), calls=%async_computation.7 | async-start | bytes 2433024 | tf_op jit(solution)/shard_map/all_gather | solution.py:730
  9.6 134.6 %all-gather.10.cloned.1.call-start = ((), (), s32[]{:S(2)}) async-start(), calls=%async_computation.6 | async-start | bytes 7299072 | tf_op jit(solution)/shard_map/all_gather | solution.py:730
  11.3 5.1 copy-start.10
  11.3 5.1 copy-start.11
  11.3 5.1 copy-start.12
  12.9 59.9 %copy-start.4 = (s32[96,96]{1,0:T(8,128)S(1)}, s32[96,96]{1,0:T(8,128)}, u32[]{:S(2)}) copy-start(s32[96,96]{1,0:T(8,128)} %param.23) | copy-start | bytes 110596
  14.7 0.7 copy-start.2
  15.4 212.4 %all-gather.14.cloned.1.call-start = ((), (), s32[]{:S(2)}) async-start(), calls=%async_computation.8 | async-start | bytes 9732096 | tf_op jit(solution)/shard_map/all_gather | solution.py:730
  16.3 439.0 %reduce-scatter.6.cloned.1.call-start = ((), (), s32[]{:S(2)}) async-start(), calls=%async_computation.4 | async-start | bytes 2433024 | tf_op jit(solution)/shard_map/reduce_scatter | solution.py:736
  321.7 219.3 %reduce-scatter.4.cloned.1.call-start = ((), (), s32[]{:S(2)}) async-start(), calls=%async_computation.3 | async-start | bytes 6082560 | tf_op jit(solution)/shard_map/reduce_scatter | solution.py:736
  371.1 316.9 %reduce-scatter.8.cloned.1.call-start = ((), (), s32[]{:S(2)}) async-start(), calls=%async_computation.5 | async-start | bytes 10948608 | tf_op jit(solution)/shard_map/reduce_scatter | solution.py:736
  371.7 25.6 %copy-start.3 = (f32[32,6,256]{2,1,0:T(8,128)S(1)}, f32[32,6,256]{2,1,0:T(8,128)}, u32[]{:S(2)}) copy-start(f32[32,6,256]{2,1,0:T(8,128)} %get-tuple-element.63) | copy-start | bytes 589828
  371.7 25.9 %copy-start.9 = (f32[1,768]{1,0:T(1,128)S(1)}, f32[1,768]{1,0:T(1,128)}, u32[]{:S(2)}) copy-start(f32[1,768]{1,0:T(1,128)} %get-tuple-element.62) | copy-start | bytes 9220
  371.7 25.9 %copy-start.8 = (f32[2,768]{1,0:T(2,128)S(1)}, f32[2,768]{1,0:T(2,128)}, u32[]{:S(2)}) copy-start(f32[2,768]{1,0:T(2,128)} %get-tuple-element.61) | copy-start | bytes 18436
  544.6 147.4 %copy-start.1 = (bf16[32,12]{0,1:T(8,128)(2,1)S(1)}, bf16[32,12]{0,1:T(8,128)(2,1)}, u32[]{:S(2)}) copy-start(bf16[32,12]{0,1:T(8,128)(2,1)} %param.39) | copy-start | bytes 2308
  688.0 3.3 slice-start
Sparse Core Ops, SparseCore 0:
  11.5 57.5 all-gather.11
  72.7 71.5 all-gather.9
  147.7 80.0 all-gather.13
  321.8 101.3 reduce-scatter.5
  428.7 112.2 reduce-scatter.3
  547.0 141.0 reduce-scatter.7

commit v2 on v1

--- a/solution.py
+++ b/solution.py
@@ -30,6 +30,12 @@
     return pltpu.CompilerParams(vmem_limit_bytes=60 * 1024 * 1024)
 
 
+def cost(flops, size, exps=0):
+    return pl.CostEstimate(
+        flops=int(flops), bytes_accessed=int(size), transcendentals=int(exps)
+    )
+
+
 def column_tile(packed_ref, index):
     tile = packed_ref[:, index * group_rows : (index + 1) * group_rows, :]
     return tile.reshape(tile.shape[0] * group_rows, lane_tile)
@@ -67,6 +73,20 @@
         put_column_tile(packed_ref, base + t, part)
 
 
+def put_slots(owners, keep_ref, send_ref, stage_ref, index, values):
+    stage_ref[...] = values
+    half = keep_ref.shape[0]
+    part = slice(index * group_rows, (index + 1) * group_rows)
+
+    def place(slot, carry):
+        for offset, out_ref in ((0, keep_ref), (half, send_ref)):
+            start = pl.multiple_of(owners[slot + offset] * group_rows, 8)
+            out_ref[slot, part, :] = stage_ref[pl.ds(start, group_rows), :].astype(bf16)
+        return carry
+
+    lax.fori_loop(0, half, place, 0)
+
+
 def norm_scale(values):
     return lax.rsqrt(jnp.mean(values * values, axis=-1, keepdims=True) + epsilon)
 
@@ -80,16 +100,32 @@
     return grad_values, grad_gain
 
 
-def memory_kernel(lengths, memory_ref, packed_ref, keys_ref, values_ref):
+def memory_kernel(lengths, slots, memory_ref, packed_ref, keys_ref, values_ref, weight_ref):
     seq = pl.program_id(0)
     memory_len = memory_ref.shape[1]
+    tiles = weight_ref.shape[1] // lane_tile
+
+    @pl.when(seq == 0)
+    def _():
+        def place(pair, carry):
+            first = slots[2 * pair]
+            second = slots[2 * pair + 1]
+            rows = pl.ds(pl.multiple_of(2 * group_rows * pair, 16), 2 * group_rows)
+            for t in range(tiles):
+                part = slice(t * group_rows, (t + 1) * group_rows)
+                weight_ref[rows, t * lane_tile : (t + 1) * lane_tile] = jnp.concatenate(
+                    [packed_ref[first, part, :], packed_ref[second, part, :]], axis=0
+                )
+            return carry
+
+        lax.fori_loop(0, weight_ref.shape[0] // (2 * group_rows), place, 0)
 
     def fill(count):
         rows = memory_ref[0, :count, :]
         for base, out_ref in ((0, keys_ref), (3, values_ref)):
             for t in range(3):
                 out_ref[0, :count, t * lane_tile : (t + 1) * lane_tile] = dot(
-                    rows, column_tile(packed_ref, base + t)
+                    rows, weight_ref[:, (base + t) * lane_tile : (base + t + 1) * lane_tile]
                 ).astype(bf16)
 
     @pl.when(lengths[seq] > memory_len // 2)
@@ -101,21 +137,23 @@
         fill(memory_len // 2)
 
 
-def project_memory(mem_lengths, memory, packed):
+def project_memory(mem_lengths, slots, memory, packed):
     batch, memory_len, width = memory.shape
-    block = pl.BlockSpec((1, memory_len, width), lambda b, n: (b, 0, 0))
+    block = pl.BlockSpec((1, memory_len, width), lambda b, n, s: (b, 0, 0))
     return pl.pallas_call(
         memory_kernel,
-        out_shape=[jax.ShapeDtypeStruct(memory.shape, bf16)] * 2,
+        out_shape=[jax.ShapeDtypeStruct(memory.shape, bf16)] * 2
+        + [jax.ShapeDtypeStruct((width, 2 * width), bf16)],
         grid_spec=pltpu.PrefetchScalarGridSpec(
-            num_scalar_prefetch=1,
+            num_scalar_prefetch=2,
             grid=(batch,),
-            in_specs=[block, pl.BlockSpec(packed.shape, lambda b, n: (0, 0, 0))],
-            out_specs=[block, block],
+            in_specs=[block, pl.BlockSpec(packed.shape, lambda b, n, s: (0, 0, 0))],
+            out_specs=[block, block, pl.BlockSpec((width, 2 * width), lambda b, n, s: (0, 0))],
         ),
         compiler_params=params(),
+        cost_estimate=cost(4 * memory.size * width, 6 * memory.size),
         name="memory_project",
-    )(mem_lengths, memory, packed)
+    )(mem_lengths, slots, memory, packed)
 
 
 def stacked_pair(rows, half, pad):
@@ -196,6 +234,7 @@
         body,
         out_shape=[low, low, low, low, low, wide, low, low],
         compiler_params=params(),
+        cost_estimate=cost(20 * targets.size * targets.shape[1], 16 * targets.size),
         name="self_forward",
     )(targets, packed, bias, gain_self, gain_cross)
 
@@ -253,6 +292,7 @@
             out_specs=[rows, weights],
         ),
         compiler_params=params(),
+        cost_estimate=cost(16 * side.size * memory_len, 6 * mem_keys.size, batch * head_count * target_len * memory_len),
         name="cross_forward",
     )(mem_lengths, side, mem_keys, mem_values)
 
@@ -390,6 +430,7 @@
             pltpu.VMEM((rows, width), f32),
         ],
         compiler_params=params(),
+        cost_estimate=cost(18 * rows * width * steps * lane_tile, 30 * rows * width),
         name="feed_both",
     )(after_self, context, cotangent, gain, packed_self, packed_feed, packed_feed, packed_feed)
 
@@ -462,12 +503,22 @@
             out_specs=[rows, turned, turned],
         ),
         compiler_params=params(),
+        cost_estimate=cost(32 * side.size * memory_len, 10 * mem_keys.size),
         name="cross_backward",
     )(mem_lengths, grad_context, context, side, mem_keys, mem_values, weights)
 
 
 def memory_weight_kernel(
-    lengths, memory_ref, grad_keys_ref, grad_values_ref, packed_ref, key_total_ref, value_total_ref
+    lengths,
+    owners,
+    memory_ref,
+    grad_keys_ref,
+    grad_values_ref,
+    keep_ref,
+    send_ref,
+    key_total_ref,
+    value_total_ref,
+    stage_ref,
 ):
     seq = pl.program_id(0)
     memory_len = memory_ref.shape[1]
@@ -494,34 +545,40 @@
     def _():
         for base, total_ref in ((0, key_total_ref), (3, value_total_ref)):
             for t in range(3):
-                put_column_tile(
-                    packed_ref,
+                put_slots(
+                    owners,
+                    keep_ref,
+                    send_ref,
+                    stage_ref,
                     base + t,
                     jnp.transpose(total_ref[t * lane_tile : (t + 1) * lane_tile, :]),
                 )
 
 
-def memory_weight_grads(mem_lengths, memory, grad_keys, grad_values, packed_shape):
+def memory_weight_grads(mem_lengths, owners, memory, grad_keys, grad_values):
     batch, memory_len, width = memory.shape
-    block = pl.BlockSpec((1, memory_len, width), lambda b, n: (b, 0, 0))
-    turned = pl.BlockSpec((1, width, memory_len), lambda b, n: (b, 0, 0))
+    block = pl.BlockSpec((1, memory_len, width), lambda b, n, o: (b, 0, 0))
+    turned = pl.BlockSpec((1, width, memory_len), lambda b, n, o: (b, 0, 0))
+    half = (owners.shape[0] // 2, 2 * width // lane_tile * group_rows, lane_tile)
     return pl.pallas_call(
         memory_weight_kernel,
-        out_shape=jax.ShapeDtypeStruct(packed_shape, bf16),
+        out_shape=[jax.ShapeDtypeStruct(half, bf16)] * 2,
         grid_spec=pltpu.PrefetchScalarGridSpec(
-            num_scalar_prefetch=1,
+            num_scalar_prefetch=2,
             grid=(batch,),
             in_specs=[block, turned, turned],
-            out_specs=pl.BlockSpec(packed_shape, lambda b, n: (0, 0, 0)),
-            scratch_shapes=[pltpu.VMEM((width, width), f32)] * 2,
+            out_specs=[pl.BlockSpec(half, lambda b, n, o: (0, 0, 0))] * 2,
+            scratch_shapes=[pltpu.VMEM((width, width), f32)] * 2
+            + [pltpu.VMEM((width, lane_tile), f32)],
         ),
         compiler_params=params(),
+        cost_estimate=cost(4 * memory.size * width, 6 * memory.size),
         name="memory_weight_grads",
-    )(mem_lengths, memory, grad_keys, grad_values)
+    )(mem_lengths, owners, memory, grad_keys, grad_values)
 
 
 def memory_grad_kernel(
-    lengths, grad_keys_ref, grad_values_ref, packed_ref, out_ref, key_turned_ref, value_turned_ref
+    lengths, grad_keys_ref, grad_values_ref, weight_ref, out_ref, key_turned_ref, value_turned_ref
 ):
     seq = pl.program_id(0)
     memory_len = out_ref.shape[1]
@@ -531,7 +588,7 @@
         for base, turned_ref in ((0, key_turned_ref), (3, value_turned_ref)):
             for t in range(3):
                 turned_ref[t * lane_tile : (t + 1) * lane_tile, :] = jnp.transpose(
-                    column_tile(packed_ref, base + t)
+                    weight_ref[:, (base + t) * lane_tile : (base + t + 1) * lane_tile]
                 )
 
     def fill(count):
@@ -550,7 +607,7 @@
         out_ref[0, memory_len // 2 :, :] = jnp.zeros_like(out_ref[0, memory_len // 2 :, :])
 
 
-def memory_gradient(mem_lengths, grad_keys, grad_values, packed):
+def memory_gradient(mem_lengths, grad_keys, grad_values, weight):
     batch, width, memory_len = grad_keys.shape
     turned = pl.BlockSpec((1, width, memory_len), lambda b, n: (b, 0, 0))
     return pl.pallas_call(
@@ -559,17 +616,19 @@
         grid_spec=pltpu.PrefetchScalarGridSpec(
             num_scalar_prefetch=1,
             grid=(batch,),
-            in_specs=[turned, turned, pl.BlockSpec(packed.shape, lambda b, n: (0, 0, 0))],
+            in_specs=[turned, turned, pl.BlockSpec(weight.shape, lambda b, n: (0, 0))],
             out_specs=pl.BlockSpec((1, memory_len, width), lambda b, n: (b, 0, 0)),
             scratch_shapes=[pltpu.VMEM((width, width), bf16)] * 2,
         ),
         compiler_params=params(),
+        cost_estimate=cost(4 * grad_keys.size * width, 6 * grad_keys.size),
         name="memory_grad",
-    )(mem_lengths, grad_keys, grad_values, packed)
+    )(mem_lengths, grad_keys, grad_values, weight)
 
 
 def self_backward_kernel(
     target_len,
+    owners,
     grad_side_ref,
     after_ref,
     grad_after_ref,
@@ -586,7 +645,8 @@
     gain_self_ref,
     gain_cross_ref,
     target_grad_ref,
-    grads_ref,
+    keep_ref,
+    send_ref,
     grad_gains_ref,
     table_ref,
     grad_queries_ref,
@@ -595,16 +655,22 @@
     grad_context_ref,
     total_ref,
     score_total_ref,
+    stage_ref,
 ):
+    def put(base, rows, grads):
+        for t in range(grads.shape[1] // lane_tile):
+            part = dot(rows, grads[:, t * lane_tile : (t + 1) * lane_tile], TN)
+            put_slots(owners, keep_ref, send_ref, stage_ref, base + t, part)
+
     grad_side = grad_side_ref[...]
     grad_in, grad_gain_cross = norm_pullback(
         after_ref[...], gain_cross_ref[...], through(grad_side, packed_ref, 12, 3)
     )
-    put_weight_grad(grads_ref, 12, normed_two_ref[...], grad_side)
+    put(12, normed_two_ref[...], grad_side)
     grad_after = grad_after_ref[...] + grad_in
     total_ref[...] = grad_after
     low = grad_after.astype(bf16)
-    put_weight_grad(grads_ref, 9, context_ref[...], low)
+    put(9, context_ref[...], low)
     grad_context_ref[...] = through(low, packed_ref, 9, 3).astype(bf16)
     half = lane_halves(target_len)
     pad = pair_width - target_len
@@ -657,7 +723,7 @@
     total = None
     for base, grad_ref in ((0, grad_queries_ref), (3, grad_keys_ref), (6, grad_values_ref)):
         grads = grad_ref[...]
-        put_weight_grad(grads_ref, base, normed_one, grads)
+        put(base, normed_one, grads)
         part = through(grads, packed_ref, base, 3)
         total = part if total is None else total + part
     grad_in, grad_gain_self = norm_pullback(
@@ -668,11 +734,12 @@
     grad_gains_ref[1:2, :] = grad_gain_cross
 
 
-def self_backward(target_len, bucket_count, operands):
+def self_backward(target_len, bucket_count, owners, operands):
     targets = operands[9]
-    packed = operands[10]
     bias = operands[11]
     rows, width = targets.shape
+    half = (owners.shape[0] // 2, 15 * group_rows, lane_tile)
+    whole = pl.BlockSpec(memory_space=pltpu.VMEM)
 
     def body(*refs):
         self_backward_kernel(target_len, *refs)
@@ -681,15 +748,22 @@
         body,
         out_shape=[
             jax.ShapeDtypeStruct((rows, width), bf16),
-            jax.ShapeDtypeStruct((packed.shape[0], 15 * group_rows, lane_tile), bf16),
+            jax.ShapeDtypeStruct(half, bf16),
+            jax.ShapeDtypeStruct(half, bf16),
             jax.ShapeDtypeStruct((2, width), f32),
             jax.ShapeDtypeStruct((bucket_count, bias.shape[0], bias.shape[2]), f32),
         ],
+        in_specs=[pl.BlockSpec(memory_space=pltpu.SMEM)] + [whole] * len(operands),
         scratch_shapes=[pltpu.VMEM((rows, width), bf16)] * 4
-        + [pltpu.VMEM((rows, width), f32), pltpu.VMEM(bias.shape, f32)],
+        + [
+            pltpu.VMEM((rows, width), f32),
+            pltpu.VMEM(bias.shape, f32),
+            pltpu.VMEM((width, lane_tile), f32),
+        ],
         compiler_params=params(),
+        cost_estimate=cost(40 * targets.size * width, 20 * targets.size),
         name="self_backward",
-    )(*operands)
+    )(owners, *operands)
 
 
 def pack(shard):
@@ -734,19 +808,71 @@
 def scatter(packed, shapes, groups, devices):
     packed = regroup(packed, groups, devices, shapes)
     share = lax.psum_scatter(packed, axes, scatter_dimension=0, tiled=False)
+    return split_share(share, shapes, devices)
+
+
+core_step = (2,)
+plane_steps = (1, 4, 5)
+line_steps = (8, 16, 24)
+
+
+def exchange(values, step):
+    return lax.ppermute(values, axes, [(i, i ^ step) for i in range(32)])
+
+
+def slot_tables():
+    here = lax.axis_index(axes)
+    device = jnp.arange(32, dtype=jnp.int32)
+    gap = device ^ here
+    slots = ((gap >> 1) & 1) * 16 + ((gap & 1) + ((gap >> 2) & 1) * 2) * 4 + (gap >> 3)
+    far = device & 15
+    owners = here ^ ((device >> 4) * 2 + (far >> 2 & 1) + (far >> 3) * 4 + (far & 3) * 8)
+    return slots.astype(jnp.int32), owners.astype(jnp.int32)
+
+
+def permute_gather(shard):
+    line = jnp.stack([shard] + [exchange(shard, step) for step in line_steps])
+    plane = jnp.concatenate([line] + [exchange(line, step) for step in plane_steps])
+    return jnp.concatenate([plane, exchange(plane, core_step[0])])
+
+
+def pair_sum(keep, send):
+    return (keep.astype(f32) + exchange(send, core_step[0]).astype(f32)).astype(bf16)
+
+
+def permute_scatter(pair):
+    parts = [pair[4 * j : 4 * j + 4] for j in range(4)]
+    total = parts[0].astype(f32)
+    for part, step in zip(parts[1:], plane_steps):
+        total = total + exchange(part, step).astype(f32)
+    total = total.astype(bf16)
+    final = total[0].astype(f32)
+    for k, step in enumerate(line_steps):
+        final = final + exchange(total[k + 1], step).astype(f32)
+    return final
+
+
+def permute_sum(values):
+    values = values + exchange(values, core_step[0])
+    for steps in (plane_steps, line_steps):
+        first, second, third = (exchange(values, step) for step in steps)
+        values = (values + first) + (second + third)
+    return values
+
+
+def split_share(share, shapes, devices):
     parts = []
     offset = 0
     for rows, columns in shapes:
         size = rows // devices * (columns // lane_tile)
-        parts.append(
-            unpack(share[offset : offset + size], rows // devices, columns).astype(f32)
-        )
+        parts.append(unpack(share[offset : offset + size], rows // devices, columns).astype(f32))
         offset += size
     return parts
 
 
 def on_device(
     devices,
+    direct,
     targets,
     memory,
     mem_lengths,
@@ -776,16 +902,30 @@
     feed_width = gate_weight.shape[1]
     feed_shapes = [(width, feed_width), (width, feed_width), (feed_width, width)]
 
-    packed_memory = gather([cross_key, cross_value], [square] * 2, groups, devices)
+    own_gains = jnp.stack([gain_self, gain_cross, gain_feed])
+    if direct:
+        slots, owners = slot_tables()
+        extra = jnp.pad(own_gains.reshape(1, -1), ((0, 15), (0, lane_tile - own_gains.size)))
+        packed_memory = permute_gather(
+            jnp.concatenate([pack(cross_key), pack(cross_value), extra], axis=0)
+        )
+        hot = (slots[:, None] == jnp.arange(groups)[None, :]).astype(bf16)
+        gains = (
+            dot(hot, packed_memory[:, -16, : own_gains.size])
+            .reshape(groups, 3, group_rows)
+            .transpose(1, 0, 2)
+            .reshape(3, width)
+        )
+    else:
+        slots = owners = jnp.arange(groups, dtype=jnp.int32)
+        packed_memory = gather([cross_key, cross_value], [square] * 2, groups, devices)
+        gains = lax.all_gather(own_gains, axes, axis=1, tiled=True).astype(f32)
     packed_self = gather(
         [self_query, self_key, self_value, self_output, cross_query, cross_output],
         [square] * 6,
         groups,
         devices,
     )
-    gains = lax.all_gather(
-        jnp.stack([gain_self, gain_cross, gain_feed]), axes, axis=1, tiled=True
-    ).astype(f32)
     packed_feed = gather([gate_weight, up_weight, down_weight], feed_shapes, groups, devices)
 
     pad = pair_width - target_len
@@ -811,7 +951,9 @@
     target_rows = targets.reshape(row_count, width)
     cot_rows = cotangent.reshape(row_count, width)
 
-    mem_keys, mem_values = project_memory(mem_lengths, memory, packed_memory)
+    mem_keys, mem_values, memory_weight = project_memory(
+        mem_lengths, slots, memory, packed_memory
+    )
     normed_one, queries, key_rows, value_rows, self_context, after_self, normed_two, side = (
         self_forward(target_len, target_rows, packed_self, bias, gains[0:1], gains[1:2])
     )
@@ -825,9 +967,10 @@
     grad_side, grad_mem_keys, grad_mem_values = cross_backward(
         mem_lengths, grad_context, cross_context, side, mem_keys, mem_values, weights
     )
-    target_grad, self_grads, grad_gains, table_parts = self_backward(
+    target_grad, self_keep, self_send, grad_gains, table_parts = self_backward(
         target_len,
         bucket_count,
+        owners,
         (
             grad_side,
             after_self,
@@ -846,22 +989,41 @@
             gains[1:2],
         ),
     )
-    share_query, share_key, share_value, share_output, share_cross_query = scatter(
-        self_grads, [square] * 5, groups, devices
-    )
-    memory_grads = memory_weight_grads(
-        mem_lengths, memory, grad_mem_keys, grad_mem_values, packed_memory.shape
-    )
-    share_cross_key, share_cross_value = scatter(memory_grads, [square] * 2, groups, devices)
-    memory_grad = memory_gradient(mem_lengths, grad_mem_keys, grad_mem_values, packed_memory)
-
+    grad_mem_keys, grad_mem_values, self_keep = lax.optimization_barrier(
+        (grad_mem_keys, grad_mem_values, self_keep)
+    )
+    memory_keep, memory_send = memory_weight_grads(
+        mem_lengths, owners, memory, grad_mem_keys, grad_mem_values
+    )
     table_part = (
         table_parts.reshape(bucket_count, head_count, pair_width).sum(axis=-1).reshape(-1)
     )
     small = jnp.concatenate(
         [grad_gains[0], grad_gains[1], grad_gain_feed[0], table_part], axis=0
     )
-    small = jnp.sum(lax.all_gather(small, axes, axis=0, tiled=False), axis=0)
+    if direct:
+        self_pair = pair_sum(self_keep, self_send)
+        memory_weight, self_pair = lax.optimization_barrier((memory_weight, self_pair))
+    memory_grad = memory_gradient(mem_lengths, grad_mem_keys, grad_mem_values, memory_weight)
+    if direct:
+        self_shares = permute_scatter(self_pair)
+        memory_grad, memory_keep, memory_send, small = lax.optimization_barrier(
+            (memory_grad, memory_keep, memory_send, small)
+        )
+        memory_shares = permute_scatter(pair_sum(memory_keep, memory_send))
+        share_cross_key, share_cross_value = split_share(memory_shares, [square] * 2, devices)
+        share_query, share_key, share_value, share_output, share_cross_query = split_share(
+            self_shares, [square] * 5, devices
+        )
+        small = permute_sum(small)
+    else:
+        share_cross_key, share_cross_value = scatter(
+            jnp.concatenate([memory_keep, memory_send]), [square] * 2, groups, devices
+        )
+        share_query, share_key, share_value, share_output, share_cross_query = scatter(
+            jnp.concatenate([self_keep, self_send]), [square] * 5, groups, devices
+        )
+        small = jnp.sum(lax.all_gather(small, axes, axis=0, tiled=False), axis=0)
     table_grad = small[3 * width :].reshape(bucket_count, head_count)
     own = width // devices
     place = lax.axis_index(axes) * own
@@ -893,12 +1055,13 @@
 
 def solution(mesh):
     devices = mesh.shape["dp"] * mesh.shape["seq"]
+    direct = mesh.shape["dp"] == 16 and mesh.shape["seq"] == 2
     rows = P(axes, None, None)
     flat = P(axes)
     weight = P(axes, None)
 
     def body(*arguments):
-        return on_device(devices, *arguments)
+        return on_device(devices, direct, *arguments)
 
     return jax.shard_map(
         body,

time: 708 us -> 441 us (0.62)
  waiting for transfers between devices: 297 us -> 84.6 us
  blocking collectives: 112 us -> 0 us
  starting transfers between devices: 0.25 us -> 34.3 us
  Pallas kernels: 251 us -> 264 us
  other arithmetic: 1.8 us -> 9.99 us
    reduce_scatter x3 -> x1, waiting for transfers between devices: 226 us -> 0.01 us  [scatter(): share = lax.psum_scatter(packed, axes, scatter_dimension=0, tiled=False)]
    all_gather x2 -> x0, blocking collectives: 112 us -> none  [the longest x1 56.1 us: on_device(): lax.all_gather(jnp.stack([gain_self, gain_cross, gain_feed]), axes, axis=...]
    ppermute x0 -> x28, waiting for transfers between devices: none -> 47.7 us  [exchange(): return lax.ppermute(values, axes, [(i, i ^ step) for i in range(32)])]
    ppermute x0 -> x28, starting transfers between devices: none -> 34.1 us  [exchange(): return lax.ppermute(values, axes, [(i, i ^ step) for i in range(32)])]
    all_gather x3 -> x2, waiting for transfers between devices: 69.8 us -> 36.8 us  [gather(): whole = lax.all_gather(packed, axes, axis=0, tiled=False)]
    pallas_call x1, Pallas kernels: 48.7 us -> 59.1 us  [self_backward(): pl.pallas_call(body, out_shape=[jax.ShapeDtypeStruct((rows, width), bf16)...]
    convert_element_type x0 -> x4, other arithmetic: none -> 7.27 us  [the longest x2 5.06 us: pair_sum(): (keep.astype(f32) + exchange(send, core_step[0]).astype(f32)).astype(bf16)]
  transfers between devices with their start and end apart: 6 -> 31, of which waited for: 4 -> 18; matrix products, arithmetic and copies ran while one was open for 2% -> 6% of each run, Pallas kernels for 23% -> 52%
where the time goes in v2:
time: 441 us; the launch traced here: 436 us
  Pallas kernels  264 us (60%)
  waiting for transfers between devices  84.6 us (19%)
  starting transfers between devices  34.3 us (8%)
  local copies, waits for them, and re-layouts  27.8 us (6%)
  between operations  14.6 us (3%)
  other arithmetic  9.99 us (2%)
    pallas_call x1, Pallas kernels, self_backward(): pl.pallas_call(body, out_shape=[jax.ShapeDtypeStruct((rows, width), bf16)...  59.1 us
    ppermute x28, waiting for transfers between devices, exchange(): return lax.ppermute(values, axes, [(i, i ^ step) for i in range(32)])  47.7 us
    pallas_call x1, Pallas kernels, feed_both(): pl.pallas_call(feed_kernel, out_shape=[jax.ShapeDtypeStruct((rows, width)...  38.1 us
    all_gather x2, waiting for transfers between devices, gather(): whole = lax.all_gather(packed, axes, axis=0, tiled=False)  36.8 us
    ppermute x28, starting transfers between devices, exchange(): return lax.ppermute(values, axes, [(i, i ^ step) for i in range(32)])  34.1 us
    pallas_call x1, Pallas kernels, cross_backward(): pl.pallas_call(cross_backward_kernel, out_shape=[jax.ShapeDtypeStruct(sid...  31.3 us
    pallas_call x1, Pallas kernels, self_forward(): pl.pallas_call(body, out_shape=[low, low, low, low, low, wide, low, low],...  29.4 us
    pallas_call x1, Pallas kernels, cross_forward(): pl.pallas_call(cross_forward_kernel, out_shape=[jax.ShapeDtypeStruct(side...  28.5 us
  transfers between devices with their start and end apart: 31, of which 18 were waited for; matrix products, arithmetic and copies ran while one was open for 6% of the time, Pallas kernels for 52%

profile of v2, /device:TPU:8, one launch (start us, length us, event | category | flops | bytes accessed | tf_op | source)
XLA Modules:
  0.0 435.9 jit_solution(5291387274646583215)
XLA Ops:
  14.4 3.0 collective-permute-start.1
  18.8 4.4 %collective-permute-done.1 = bf16[160,256]{1,0:T(8,128)(2,1)S(1)} collective-permute-done((bf16[160,256]{1,0:T(8,128)(2,1)S(1)}, bf16[160,256]{1,0:T(8,128)(2,1)S(1)}, u32[]{:S(2)}, u32[]{:S(2)}) %collective-permute-start.1) | collective-permute-done | bytes 81952 | tf_op jit(solution)/shard_map/ppermute | solution.py:820
  23.2 2.0 collective-permute-done.2
  28.8 7.0 %collective-permute-done.3 = bf16[4,160,256]{2,1,0:T(8,128)(2,1)S(1)} collective-permute-done((bf16[4,160,256]{2,1,0:T(8,128)(2,1)S(1)}, bf16[4,160,256]{2,1,0:T(8,128)(2,1)S(1)}, u32[]{:S(2)}, u32[]{:S(2)}) %collective-permute-start.3) | collective-permute-done | bytes 327712 | tf_op jit(solution)/shard_map/ppermute | solution.py:820
  35.9 5.0 %collective-permute-done.4 = bf16[4,160,256]{2,1,0:T(8,128)(2,1)S(1)} collective-permute-done((bf16[4,160,256]{2,1,0:T(8,128)(2,1)S(1)}, bf16[4,160,256]{2,1,0:T(8,128)(2,1)S(1)}, u32[]{:S(2)}, u32[]{:S(2)}) %collective-permute-start.4) | collective-permute-done | bytes 327712 | tf_op jit(solution)/shard_map/ppermute | solution.py:820
  49.9 25.9 %memory_project.1 = (bf16[8,1024,768]{2,1,0:T(8,128)(2,1)}, bf16[8,1024,768]{2,1,0:T(8,128)(2,1)}, bf16[768,1536]{1,0:T(8,128)(2,1)}) custom-call(s32[8]{0:T(128)} %lengths.9, s32[32]{0:T(128)} %copy-done.16, bf16[8,1024,768]{2,1,0:T(8,128)(2,1)} %memory_ref.3, bf16[32,160,256]{2,1,0:T(8,128)(2,1)} %constant_dynamic-update-slice_fusion.13.packed_ref), custom_call_target="tpu_custom_call" | custom-call | flops 19327352832 | bytes 37748736 | tf_op jit(solution)/shard_map/memory_project/pallas_call | solution.py:143
  75.8 11.2 %all-gather.5.cloned.1.call-done = bf16[13824,256]{1,0:T(8,128)(2,1)} async-done(((bf16[432,256]{1,0:T(8,128)(2,1)}), bf16[13824,256]{1,0:T(8,128)(2,1)}) %all-gather.5.cloned.1.call-update) | async-done | bytes 7077904 | tf_op jit(solution)/shard_map/all_gather | solution.py:804
  87.0 29.4 %self_forward.1 = (bf16[768,768]{1,0:T(8,128)(2,1)}, bf16[768,768]{1,0:T(8,128)(2,1)}, bf16[768,768]{1,0:T(8,128)(2,1)}, bf16[768,768]{1,0:T(8,128)(2,1)}, bf16[...) custom-call(bf16[768,768]{1,0:T(8,128)(2,1)} %bitcast.222, ...), custom_call_target="tpu_custom_call" | custom-call | flops 9059696640 | bytes 9437184 | tf_op jit(solution)/shard_map/self_forward/pallas_call | solution.py:233
  116.4 28.5 %cross_forward.1 = (bf16[768,768]{1,0:T(8,128)(2,1)}, bf16[8,1152,1024]{2,1,0:T(8,128)(2,1)}) custom-call(s32[8]{0:T(128)} %lengths.9, bf16[768,768]{1,0:T(8,128)(2,1)} %get-tuple-element.56.side_ref, bf16[8,1024,768]{2,1,0:T(8,128)(2,1)} %get-tuple-element.57.keys_ref, bf16[8,1024,768]{2,1,0:T(8,128)(2,1)} %get-tuple-element.58.values_ref), custom_call_target="tpu_custom_call" | custom-call | flops 9663676416 | bytes 37748736 | tf_op jit(solution)/shard_map/cross_forward/pallas_call | solution.py:282
  144.9 25.6 %all-gather.7.cloned.1.call-done = bf16[18432,256]{1,0:T(8,128)(2,1)} async-done(((bf16[576,256]{1,0:T(8,128)(2,1)}), bf16[18432,256]{1,0:T(8,128)(2,1)}) %all-gather.7.cloned.1.call-update) | async-done | bytes 9437200 | tf_op jit(solution)/shard_map/all_gather | solution.py:804
  170.5 38.1 %feed_both.1 = (bf16[768,768]{1,0:T(8,128)(2,1)}, f32[768,768]{1,0:T(8,128)}, bf16[768,768]{1,0:T(8,128)(2,1)}, f32[1,768]{1,0:T(1,128)}, bf16[32,648,256]{2,1,0:T(8,128)(2,1)}) custom-call(f32[768,768]{1,0:T(8,128)} %get-tuple-element.55.after_ref.refs_2_, bf16[768,768]{1,0:T(8,128)(2,1)} %get-tuple-element.59.context_ref, bf16[768,768]{1,0:T(8,128)(2,1)} %bitcast.221, ...), custom_call_target="tpu_custom_call" | custom-call | flops 21743271936 | bytes 17694720 | tf_op jit(solution)/shard_map/feed_both/pallas_call | solution.py:399
  209.8 31.3 %cross_backward.1 = (bf16[768,768]{1,0:T(8,128)(2,1)}, bf16[8,768,1024]{2,1,0:T(8,128)(2,1)}, bf16[8,768,1024]{2,1,0:T(8,128)(2,1)}) custom-call(s32[8]{0:T(128)} %lengths.9, bf16[768,768]{1,0:T(8,128)(2,1)} %get-tuple-element.61.grad_ref, bf16[768,768]{1,0:T(8,128)(2,1)} %get-tuple-element.59.context_ref, bf16[768,768]{1,0:T(8,128)(2,1)} %get-tuple-element.56.side_ref, ...), custom_call_target="tpu_custom_call" | custom-call | flops 19327352832 | bytes 62914560 | tf_op jit(solution)/shard_map/cross_backward/pallas_call | solution.py:488
  241.1 59.1 %self_backward.1 = (bf16[768,768]{1,0:T(8,128)(2,1)}, bf16[16,360,256]{2,1,0:T(8,128)(2,1)}, bf16[16,360,256]{2,1,0:T(8,128)(2,1)}, f32[2,768]{1,0:T(2,128)}, f32[32,6,256]{2,1,0:T(8,128)}) custom-call(s32[32]{0:T(128)} %fusion.23.refs_0_.owners, bf16[768,768]{1,0:T(8,128)(2,1)} %get-tuple-element.63.refs_1_, ...), custom_call_target="tpu_custom_call" | custom-call | flops 18119393280 | bytes 11796480 | tf_op jit(solution)/shard_map/self_backward/pallas_call | solution.py:747
  303.6 26.5 %memory_weight_grads.1 = (bf16[16,144,256]{2,1,0:T(8,128)(2,1)}, bf16[16,144,256]{2,1,0:T(8,128)(2,1)}) custom-call(s32[8]{0:T(128)} %lengths.9, s32[32]{0:T(128)} %fusion.23.refs_0_.owners, bf16[8,1024,768]{2,1,0:T(8,128)(2,1)} %memory_ref.3, bf16[8,768,1024]{2,1,0:T(8,128)(2,1)} %get-tuple-element.75.grad_keys_ref, ...), custom_call_target="tpu_custom_call" | custom-call | flops 19327352832 | bytes 37748736 | tf_op jit(solution)/shard_map/memory_weight_grads/pallas_call | solution.py:563
  330.1 3.5 add_convert_fusion
  335.0 2.4 collective-permute-start.16
  338.9 25.3 %memory_grad.1 = bf16[8,1024,768]{2,1,0:T(8,128)(2,1)} custom-call(s32[8]{0:T(128)} %lengths.9, bf16[8,768,1024]{2,1,0:T(8,128)(2,1)} %get-tuple-element.75.grad_keys_ref, bf16[8,768,1024]{2,1,0:T(8,128)(2,1)} %get-tuple-element.76.grad_values_ref, bf16[768,1536]{1,0:T(8,128)(2,1)} %get-tuple-element.80.weight_ref), custom_call_target="tpu_custom_call" | custom-call | flops 19327352832 | bytes 37748736 | tf_op jit(solution)/shard_map/memory_grad/pallas_call | solution.py:613
  364.7 2.7 collective-permute-done.8
  367.4 2.1 collective-permute-start.10
  369.5 2.4 collective-permute-done.10
  372.8 3.7 collective-permute-done.11
  377.1 3.1 collective-permute-done.9
  380.2 2.9 collective-permute-start.12
  383.1 1.7 collective-permute-done.12
  384.8 1.6 collective-permute-start.13
  386.4 3.0 collective-permute-done.13
  390.0 3.1 collective-permute-done.14
  393.1 2.0 add_convert_fusion.2
  396.0 4.0 collective-permute-start.18
  403.6 2.0 collective-permute-start.23
  408.1 6.1 %collective-permute-done.20 = bf16[360,256]{1,0:T(8,128)(2,1)} collective-permute-done((bf16[360,256]{1,0:T(8,128)(2,1)S(1)}, bf16[360,256]{1,0:T(8,128)(2,1)}, u32[]{:S(2)}, u32[]{:S(2)}) %collective-permute-start.20) | collective-permute-done | bytes 184352 | tf_op jit(solution)/shard_map/ppermute | solution.py:820
  416.6 2.5 collective-permute-start.27
  (182 shorter events, 50.0 us)
Async XLA Ops:
  7.2 79.8 %all-gather.5.cloned.1.call-start = ((), (), s32[]{:S(2)}) async-start(), calls=%async_computation.2 | async-start | bytes 7299072 | tf_op jit(solution)/shard_map/all_gather | solution.py:804
  13.0 157.5 %all-gather.7.cloned.1.call-start = ((), (), s32[]{:S(2)}) async-start(), calls=%async_computation.3 | async-start | bytes 9732096 | tf_op jit(solution)/shard_map/all_gather | solution.py:804
  14.0 411.3 %reduce-scatter.2.cloned.1.call-start = ((), (), s32[]{:S(2)}) async-start(), calls=%async_computation.1 | async-start | bytes 10948608 | tf_op jit(solution)/shard_map/reduce_scatter | solution.py:810
  14.3 4.5 %collective-permute-start = (bf16[160,256]{1,0:T(8,128)(2,1)S(1)}, bf16[160,256]{1,0:T(8,128)(2,1)S(1)}, u32[]{:S(2)}, u32[]{:S(2)}) collective-permute-start(bf16[160,256]{1,0:T(8,128)(2,1)S(1)} %get-tuple-element.167), channel_id=1, source_target_pairs={{0,8},{1,9},{2,10},{3,11},{4,12},{5,13},{6,14},{7,15},{8,0},{9,1},... | collective-permute-start | bytes 245768 | tf_op jit(solution)/shard_map/ppermute | solution.py:820
  14.4 8.8 %collective-permute-start.1 = (bf16[160,256]{1,0:T(8,128)(2,1)S(1)}, bf16[160,256]{1,0:T(8,128)(2,1)S(1)}, u32[]{:S(2)}, u32[]{:S(2)}) collective-permute-start(bf16[160,256]{1,0:T(8,128)(2,1)S(1)} %get-tuple-element.167), channel_id=1, source_target_pairs={{0,16},{1,17},{2,18},{3,19},{4,20},{5,21},{6,22},{7,23},{8,24},{9,... | collective-permute-start | bytes 245768 | tf_op jit(solution)/shard_map/ppermute | solution.py:820
  17.4 7.8 %collective-permute-start.2 = (bf16[160,256]{1,0:T(8,128)(2,1)S(1)}, bf16[160,256]{1,0:T(8,128)(2,1)S(1)}, u32[]{:S(2)}, u32[]{:S(2)}) collective-permute-start(bf16[160,256]{1,0:T(8,128)(2,1)S(1)} %get-tuple-element.167), channel_id=1, source_target_pairs={{0,24},{1,25},{2,26},{3,27},{4,28},{5,29},{6,30},{7,31},{8,16},{9,... | collective-permute-start | bytes 245768 | tf_op jit(solution)/shard_map/ppermute | solution.py:820
  25.2 10.6 %collective-permute-start.3 = (bf16[4,160,256]{2,1,0:T(8,128)(2,1)S(1)}, bf16[4,160,256]{2,1,0:T(8,128)(2,1)S(1)}, u32[]{:S(2)}, u32[]{:S(2)}) collective-permute-start(bf16[4,160,256]{2,1,0:T(8,128)(2,1)S(1)} %pad_maximum_fusion), channel_id=1, source_target_pairs={{0,1},{1,0},{2,3},{3,2},{4,5},{5,4},{6,7},{7,6},{8,9},{9,8},{10,11... | collective-permute-start | bytes 983048 | tf_op jit(solution)/shard_map/ppermute | solution.py:820
  26.6 14.3 %collective-permute-start.4 = (bf16[4,160,256]{2,1,0:T(8,128)(2,1)S(1)}, bf16[4,160,256]{2,1,0:T(8,128)(2,1)S(1)}, u32[]{:S(2)}, u32[]{:S(2)}) collective-permute-start(bf16[4,160,256]{2,1,0:T(8,128)(2,1)S(1)} %pad_maximum_fusion), channel_id=1, source_target_pairs={{0,4},{1,5},{2,6},{3,7},{4,0},{5,1},{6,2},{7,3},{8,12},{9,13},{10,... | collective-permute-start | bytes 983048 | tf_op jit(solution)/shard_map/ppermute | solution.py:820
  28.1 14.1 %collective-permute-start.5 = (bf16[4,160,256]{2,1,0:T(8,128)(2,1)S(1)}, bf16[4,160,256]{2,1,0:T(8,128)(2,1)S(1)}, u32[]{:S(2)}, u32[]{:S(2)}) collective-permute-start(bf16[4,160,256]{2,1,0:T(8,128)(2,1)S(1)} %pad_maximum_fusion), channel_id=1, source_target_pairs={{0,5},{1,4},{2,7},{3,6},{4,1},{5,0},{6,3},{7,2},{8,13},{9,12},{10,... | collective-permute-start | bytes 983048 | tf_op jit(solution)/shard_map/ppermute | solution.py:820
  42.3 3.1 collective-permute-start.6
  241.1 61.7 %copy-start.12 = (f32[1,768]{1,0:T(1,128)S(1)}, f32[1,768]{1,0:T(1,128)}, u32[]{:S(2)}) copy-start(f32[1,768]{1,0:T(1,128)} %get-tuple-element.84) | copy-start | bytes 9220
  300.3 29.8 %collective-permute-start.7 = (bf16[16,360,256]{2,1,0:T(8,128)(2,1)}, bf16[16,360,256]{2,1,0:T(8,128)(2,1)}, u32[]{:S(2)}, u32[]{:S(2)}) collective-permute-start(bf16[16,360,256]{2,1,0:T(8,128)(2,1)} %get-tuple-element.79), channel_id=1, source_target_pairs={{0,2},{1,3},{2,0},{3,1},{4,6},{5,7},{6,4},{7,5},{8,10},{9,11},{10,... | collective-permute-start | bytes 8847368 | tf_op jit(solution)/shard_map/ppermute | solution.py:820
  335.0 58.1 %collective-permute-start.15 = (bf16[4,360,256]{2,1,0:T(8,128)(2,1)}, bf16[4,360,256]{2,1,0:T(8,128)(2,1)}, u32[]{:S(2)}, u32[]{:S(2)}) collective-permute-start(bf16[4,360,256]{2,1,0:T(8,128)(2,1)} %get-tuple-element.130), channel_id=1, source_target_pairs={{0,1},{1,0},{2,3},{3,2},{4,5},{5,4},{6,7},{7,6},{8,9},{9,8},{10,11... | collective-permute-start | bytes 2211848 | tf_op jit(solution)/shard_map/ppermute | solution.py:820
  335.0 58.1 %collective-permute-start.16 = (bf16[4,360,256]{2,1,0:T(8,128)(2,1)}, bf16[4,360,256]{2,1,0:T(8,128)(2,1)}, u32[]{:S(2)}, u32[]{:S(2)}) collective-permute-start(bf16[4,360,256]{2,1,0:T(8,128)(2,1)} %get-tuple-element.132), channel_id=1, source_target_pairs={{0,4},{1,5},{2,6},{3,7},{4,0},{5,1},{6,2},{7,3},{8,12},{9,13},{10,... | collective-permute-start | bytes 2211848 | tf_op jit(solution)/shard_map/ppermute | solution.py:820
  337.5 55.7 %collective-permute-start.17 = (bf16[4,360,256]{2,1,0:T(8,128)(2,1)}, bf16[4,360,256]{2,1,0:T(8,128)(2,1)}, u32[]{:S(2)}, u32[]{:S(2)}) collective-permute-start(bf16[4,360,256]{2,1,0:T(8,128)(2,1)} %get-tuple-element.131), channel_id=1, source_target_pairs={{0,5},{1,4},{2,7},{3,6},{4,1},{5,0},{6,3},{7,2},{8,13},{9,12},{10,... | collective-permute-start | bytes 2211848 | tf_op jit(solution)/shard_map/ppermute | solution.py:820
  364.2 37.3 %collective-permute-start.21 = (bf16[16,144,256]{2,1,0:T(8,128)(2,1)}, bf16[16,144,256]{2,1,0:T(8,128)(2,1)}, u32[]{:S(2)}, u32[]{:S(2)}) collective-permute-start(bf16[16,144,256]{2,1,0:T(8,128)(2,1)} %get-tuple-element.90), channel_id=1, source_target_pairs={{0,2},{1,3},{2,0},{3,1},{4,6},{5,7},{6,4},{7,5},{8,10},{9,11},{10,... | collective-permute-start | bytes 3538952 | tf_op jit(solution)/shard_map/ppermute | solution.py:820
  364.2 3.2 collective-permute-start.8
  367.4 4.5 %collective-permute-start.10 = (f32[2688]{0:T(1024)S(1)}, f32[2688]{0:T(1024)S(1)}, u32[]{:S(2)}, u32[]{:S(2)}) collective-permute-start(f32[2688]{0:T(1024)S(1)} %add.122), channel_id=1, source_target_pairs={{0,4},{1,5},{2,6},{3,7},{4,0},{5,1},{6,2},{7,3},{8,12},{9,13},{10,... | collective-permute-start | bytes 32264 | tf_op jit(solution)/shard_map/ppermute | solution.py:820
  371.9 4.6 %collective-permute-start.11 = (f32[2688]{0:T(1024)S(1)}, f32[2688]{0:T(1024)S(1)}, u32[]{:S(2)}, u32[]{:S(2)}) collective-permute-start(f32[2688]{0:T(1024)S(1)} %add.122), channel_id=1, source_target_pairs={{0,5},{1,4},{2,7},{3,6},{4,1},{5,0},{6,3},{7,2},{8,13},{9,12},{10,... | collective-permute-start | bytes 32264 | tf_op jit(solution)/shard_map/ppermute | solution.py:820
  376.5 3.7 collective-permute-start.9
  380.2 4.6 %collective-permute-start.12 = (f32[2688]{0:T(1024)S(1)}, f32[2688]{0:T(1024)S(1)}, u32[]{:S(2)}, u32[]{:S(2)}) collective-permute-start(f32[2688]{0:T(1024)S(1)} %add_add_fusion.1), channel_id=1, source_target_pairs={{0,8},{1,9},{2,10},{3,11},{4,12},{5,13},{6,14},{7,15},{8,0},{9,1},... | collective-permute-start | bytes 32264 | tf_op jit(solution)/shard_map/ppermute | solution.py:820
  384.8 4.6 %collective-permute-start.13 = (f32[2688]{0:T(1024)S(1)}, f32[2688]{0:T(1024)S(1)}, u32[]{:S(2)}, u32[]{:S(2)}) collective-permute-start(f32[2688]{0:T(1024)S(1)} %add_add_fusion.1), channel_id=1, source_target_pairs={{0,16},{1,17},{2,18},{3,19},{4,20},{5,21},{6,22},{7,23},{8,24},{9,... | collective-permute-start | bytes 32264 | tf_op jit(solution)/shard_map/ppermute | solution.py:820
  389.4 3.7 collective-permute-start.14
  396.0 9.6 %collective-permute-start.18 = (bf16[360,256]{1,0:T(8,128)(2,1)S(1)}, bf16[360,256]{1,0:T(8,128)(2,1)S(1)}, u32[]{:S(2)}, u32[]{:S(2)}) collective-permute-start(bf16[360,256]{1,0:T(8,128)(2,1)S(1)} %get-tuple-element.136), channel_id=1, source_target_pairs={{0,8},{1,9},{2,10},{3,11},{4,12},{5,13},{6,14},{7,15},{8,0},{9,1},... | collective-permute-start | bytes 552968 | tf_op jit(solution)/shard_map/ppermute | solution.py:820
  400.0 8.1 %collective-permute-start.19 = (bf16[360,256]{1,0:T(8,128)(2,1)}, bf16[360,256]{1,0:T(8,128)(2,1)S(1)}, u32[]{:S(2)}, u32[]{:S(2)}) collective-permute-start(bf16[360,256]{1,0:T(8,128)(2,1)} %get-tuple-element.138), channel_id=1, source_target_pairs={{0,16},{1,17},{2,18},{3,19},{4,20},{5,21},{6,22},{7,23},{8,24},{9,... | collective-permute-start | bytes 552968 | tf_op jit(solution)/shard_map/ppermute | solution.py:820
  400.0 14.2 %collective-permute-start.20 = (bf16[360,256]{1,0:T(8,128)(2,1)S(1)}, bf16[360,256]{1,0:T(8,128)(2,1)}, u32[]{:S(2)}, u32[]{:S(2)}) collective-permute-start(bf16[360,256]{1,0:T(8,128)(2,1)S(1)} %get-tuple-element.137), channel_id=1, source_target_pairs={{0,24},{1,25},{2,26},{3,27},{4,28},{5,29},{6,30},{7,31},{8,16},{9,... | collective-permute-start | bytes 552968 | tf_op jit(solution)/shard_map/ppermute | solution.py:820
  403.1 12.2 %collective-permute-start.22 = (bf16[4,144,256]{2,1,0:T(8,128)(2,1)S(1)}, bf16[4,144,256]{2,1,0:T(8,128)(2,1)S(1)}, u32[]{:S(2)}, u32[]{:S(2)}) collective-permute-start(bf16[4,144,256]{2,1,0:T(8,128)(2,1)S(1)} %get-tuple-element.133), channel_id=1, source_target_pairs={{0,1},{1,0},{2,3},{3,2},{4,5},{5,4},{6,7},{7,6},{8,9},{9,8},{10,11... | collective-permute-start | bytes 884744 | tf_op jit(solution)/shard_map/ppermute | solution.py:820
  403.6 11.8 %collective-permute-start.23 = (bf16[4,144,256]{2,1,0:T(8,128)(2,1)S(1)}, bf16[4,144,256]{2,1,0:T(8,128)(2,1)S(1)}, u32[]{:S(2)}, u32[]{:S(2)}) collective-permute-start(bf16[4,144,256]{2,1,0:T(8,128)(2,1)S(1)} %get-tuple-element.135), channel_id=1, source_target_pairs={{0,4},{1,5},{2,6},{3,7},{4,0},{5,1},{6,2},{7,3},{8,12},{9,13},{10,... | collective-permute-start | bytes 884744 | tf_op jit(solution)/shard_map/ppermute | solution.py:820
  405.6 9.8 %collective-permute-start.24 = (bf16[4,144,256]{2,1,0:T(8,128)(2,1)S(1)}, bf16[4,144,256]{2,1,0:T(8,128)(2,1)S(1)}, u32[]{:S(2)}, u32[]{:S(2)}) collective-permute-start(bf16[4,144,256]{2,1,0:T(8,128)(2,1)S(1)} %get-tuple-element.134), channel_id=1, source_target_pairs={{0,5},{1,4},{2,7},{3,6},{4,1},{5,0},{6,3},{7,2},{8,13},{9,12},{10,... | collective-permute-start | bytes 884744 | tf_op jit(solution)/shard_map/ppermute | solution.py:820
  415.6 7.0 %collective-permute-start.25 = (bf16[144,256]{1,0:T(8,128)(2,1)S(1)}, bf16[144,256]{1,0:T(8,128)(2,1)S(1)}, u32[]{:S(2)}, u32[]{:S(2)}) collective-permute-start(bf16[144,256]{1,0:T(8,128)(2,1)S(1)} %get-tuple-element.153), channel_id=1, source_target_pairs={{0,8},{1,9},{2,10},{3,11},{4,12},{5,13},{6,14},{7,15},{8,0},{9,1},... | collective-permute-start | bytes 221192 | tf_op jit(solution)/shard_map/ppermute | solution.py:820
  416.6 6.0 %collective-permute-start.26 = (bf16[144,256]{1,0:T(8,128)(2,1)S(1)}, bf16[144,256]{1,0:T(8,128)(2,1)S(1)}, u32[]{:S(2)}, u32[]{:S(2)}) collective-permute-start(bf16[144,256]{1,0:T(8,128)(2,1)S(1)} %get-tuple-element.155), channel_id=1, source_target_pairs={{0,16},{1,17},{2,18},{3,19},{4,20},{5,21},{6,22},{7,23},{8,24},{9,... | collective-permute-start | bytes 221192 | tf_op jit(solution)/shard_map/ppermute | solution.py:820
  416.6 7.2 %collective-permute-start.27 = (bf16[144,256]{1,0:T(8,128)(2,1)S(1)}, bf16[144,256]{1,0:T(8,128)(2,1)S(1)}, u32[]{:S(2)}, u32[]{:S(2)}) collective-permute-start(bf16[144,256]{1,0:T(8,128)(2,1)S(1)} %get-tuple-element.154), channel_id=1, source_target_pairs={{0,24},{1,25},{2,26},{3,27},{4,28},{5,29},{6,30},{7,31},{8,16},{9,... | collective-permute-start | bytes 221192 | tf_op jit(solution)/shard_map/ppermute | solution.py:820
  (17 other events, 120.4 us)
Sparse Core Ops, SparseCore 0:
  13.2 73.8 all-gather.4
  90.5 79.9 all-gather.6
  208.8 140.6 reduce-scatter.1

commit v3 on v2

--- a/solution.py
+++ b/solution.py
@@ -15,6 +15,7 @@
 lane_tile = 256
 group_rows = 24
 pair_width = 128
+pair_group = 3
 NN = (((1,), (0,)), ((), ()))
 NT = (((1,), (1,)), ((), ()))
 TN = (((0,), (0,)), ((), ()))
@@ -39,13 +40,6 @@
 def column_tile(packed_ref, index):
     tile = packed_ref[:, index * group_rows : (index + 1) * group_rows, :]
     return tile.reshape(tile.shape[0] * group_rows, lane_tile)
-
-
-def put_column_tile(packed_ref, index, values):
-    groups = packed_ref.shape[0]
-    packed_ref[:, index * group_rows : (index + 1) * group_rows, :] = values.reshape(
-        groups, group_rows, lane_tile
-    ).astype(bf16)
 
 
 def lane_halves(rows):
@@ -67,21 +61,46 @@
     return total
 
 
-def put_weight_grad(packed_ref, base, rows, grads):
-    for t in range(grads.shape[1] // lane_tile):
-        part = dot(rows, grads[:, t * lane_tile : (t + 1) * lane_tile], TN)
-        put_column_tile(packed_ref, base + t, part)
-
-
-def put_slots(owners, keep_ref, send_ref, stage_ref, index, values):
-    stage_ref[...] = values
+def assemble(owners, near_ref, far_ref, weight_ref):
+    half = near_ref.shape[0]
+    for offset, packed_ref in ((0, near_ref), (half, far_ref)):
+
+        def place(pair, carry):
+            slot = (pair >> 2) * 8 + (pair & 3)
+            owner = owners[offset + slot]
+            odd = owner & 1
+            rows = pl.ds(pl.multiple_of((owner >> 1) * (2 * group_rows), 16), 2 * group_rows)
+            for t in range(weight_ref.shape[1] // lane_tile):
+                part = slice(t * group_rows, (t + 1) * group_rows)
+                weight_ref[rows, t * lane_tile : (t + 1) * lane_tile] = jnp.concatenate(
+                    [
+                        packed_ref[slot + 4 * odd, part, :],
+                        packed_ref[slot + 4 - 4 * odd, part, :],
+                    ],
+                    axis=0,
+                )
+            return carry
+
+        lax.fori_loop(0, half // 2, place, 0)
+
+
+def put_slots(owners, keep_ref, send_ref, stage_ref, extra=None):
     half = keep_ref.shape[0]
-    part = slice(index * group_rows, (index + 1) * group_rows)
+    tiles = stage_ref.shape[1] // lane_tile
 
     def place(slot, carry):
         for offset, out_ref in ((0, keep_ref), (half, send_ref)):
-            start = pl.multiple_of(owners[slot + offset] * group_rows, 8)
-            out_ref[slot, part, :] = stage_ref[pl.ds(start, group_rows), :].astype(bf16)
+            owner = owners[slot + offset]
+            rows = pl.ds(pl.multiple_of(owner * group_rows, 8), group_rows)
+            parts = [
+                stage_ref[rows, t * lane_tile : (t + 1) * lane_tile] for t in range(tiles)
+            ]
+            if extra is not None:
+                parts.append(extra(owner))
+            for t in range(0, len(parts), 2):
+                both = jnp.concatenate(parts[t : t + 2], axis=0).astype(bf16)
+                start = t * group_rows
+                out_ref[slot, start : start + both.shape[0], :] = both
         return carry
 
     lax.fori_loop(0, half, place, 0)
@@ -100,25 +119,15 @@
     return grad_values, grad_gain
 
 
-def memory_kernel(lengths, slots, memory_ref, packed_ref, keys_ref, values_ref, weight_ref):
+def memory_kernel(
+    lengths, owners, memory_ref, near_ref, far_ref, keys_ref, values_ref, weight_ref
+):
     seq = pl.program_id(0)
     memory_len = memory_ref.shape[1]
-    tiles = weight_ref.shape[1] // lane_tile
 
     @pl.when(seq == 0)
     def _():
-        def place(pair, carry):
-            first = slots[2 * pair]
-            second = slots[2 * pair + 1]
-            rows = pl.ds(pl.multiple_of(2 * group_rows * pair, 16), 2 * group_rows)
-            for t in range(tiles):
-                part = slice(t * group_rows, (t + 1) * group_rows)
-                weight_ref[rows, t * lane_tile : (t + 1) * lane_tile] = jnp.concatenate(
-                    [packed_ref[first, part, :], packed_ref[second, part, :]], axis=0
-                )
-            return carry
-
-        lax.fori_loop(0, weight_ref.shape[0] // (2 * group_rows), place, 0)
+        assemble(owners, near_ref, far_ref, weight_ref)
 
     def fill(count):
         rows = memory_ref[0, :count, :]
@@ -137,7 +146,7 @@
         fill(memory_len // 2)
 
 
-def project_memory(mem_lengths, slots, memory, packed):
+def project_memory(mem_lengths, owners, memory, near, far):
     batch, memory_len, width = memory.shape
     block = pl.BlockSpec((1, memory_len, width), lambda b, n, s: (b, 0, 0))
     return pl.pallas_call(
@@ -147,13 +156,13 @@
         grid_spec=pltpu.PrefetchScalarGridSpec(
             num_scalar_prefetch=2,
             grid=(batch,),
-            in_specs=[block, pl.BlockSpec(packed.shape, lambda b, n, s: (0, 0, 0))],
+            in_specs=[block] + [pl.BlockSpec(near.shape, lambda b, n, s: (0, 0, 0))] * 2,
             out_specs=[block, block, pl.BlockSpec((width, 2 * width), lambda b, n, s: (0, 0))],
         ),
         compiler_params=params(),
         cost_estimate=cost(4 * memory.size * width, 6 * memory.size),
         name="memory_project",
-    )(mem_lengths, slots, memory, packed)
+    )(mem_lengths, owners, memory, near, far)
 
 
 def stacked_pair(rows, half, pad):
@@ -175,8 +184,10 @@
 
 def self_forward_kernel(
     target_len,
+    owners,
     targets_ref,
-    packed_ref,
+    near_ref,
+    far_ref,
     bias_ref,
     gain_self_ref,
     gain_cross_ref,
@@ -188,42 +199,50 @@
     after_ref,
     normed_two_ref,
     side_ref,
+    weight_ref,
 ):
+    width = targets_ref.shape[1]
+
+    def weight(index):
+        return weight_ref[:, index * width : (index + 1) * width]
+
+    assemble(owners, near_ref, far_ref, weight_ref)
     inputs = targets_ref[...].astype(f32)
     normed_one = (inputs * norm_scale(inputs) * gain_self_ref[...]).astype(bf16)
     normed_one_ref[...] = normed_one
-    for base, out_ref in ((0, queries_ref), (3, keys_ref), (6, values_ref)):
-        for t in range(3):
-            out_ref[:, t * lane_tile : (t + 1) * lane_tile] = dot(
-                normed_one, column_tile(packed_ref, base + t)
-            ).astype(bf16)
+    for index, out_ref in ((0, queries_ref), (1, keys_ref), (2, values_ref)):
+        out_ref[...] = dot(normed_one, weight(index)).astype(bf16)
     half = lane_halves(target_len)
     pad = pair_width - target_len
     pairs = bias_ref.shape[0]
+    columns = [slice(p * pair_width, (p + 1) * pair_width) for p in range(pairs)]
 
     def attend(seq, carry):
         rows = pl.ds(pl.multiple_of(seq * target_len, 32), target_len)
-        for p in range(pairs):
-            cols = slice(p * pair_width, (p + 1) * pair_width)
-            key_stack = stacked_pair(keys_ref[rows, cols], half, pad)
+        scores = [
+            dot(queries_ref[rows, cols], stacked_pair(keys_ref[rows, cols], half, pad), NT)
+            + bias_ref[p]
+            for p, cols in enumerate(columns)
+        ]
+        probs = [
+            jnp.concatenate(pair_softmax(score), axis=1).astype(bf16) for score in scores
+        ]
+        for p, cols in enumerate(columns):
             value_stack = stacked_pair(values_ref[rows, cols], half, pad)
-            scores = dot(queries_ref[rows, cols], key_stack, NT) + bias_ref[p]
-            probs = jnp.concatenate(pair_softmax(scores), axis=1)
-            context_ref[rows, cols] = dot(probs.astype(bf16), value_stack).astype(bf16)
+            context_ref[rows, cols] = dot(probs[p], value_stack).astype(bf16)
         return carry
 
     lax.fori_loop(0, targets_ref.shape[0] // target_len, attend, 0)
-    after = inputs + jnp.concatenate(project(context_ref[...], packed_ref, 9, 3), axis=1)
+    after = inputs + dot(context_ref[...], weight(3))
     after_ref[...] = after
     normed_two = (after * norm_scale(after) * gain_cross_ref[...]).astype(bf16)
     normed_two_ref[...] = normed_two
-    for t in range(3):
-        side_ref[:, t * lane_tile : (t + 1) * lane_tile] = dot(
-            normed_two, column_tile(packed_ref, 12 + t)
-        ).astype(bf16)
-
-
-def self_forward(target_len, targets, packed, bias, gain_self, gain_cross):
+    side_ref[...] = dot(normed_two, weight(4)).astype(bf16)
+
+
+def self_forward(target_len, owners, targets, near, far, bias, gain_self, gain_cross):
+    width = targets.shape[1]
+    whole = pl.BlockSpec(memory_space=pltpu.VMEM)
     low = jax.ShapeDtypeStruct(targets.shape, bf16)
     wide = jax.ShapeDtypeStruct(targets.shape, f32)
 
@@ -232,11 +251,13 @@
 
     return pl.pallas_call(
         body,
-        out_shape=[low, low, low, low, low, wide, low, low],
+        out_shape=[low, low, low, low, low, wide, low, low]
+        + [jax.ShapeDtypeStruct((width, 5 * width), bf16)],
+        in_specs=[pl.BlockSpec(memory_space=pltpu.SMEM)] + [whole] * 6,
         compiler_params=params(),
         cost_estimate=cost(20 * targets.size * targets.shape[1], 16 * targets.size),
         name="self_forward",
-    )(targets, packed, bias, gain_self, gain_cross)
+    )(owners, targets, near, far, bias, gain_self, gain_cross)
 
 
 def masked_stack(rows, half):
@@ -383,19 +404,25 @@
         grad_after = cot_ref[...].astype(f32) + grad_in
         grad_after_ref[...] = grad_after
         low = grad_after.astype(bf16)
-        put_weight_grad(packed_ref, 3 * down_base // (2 * group_rows), context_ref[...], low)
+        for c in range(3):
+            cols = slice(c * lane_tile, (c + 1) * lane_tile)
+            start = 3 * down_base // 2 + c * group_rows
+            packed_ref[:, start : start + group_rows, :] = (
+                dot(context_ref[...], low[:, cols], TN)
+                .reshape(groups, group_rows, lane_tile)
+                .astype(bf16)
+            )
         grad_context_ref[...] = through(low, side_output_ref, 0, 3).astype(bf16)
 
 
-def feed_both(after_self, context, cotangent, gain, packed_self, packed_feed):
+def feed_both(after_self, context, cotangent, gain, packed_feed):
     rows, width = context.shape
     groups, feed_rows, _ = packed_feed.shape
-    steps = feed_rows // (3 * group_rows)
+    steps = feed_rows // (3 * group_rows) - 1
     owners = groups // steps
     whole = lambda f: (0, 0)
     full = pl.BlockSpec((rows, width), whole)
     tile = (groups, group_rows, lane_tile)
-    out_rows = feed_rows + 3 * group_rows
     return pl.pallas_call(
         feed_kernel,
         out_shape=[
@@ -403,7 +430,7 @@
             jax.ShapeDtypeStruct((rows, width), f32),
             jax.ShapeDtypeStruct((rows, width), bf16),
             jax.ShapeDtypeStruct((1, width), f32),
-            jax.ShapeDtypeStruct((groups, out_rows, lane_tile), bf16),
+            jax.ShapeDtypeStruct((groups, feed_rows, lane_tile), bf16),
         ],
         grid=(steps,),
         in_specs=[
@@ -411,7 +438,7 @@
             full,
             full,
             pl.BlockSpec((1, width), whole),
-            pl.BlockSpec((groups, 3 * group_rows, lane_tile), lambda f: (0, 5, 0)),
+            pl.BlockSpec((groups, 3 * group_rows, lane_tile), lambda f: (0, steps, 0)),
             pl.BlockSpec(tile, lambda f: (0, f, 0)),
             pl.BlockSpec(tile, lambda f: (0, steps + f, 0)),
             pl.BlockSpec((owners, steps * group_rows, lane_tile), lambda f: (f, 2, 0)),
@@ -421,7 +448,7 @@
             full,
             full,
             pl.BlockSpec((1, width), whole),
-            pl.BlockSpec((groups, out_rows, lane_tile), lambda f: (0, 0, 0)),
+            pl.BlockSpec((groups, feed_rows, lane_tile), lambda f: (0, 0, 0)),
         ],
         scratch_shapes=[
             pltpu.VMEM((rows, width), f32),
@@ -432,7 +459,7 @@
         compiler_params=params(),
         cost_estimate=cost(18 * rows * width * steps * lane_tile, 30 * rows * width),
         name="feed_both",
-    )(after_self, context, cotangent, gain, packed_self, packed_feed, packed_feed, packed_feed)
+    )(after_self, context, cotangent, gain, packed_feed, packed_feed, packed_feed, packed_feed)
 
 
 def cross_backward_kernel(
@@ -543,16 +570,13 @@
 
     @pl.when(seq == pl.num_programs(0) - 1)
     def _():
-        for base, total_ref in ((0, key_total_ref), (3, value_total_ref)):
-            for t in range(3):
-                put_slots(
-                    owners,
-                    keep_ref,
-                    send_ref,
-                    stage_ref,
-                    base + t,
-                    jnp.transpose(total_ref[t * lane_tile : (t + 1) * lane_tile, :]),
+        width = key_total_ref.shape[0]
+        for base, total_ref in ((0, key_total_ref), (width, value_total_ref)):
+            for start in range(0, width, lane_tile):
+                stage_ref[:, base + start : base + start + lane_tile] = jnp.transpose(
+                    total_ref[start : start + lane_tile, :]
                 )
+        put_slots(owners, keep_ref, send_ref, stage_ref)
 
 
 def memory_weight_grads(mem_lengths, owners, memory, grad_keys, grad_values):
@@ -569,7 +593,7 @@
             in_specs=[block, turned, turned],
             out_specs=[pl.BlockSpec(half, lambda b, n, o: (0, 0, 0))] * 2,
             scratch_shapes=[pltpu.VMEM((width, width), f32)] * 2
-            + [pltpu.VMEM((width, lane_tile), f32)],
+            + [pltpu.VMEM((width, 2 * width), f32)],
         ),
         compiler_params=params(),
         cost_estimate=cost(4 * memory.size * width, 6 * memory.size),
@@ -626,55 +650,92 @@
     )(mem_lengths, grad_keys, grad_values, weight)
 
 
-def self_backward_kernel(
-    target_len,
+def self_output_kernel(
     owners,
     grad_side_ref,
     after_ref,
     grad_after_ref,
     normed_two_ref,
+    context_ref,
+    weight_ref,
+    gain_cross_ref,
+    grad_total_ref,
+    grad_context_ref,
+    grad_gain_ref,
+    keep_ref,
+    send_ref,
+    stage_ref,
+):
+    width = after_ref.shape[1]
+    grad_side = grad_side_ref[...]
+    grad_normed = dot(grad_side, weight_ref[:, 4 * width :], NT)
+    grad_in, grad_gain = norm_pullback(after_ref[...], gain_cross_ref[...], grad_normed)
+    grad_gain_ref[...] = grad_gain
+    grad_total = grad_after_ref[...] + grad_in
+    grad_total_ref[...] = grad_total
+    low = grad_total.astype(bf16)
+    stage_ref[:, :width] = dot(context_ref[...], low, TN)
+    stage_ref[:, width:] = dot(normed_two_ref[...], grad_side, TN)
+    grad_context_ref[...] = dot(low, weight_ref[:, 3 * width : 4 * width], NT).astype(bf16)
+    put_slots(owners, keep_ref, send_ref, stage_ref)
+
+
+def self_output_backward(
+    owners, grad_side, after, grad_after, normed_two, context, weight, gain_cross
+):
+    rows, width = after.shape
+    half = (owners.shape[0] // 2, 2 * width // lane_tile * group_rows, lane_tile)
+    whole = pl.BlockSpec(memory_space=pltpu.VMEM)
+    return pl.pallas_call(
+        self_output_kernel,
+        out_shape=[
+            jax.ShapeDtypeStruct((rows, width), f32),
+            jax.ShapeDtypeStruct((rows, width), bf16),
+            jax.ShapeDtypeStruct((1, width), f32),
+            jax.ShapeDtypeStruct(half, bf16),
+            jax.ShapeDtypeStruct(half, bf16),
+        ],
+        in_specs=[pl.BlockSpec(memory_space=pltpu.SMEM)] + [whole] * 7,
+        scratch_shapes=[pltpu.VMEM((width, 2 * width), f32)],
+        compiler_params=params(),
+        cost_estimate=cost(8 * after.size * width, 20 * after.size),
+        name="self_output_backward",
+    )(owners, grad_side, after, grad_after, normed_two, context, weight, gain_cross)
+
+
+def self_backward_kernel(
+    target_len,
+    bucket_count,
+    owners,
+    grad_context_ref,
+    grad_total_ref,
     normed_one_ref,
     queries_ref,
     keys_ref,
     values_ref,
-    context_ref,
     targets_ref,
-    packed_ref,
+    weight_ref,
     bias_ref,
     buckets_ref,
     gain_self_ref,
-    gain_cross_ref,
+    grad_gain_cross_ref,
+    grad_gain_feed_ref,
     target_grad_ref,
     keep_ref,
     send_ref,
-    grad_gains_ref,
-    table_ref,
     grad_queries_ref,
     grad_keys_ref,
     grad_values_ref,
-    grad_context_ref,
-    total_ref,
     score_total_ref,
     stage_ref,
+    table_ref,
+    gains_ref,
 ):
-    def put(base, rows, grads):
-        for t in range(grads.shape[1] // lane_tile):
-            part = dot(rows, grads[:, t * lane_tile : (t + 1) * lane_tile], TN)
-            put_slots(owners, keep_ref, send_ref, stage_ref, base + t, part)
-
-    grad_side = grad_side_ref[...]
-    grad_in, grad_gain_cross = norm_pullback(
-        after_ref[...], gain_cross_ref[...], through(grad_side, packed_ref, 12, 3)
-    )
-    put(12, normed_two_ref[...], grad_side)
-    grad_after = grad_after_ref[...] + grad_in
-    total_ref[...] = grad_after
-    low = grad_after.astype(bf16)
-    put(9, context_ref[...], low)
-    grad_context_ref[...] = through(low, packed_ref, 9, 3).astype(bf16)
+    width = targets_ref.shape[1]
     half = lane_halves(target_len)
     pad = pair_width - target_len
     pairs = bias_ref.shape[0]
+    columns = [slice(p * pair_width, (p + 1) * pair_width) for p in range(pairs)]
     score_total_ref[...] = jnp.zeros_like(score_total_ref)
 
     def pick(values):
@@ -684,26 +745,39 @@
 
     def attend(seq, carry):
         rows = pl.ds(pl.multiple_of(seq * target_len, 32), target_len)
-        for p in range(pairs):
-            cols = slice(p * pair_width, (p + 1) * pair_width)
-            queries = queries_ref[rows, cols]
-            grad_rows = grad_context_ref[rows, cols]
-            key_stack = stacked_pair(keys_ref[rows, cols], half, pad)
-            value_stack = stacked_pair(values_ref[rows, cols], half, pad)
-            scores = dot(queries, key_stack, NT) + bias_ref[p]
-            probs = pair_softmax(scores)
-            grad_probs = dot(grad_rows, value_stack, NT)
-            parts = []
-            for h in range(2):
-                one = grad_probs[:, h * pair_width : (h + 1) * pair_width]
-                inner = jnp.sum(one * probs[h], axis=-1, keepdims=True)
-                parts.append(probs[h] * (one - inner))
-            grad_scores = jnp.concatenate(parts, axis=1).astype(bf16)
-            weights = jnp.concatenate(probs, axis=1).astype(bf16)
-            score_total_ref[p] += grad_scores.astype(f32)
-            grad_queries_ref[rows, cols] = dot(grad_scores, key_stack).astype(bf16)
-            grad_keys_ref[rows, cols] = pick(dot(grad_scores, queries, TN))
-            grad_values_ref[rows, cols] = pick(dot(weights, grad_rows, TN))
+        for first in range(0, pairs, pair_group):
+            chosen = range(first, first + pair_group)
+            key_stacks = [stacked_pair(keys_ref[rows, columns[p]], half, pad) for p in chosen]
+            scores = [
+                dot(queries_ref[rows, columns[p]], stack, NT) + bias_ref[p]
+                for p, stack in zip(chosen, key_stacks)
+            ]
+            grad_probs = [
+                dot(
+                    grad_context_ref[rows, columns[p]],
+                    stacked_pair(values_ref[rows, columns[p]], half, pad),
+                    NT,
+                )
+                for p in chosen
+            ]
+            probs = [pair_softmax(score) for score in scores]
+            grad_scores = []
+            for prob, grad_prob in zip(probs, grad_probs):
+                parts = []
+                for h in range(2):
+                    one = grad_prob[:, h * pair_width : (h + 1) * pair_width]
+                    inner = jnp.sum(one * prob[h], axis=-1, keepdims=True)
+                    parts.append(prob[h] * (one - inner))
+                grad_scores.append(jnp.concatenate(parts, axis=1).astype(bf16))
+            for p, stack, prob, grad_score in zip(chosen, key_stacks, probs, grad_scores):
+                cols = columns[p]
+                weights = jnp.concatenate(prob, axis=1).astype(bf16)
+                score_total_ref[p] += grad_score.astype(f32)
+                grad_queries_ref[rows, cols] = dot(grad_score, stack).astype(bf16)
+                grad_keys_ref[rows, cols] = pick(dot(grad_score, queries_ref[rows, cols], TN))
+                grad_values_ref[rows, cols] = pick(
+                    dot(weights, grad_context_ref[rows, cols], TN)
+                )
         return carry
 
     lax.fori_loop(0, targets_ref.shape[0] // target_len, attend, 0)
@@ -713,36 +787,55 @@
     def count(bucket, carry):
         chosen = both == bucket
         for p in range(pairs):
-            table_ref[bucket, p : p + 1, :] = jnp.sum(
+            table_ref[pl.ds(p * bucket_count + bucket, 1), :] = jnp.sum(
                 jnp.where(chosen, score_total_ref[p], 0.0), axis=0, keepdims=True
             )
         return carry
 
-    lax.fori_loop(0, table_ref.shape[0], count, 0)
+    lax.fori_loop(0, bucket_count, count, 0)
+    lanes = lax.broadcasted_iota(jnp.int32, (8, lane_tile), 1) >> 7
+    head = (lanes == lax.broadcasted_iota(jnp.int32, (8, lane_tile), 0)).astype(f32)
+    table = lax.dot_general(
+        head, table_ref[...], NT, precision=lax.Precision.HIGHEST, preferred_element_type=f32
+    )
+
     normed_one = normed_one_ref[...]
     total = None
-    for base, grad_ref in ((0, grad_queries_ref), (3, grad_keys_ref), (6, grad_values_ref)):
+    for index, grad_ref in enumerate((grad_queries_ref, grad_keys_ref, grad_values_ref)):
+        cols = slice(index * width, (index + 1) * width)
         grads = grad_ref[...]
-        put(base, normed_one, grads)
-        part = through(grads, packed_ref, base, 3)
+        stage_ref[:, cols] = dot(normed_one, grads, TN)
+        part = dot(grads, weight_ref[:, cols], NT)
         total = part if total is None else total + part
     grad_in, grad_gain_self = norm_pullback(
         targets_ref[...].astype(f32), gain_self_ref[...], total
     )
-    target_grad_ref[...] = (total_ref[...] + grad_in).astype(bf16)
-    grad_gains_ref[0:1, :] = grad_gain_self
-    grad_gains_ref[1:2, :] = grad_gain_cross
+    target_grad_ref[...] = (grad_total_ref[...] + grad_in).astype(bf16)
+    gains_ref[...] = jnp.concatenate(
+        [grad_gain_self, grad_gain_cross_ref[...], grad_gain_feed_ref[...]]
+        + [jnp.zeros((5, width), f32)],
+        axis=0,
+    )
+    tail = jnp.concatenate([table, jnp.zeros((8, lane_tile - table.shape[1]), f32)], axis=1)
+    tail = jnp.concatenate([tail, jnp.zeros_like(tail)], axis=0)
+
+    def extra(owner):
+        shift = lax.rem(width - owner * group_rows, width)
+        own = pltpu.roll(gains_ref[...], shift, 1)[:, :lane_tile]
+        return jnp.concatenate([own, tail], axis=0)
+
+    put_slots(owners, keep_ref, send_ref, stage_ref, extra)
 
 
 def self_backward(target_len, bucket_count, owners, operands):
-    targets = operands[9]
-    bias = operands[11]
+    targets = operands[6]
+    bias = operands[8]
     rows, width = targets.shape
-    half = (owners.shape[0] // 2, 15 * group_rows, lane_tile)
+    half = (owners.shape[0] // 2, 10 * group_rows, lane_tile)
     whole = pl.BlockSpec(memory_space=pltpu.VMEM)
 
     def body(*refs):
-        self_backward_kernel(target_len, *refs)
+        self_backward_kernel(target_len, bucket_count, *refs)
 
     return pl.pallas_call(
         body,
@@ -750,18 +843,17 @@
             jax.ShapeDtypeStruct((rows, width), bf16),
             jax.ShapeDtypeStruct(half, bf16),
             jax.ShapeDtypeStruct(half, bf16),
-            jax.ShapeDtypeStruct((2, width), f32),
-            jax.ShapeDtypeStruct((bucket_count, bias.shape[0], bias.shape[2]), f32),
         ],
         in_specs=[pl.BlockSpec(memory_space=pltpu.SMEM)] + [whole] * len(operands),
-        scratch_shapes=[pltpu.VMEM((rows, width), bf16)] * 4
+        scratch_shapes=[pltpu.VMEM((rows, width), bf16)] * 3
         + [
-            pltpu.VMEM((rows, width), f32),
             pltpu.VMEM(bias.shape, f32),
-            pltpu.VMEM((width, lane_tile), f32),
+            pltpu.VMEM((width, 3 * width), f32),
+            pltpu.VMEM((bias.shape[0] * bucket_count, lane_tile), f32),
+            pltpu.VMEM((8, width), f32),
         ],
         compiler_params=params(),
-        cost_estimate=cost(40 * targets.size * width, 20 * targets.size),
+        cost_estimate=cost(32 * targets.size * width, 20 * targets.size),
         name="self_backward",
     )(owners, *operands)
 
@@ -811,7 +903,7 @@
     return split_share(share, shapes, devices)
 
 
-core_step = (2,)
+core_step = 2
 plane_steps = (1, 4, 5)
 line_steps = (8, 16, 24)
 
@@ -820,8 +912,7 @@
     return lax.ppermute(values, axes, [(i, i ^ step) for i in range(32)])
 
 
-def slot_tables():
-    here = lax.axis_index(axes)
+def slot_tables(here):
     device = jnp.arange(32, dtype=jnp.int32)
     gap = device ^ here
     slots = ((gap >> 1) & 1) * 16 + ((gap & 1) + ((gap >> 2) & 1) * 2) * 4 + (gap >> 3)
@@ -830,34 +921,41 @@
     return slots.astype(jnp.int32), owners.astype(jnp.int32)
 
 
-def permute_gather(shard):
-    line = jnp.stack([shard] + [exchange(shard, step) for step in line_steps])
-    plane = jnp.concatenate([line] + [exchange(line, step) for step in plane_steps])
-    return jnp.concatenate([plane, exchange(plane, core_step[0])])
-
-
-def pair_sum(keep, send):
-    return (keep.astype(f32) + exchange(send, core_step[0]).astype(f32)).astype(bf16)
-
-
-def permute_scatter(pair):
-    parts = [pair[4 * j : 4 * j + 4] for j in range(4)]
-    total = parts[0].astype(f32)
-    for part, step in zip(parts[1:], plane_steps):
-        total = total + exchange(part, step).astype(f32)
-    total = total.astype(bf16)
-    final = total[0].astype(f32)
-    for k, step in enumerate(line_steps):
-        final = final + exchange(total[k + 1], step).astype(f32)
-    return final
-
-
-def permute_sum(values):
-    values = values + exchange(values, core_step[0])
-    for steps in (plane_steps, line_steps):
-        first, second, third = (exchange(values, step) for step in steps)
-        values = (values + first) + (second + third)
-    return values
+def line_gather(shard):
+    return [shard] + [exchange(shard, step) for step in line_steps]
+
+
+def plane_gather(line):
+    line = jnp.stack(line)
+    return [line] + [exchange(line, step) for step in plane_steps]
+
+
+def core_gather(blocks):
+    plane = jnp.concatenate(blocks)
+    return plane, exchange(plane, core_step)
+
+
+def tree_sum(parts):
+    first, second, third, fourth = (part.astype(f32) for part in parts)
+    return (first + second) + (third + fourth)
+
+
+def pair_sums(keep, received):
+    return [
+        (keep[4 * j : 4 * j + 4].astype(f32) + received[4 * j : 4 * j + 4].astype(f32)).astype(
+            bf16
+        )
+        for j in range(4)
+    ]
+
+
+def plane_exchange(parts):
+    return [parts[0]] + [exchange(part, step) for part, step in zip(parts[1:], plane_steps)]
+
+
+def line_sum(parts):
+    moved = [exchange(parts[k + 1], step) for k, step in enumerate(line_steps)]
+    return tree_sum([parts[0]] + moved)
 
 
 def split_share(share, shapes, devices):
@@ -903,30 +1001,39 @@
     feed_shapes = [(width, feed_width), (width, feed_width), (feed_width, width)]
 
     own_gains = jnp.stack([gain_self, gain_cross, gain_feed])
+    self_shards = [self_query, self_key, self_value, self_output, cross_query]
     if direct:
-        slots, owners = slot_tables()
+        slots, owners = slot_tables(lax.axis_index(axes))
         extra = jnp.pad(own_gains.reshape(1, -1), ((0, 15), (0, lane_tile - own_gains.size)))
-        packed_memory = permute_gather(
-            jnp.concatenate([pack(cross_key), pack(cross_value), extra], axis=0)
+        memory_blocks = plane_gather(
+            line_gather(jnp.concatenate([pack(cross_key), pack(cross_value), extra], axis=0))
         )
+        self_line = line_gather(jnp.concatenate([pack(shard) for shard in self_shards], axis=0))
+        memory_blocks, self_line = lax.optimization_barrier((memory_blocks, self_line))
+        memory_near, memory_far = core_gather(memory_blocks)
+        self_blocks = plane_gather(self_line)
         hot = (slots[:, None] == jnp.arange(groups)[None, :]).astype(bf16)
+        small = [part[:, -16, : own_gains.size] for part in (memory_near, memory_far)]
         gains = (
-            dot(hot, packed_memory[:, -16, : own_gains.size])
-            .reshape(groups, 3, group_rows)
-            .transpose(1, 0, 2)
-            .reshape(3, width)
-        )
+            dot(hot, jnp.concatenate(small)).reshape(groups, 3, group_rows).transpose(1, 0, 2)
+        ).reshape(3, width)
     else:
-        slots = owners = jnp.arange(groups, dtype=jnp.int32)
-        packed_memory = gather([cross_key, cross_value], [square] * 2, groups, devices)
+        slots, owners = slot_tables(0)
+
+        def halves(shards):
+            packed = gather(shards, [square] * len(shards), groups, devices)
+            packed = jnp.take(packed, owners, axis=0)
+            return packed[: groups // 2], packed[groups // 2 :]
+
+        memory_near, memory_far = halves([cross_key, cross_value])
+        self_near, self_far = halves(self_shards)
         gains = lax.all_gather(own_gains, axes, axis=1, tiled=True).astype(f32)
-    packed_self = gather(
-        [self_query, self_key, self_value, self_output, cross_query, cross_output],
-        [square] * 6,
+    packed_feed = gather(
+        [gate_weight, up_weight, down_weight, cross_output],
+        feed_shapes + [square],
         groups,
         devices,
     )
-    packed_feed = gather([gate_weight, up_weight, down_weight], feed_shapes, groups, devices)
 
     pad = pair_width - target_len
     bucket_hot = (
@@ -952,14 +1059,27 @@
     cot_rows = cotangent.reshape(row_count, width)
 
     mem_keys, mem_values, memory_weight = project_memory(
-        mem_lengths, slots, memory, packed_memory
-    )
-    normed_one, queries, key_rows, value_rows, self_context, after_self, normed_two, side = (
-        self_forward(target_len, target_rows, packed_self, bias, gains[0:1], gains[1:2])
+        mem_lengths, owners, memory, memory_near, memory_far
+    )
+    if direct:
+        self_blocks, memory_weight = lax.optimization_barrier((self_blocks, memory_weight))
+        self_near, self_far = core_gather(self_blocks)
+    (
+        normed_one,
+        queries,
+        key_rows,
+        value_rows,
+        self_context,
+        after_self,
+        normed_two,
+        side,
+        self_weight,
+    ) = self_forward(
+        target_len, owners, target_rows, self_near, self_far, bias, gains[0:1], gains[1:2]
     )
     cross_context, weights = cross_forward(mem_lengths, side, mem_keys, mem_values, head_count)
     outputs, grad_after_cross, grad_context, grad_gain_feed, feed_grads = feed_both(
-        after_self, cross_context, cot_rows, gains[2:3], packed_self, packed_feed
+        after_self, cross_context, cot_rows, gains[2:3], packed_feed
     )
     share_gate, share_up, share_down, share_cross_output = scatter(
         feed_grads, feed_shapes + [square], groups, devices
@@ -967,77 +1087,106 @@
     grad_side, grad_mem_keys, grad_mem_values = cross_backward(
         mem_lengths, grad_context, cross_context, side, mem_keys, mem_values, weights
     )
-    target_grad, self_keep, self_send, grad_gains, table_parts = self_backward(
+    grad_total, grad_self_context, grad_gain_cross, output_keep, output_send = (
+        self_output_backward(
+            owners,
+            grad_side,
+            after_self,
+            grad_after_cross,
+            normed_two,
+            self_context,
+            self_weight,
+            gains[1:2],
+        )
+    )
+    target_grad, self_keep, self_send = self_backward(
         target_len,
         bucket_count,
         owners,
         (
-            grad_side,
-            after_self,
-            grad_after_cross,
-            normed_two,
+            grad_self_context,
+            grad_total,
             normed_one,
             queries,
             key_rows,
             value_rows,
-            self_context,
             target_rows,
-            packed_self,
+            self_weight,
             bias,
             wide_buckets,
             gains[0:1],
-            gains[1:2],
+            grad_gain_cross,
+            grad_gain_feed,
         ),
     )
-    grad_mem_keys, grad_mem_values, self_keep = lax.optimization_barrier(
-        (grad_mem_keys, grad_mem_values, self_keep)
-    )
+    if direct:
+        output_parts = pair_sums(output_keep, exchange(output_send, core_step))
+        grad_mem_keys, self_keep, output_parts = lax.optimization_barrier(
+            (grad_mem_keys, self_keep, output_parts)
+        )
     memory_keep, memory_send = memory_weight_grads(
         mem_lengths, owners, memory, grad_mem_keys, grad_mem_values
     )
-    table_part = (
-        table_parts.reshape(bucket_count, head_count, pair_width).sum(axis=-1).reshape(-1)
-    )
-    small = jnp.concatenate(
-        [grad_gains[0], grad_gains[1], grad_gain_feed[0], table_part], axis=0
-    )
     if direct:
-        self_pair = pair_sum(self_keep, self_send)
-        memory_weight, self_pair = lax.optimization_barrier((memory_weight, self_pair))
+        output_parts = plane_exchange(output_parts)
+        self_parts = pair_sums(self_keep, exchange(self_send, core_step))
+        memory_weight, memory_keep, self_parts, output_parts = lax.optimization_barrier(
+            (memory_weight, memory_keep, self_parts, output_parts)
+        )
     memory_grad = memory_gradient(mem_lengths, grad_mem_keys, grad_mem_values, memory_weight)
     if direct:
-        self_shares = permute_scatter(self_pair)
-        memory_grad, memory_keep, memory_send, small = lax.optimization_barrier(
-            (memory_grad, memory_keep, memory_send, small)
+        self_parts = plane_exchange(self_parts)
+        memory_received = exchange(memory_send, core_step)
+        memory_grad, memory_received = lax.optimization_barrier((memory_grad, memory_received))
+        memory_grad, self_parts = lax.optimization_barrier((memory_grad, self_parts))
+        memory_parts = plane_exchange(pair_sums(memory_keep, memory_received))
+        joint = line_sum(
+            jnp.concatenate(
+                [tree_sum(output_parts).astype(bf16), tree_sum(self_parts).astype(bf16)], axis=1
+            )
         )
-        memory_shares = permute_scatter(pair_sum(memory_keep, memory_send))
-        share_cross_key, share_cross_value = split_share(memory_shares, [square] * 2, devices)
-        share_query, share_key, share_value, share_output, share_cross_query = split_share(
-            self_shares, [square] * 5, devices
+        output_share = joint[: 6 * group_rows]
+        self_share = joint[6 * group_rows :]
+        memory_share = line_sum(tree_sum(memory_parts).astype(bf16))
+        share_output, share_cross_query = split_share(output_share, [square] * 2, devices)
+        share_query, share_key, share_value = split_share(self_share, [square] * 3, devices)
+        share_cross_key, share_cross_value = split_share(memory_share, [square] * 2, devices)
+        own_grads = self_share[9 * group_rows : 9 * group_rows + 3, : width // devices]
+        table = self_share[9 * group_rows + 8 : 9 * group_rows + 10]
+    else:
+
+        def reduced(keep, send, count):
+            packed = jnp.take(jnp.concatenate([keep, send]), slots, axis=0)
+            return scatter(
+                packed[:, : 3 * count * group_rows], [square] * count, groups, devices
+            )
+
+        share_output, share_cross_query = reduced(output_keep, output_send, 2)
+        share_query, share_key, share_value = reduced(self_keep, self_send, 3)
+        share_cross_key, share_cross_value = reduced(memory_keep, memory_send, 2)
+        small = jnp.take(jnp.concatenate([self_keep, self_send]), slots, axis=0)
+        small = small[:, 9 * group_rows :].astype(f32)
+        grad_gains = small[:, :3, :group_rows].transpose(1, 0, 2).reshape(-1)
+        small = jnp.concatenate([grad_gains, small[0, 8:10].reshape(-1)])
+        small = jnp.sum(lax.all_gather(small, axes, axis=0, tiled=False), axis=0)
+        own_grads = lax.dynamic_index_in_dim(
+            small[: 3 * width].reshape(3, devices, -1), lax.axis_index(axes), 1, False
         )
-        small = permute_sum(small)
-    else:
-        share_cross_key, share_cross_value = scatter(
-            jnp.concatenate([memory_keep, memory_send]), [square] * 2, groups, devices
-        )
-        share_query, share_key, share_value, share_output, share_cross_query = scatter(
-            jnp.concatenate([self_keep, self_send]), [square] * 5, groups, devices
-        )
-        small = jnp.sum(lax.all_gather(small, axes, axis=0, tiled=False), axis=0)
-    table_grad = small[3 * width :].reshape(bucket_count, head_count)
-    own = width // devices
-    place = lax.axis_index(axes) * own
-
-    def own_gain(index):
-        return lax.dynamic_slice(small, (index * width + place,), (own,))
+        table = small[3 * width :].reshape(2, lane_tile)
+    table_grad = (
+        table[:, : bucket_count * head_count // 2]
+        .reshape(2, head_count // 2, bucket_count)
+        .transpose(2, 1, 0)
+        .reshape(bucket_count, head_count)
+    )
 
     return (
         outputs.reshape(targets.shape),
         target_grad.reshape(targets.shape),
         memory_grad,
-        own_gain(0),
-        own_gain(1),
-        own_gain(2),
+        own_grads[0],
+        own_grads[1],
+        own_grads[2],
         share_query,
         share_key,
         share_value,

time: 441 us -> 399 us (0.905)
  Pallas kernels: 264 us -> 220 us
  starting transfers between devices: 34.3 us -> 46.4 us
  waiting for transfers between devices: 84.6 us -> 74.6 us
    all_gather x2 -> x1, waiting for transfers between devices: 36.8 us -> 0.01 us  [gather(): whole = lax.all_gather(packed, axes, axis=0, tiled=False)]
    pallas_call x1, Pallas kernels: 59.1 us -> 30.9 us  [self_backward(): pl.pallas_call(body, out_shape=[jax.ShapeDtypeStruct((rows, width), bf16)...]
    ppermute x28 -> x32, waiting for transfers between devices: 47.7 us -> 74.6 us  [exchange(): return lax.ppermute(values, axes, [(i, i ^ step) for i in range(32)])]
    ppermute x28 -> x32, starting transfers between devices: 34.1 us -> 46.3 us  [exchange(): return lax.ppermute(values, axes, [(i, i ^ step) for i in range(32)])]
    pallas_call x1, Pallas kernels: 25.9 us -> 20.8 us  [project_memory(): pl.pallas_call(memory_kernel, out_shape=[jax.ShapeDtypeStruct(memory.shap...]
    pallas_call x1, Pallas kernels: 26.5 us -> 21.4 us  [memory_weight_grads(): pl.pallas_call(memory_weight_kernel, out_shape=[jax.ShapeDtypeStruct(half...]
    pallas_call x1, Pallas kernels: 25.3 us -> 20.7 us  [memory_gradient(): pl.pallas_call(memory_grad_kernel, out_shape=jax.ShapeDtypeStruct((batch,...]
    pallas_call x1 -> x2, Pallas kernels: 29.4 us -> 32.6 us  [the longest x1 18.8 us: self_forward(): pl.pallas_call(body, out_shape=[low, low, low, low, low, wide, low, low]...]
  transfers between devices with their start and end apart: 31 -> 34, of which waited for: 18 -> 12; matrix products, arithmetic and copies ran while one was open for 6% -> 7% of each run, Pallas kernels for 52% -> 47%
where the time goes in v3:
time: 399 us; the launch traced here: 391 us
  Pallas kernels  220 us (55%)
  waiting for transfers between devices  74.6 us (19%)
  starting transfers between devices  46.4 us (12%)
  local copies, waits for them, and re-layouts  26.2 us (7%)
  between operations  15.1 us (4%)
  other arithmetic  7.81 us (2%)
    ppermute x32, waiting for transfers between devices, exchange(): return lax.ppermute(values, axes, [(i, i ^ step) for i in range(32)])  74.6 us
    ppermute x32, starting transfers between devices, exchange(): return lax.ppermute(values, axes, [(i, i ^ step) for i in range(32)])  46.3 us
    pallas_call x1, Pallas kernels, feed_both(): pl.pallas_call(feed_kernel, out_shape=[jax.ShapeDtypeStruct((rows, width)...  38 us
    pallas_call x1, Pallas kernels, self_backward(): pl.pallas_call(body, out_shape=[jax.ShapeDtypeStruct((rows, width), bf16)...  30.9 us
    pallas_call x1, Pallas kernels, cross_backward(): pl.pallas_call(cross_backward_kernel, out_shape=[jax.ShapeDtypeStruct(sid...  30.7 us
    pallas_call x1, Pallas kernels, cross_forward(): pl.pallas_call(cross_forward_kernel, out_shape=[jax.ShapeDtypeStruct(side...  25.1 us
    pallas_call x1, Pallas kernels, memory_weight_grads(): pl.pallas_call(memory_weight_kernel, out_shape=[jax.ShapeDtypeStruct(half...  21.4 us
    pallas_call x1, Pallas kernels, project_memory(): pl.pallas_call(memory_kernel, out_shape=[jax.ShapeDtypeStruct(memory.shap...  20.8 us
  transfers between devices with their start and end apart: 34, of which 12 were waited for; matrix products, arithmetic and copies ran while one was open for 7% of the time, Pallas kernels for 47%

profile of v3, /device:TPU:8, one launch (start us, length us, event | category | flops | bytes accessed | tf_op | source)
XLA Modules:
  0.0 390.8 jit_solution(3763951599335187180)
XLA Ops:
  12.0 2.7 collective-permute-start.1
  14.7 1.8 collective-permute-start
  17.1 2.9 collective-permute-done.1
  20.0 1.5 collective-permute-done.2
  22.0 1.6 collective-permute-start.3
  25.5 3.1 collective-permute-start.7
  28.6 2.8 collective-permute-start.8
  31.4 12.2 %collective-permute-done.7 = bf16[360,256]{1,0:T(8,128)(2,1)S(1)} collective-permute-done((bf16[360,256]{1,0:T(8,128)(2,1)S(1)}, bf16[360,256]{1,0:T(8,128)(2,1)S(1)}, u32[]{:S(2)}, u32[]{:S(2)}) %collective-permute-start.7) | collective-permute-done | bytes 184352 | tf_op jit(solution)/shard_map/ppermute | solution.py:912
  43.7 4.5 %collective-permute-done.8 = bf16[360,256]{1,0:T(8,128)(2,1)S(1)} collective-permute-done((bf16[360,256]{1,0:T(8,128)(2,1)S(1)}, bf16[360,256]{1,0:T(8,128)(2,1)S(1)}, u32[]{:S(2)}, u32[]{:S(2)}) %collective-permute-start.8) | collective-permute-done | bytes 184352 | tf_op jit(solution)/shard_map/ppermute | solution.py:912
  55.4 20.8 %memory_project.1 = (bf16[8,1024,768]{2,1,0:T(8,128)(2,1)}, bf16[8,1024,768]{2,1,0:T(8,128)(2,1)}, bf16[768,1536]{1,0:T(8,128)(2,1)}) custom-call(s32[8]{0:T(128)} %lengths.9, s32[32]{0:T(128)} %get-tuple-element.189.owners.refs_0_, bf16[8,1024,768]{2,1,0:T(8,128)(2,1)} %memory_ref.3, bf16[16,160,256]{2,1,0:T(8,128)(2,1)} %constant_dynamic-update-slice_fusion.5.near_ref, ...), custom_call_target="tpu_custom_call" | custom-call | flops 19327352832 | bytes 37748736 | tf_op jit(solution)/shard_map/memory_project/pallas_call | solution.py:152
  76.2 15.7 %collective-permute-done.10 = bf16[4,360,256]{2,1,0:T(8,128)(2,1)S(1)} collective-permute-done((bf16[4,360,256]{2,1,0:T(8,128)(2,1)S(1)}, bf16[4,360,256]{2,1,0:T(8,128)(2,1)S(1)}, u32[]{:S(2)}, u32[]{:S(2)}) %collective-permute-start.10) | collective-permute-done | bytes 737312 | tf_op jit(solution)/shard_map/ppermute | solution.py:912
  91.9 9.7 %collective-permute-done.9 = bf16[4,360,256]{2,1,0:T(8,128)(2,1)S(1)} collective-permute-done((bf16[4,360,256]{2,1,0:T(8,128)(2,1)S(1)}, bf16[4,360,256]{2,1,0:T(8,128)(2,1)S(1)}, u32[]{:S(2)}, u32[]{:S(2)}) %collective-permute-start.9) | collective-permute-done | bytes 737312 | tf_op jit(solution)/shard_map/ppermute | solution.py:912
  111.1 18.8 %self_forward.1 = (bf16[768,768]{1,0:T(8,128)(2,1)}, bf16[768,768]{1,0:T(8,128)(2,1)}, bf16[768,768]{1,0:T(8,128)(2,1)}, bf16[768,768]{1,0:T(8,128)(2,1)}, bf16[...) custom-call(s32[32]{0:T(128)} %get-tuple-element.189.owners.refs_0_,, ...), custom_call_target="tpu_custom_call" | custom-call | flops 9059696640 | bytes 9437184 | tf_op jit(solution)/shard_map/self_forward/pallas_call | solution.py:252
  130.0 25.1 %cross_forward.1 = (bf16[768,768]{1,0:T(8,128)(2,1)}, bf16[8,1152,1024]{2,1,0:T(8,128)(2,1)}) custom-call(s32[8]{0:T(128)} %lengths.9, bf16[768,768]{1,0:T(8,128)(2,1)} %get-tuple-element.100.side_ref, bf16[8,1024,768]{2,1,0:T(8,128)(2,1)} %get-tuple-element.101.keys_ref, bf16[8,1024,768]{2,1,0:T(8,128)(2,1)} %get-tuple-element.102.values_ref), custom_call_target="tpu_custom_call" | custom-call | flops 9663676416 | bytes 37748736 | tf_op jit(solution)/shard_map/cross_forward/pallas_call | solution.py:303
  155.0 38.0 %feed_both.1 = (bf16[768,768]{1,0:T(8,128)(2,1)}, f32[768,768]{1,0:T(8,128)}, bf16[768,768]{1,0:T(8,128)(2,1)}, f32[1,768]{1,0:T(1,128)}, bf16[32,648,256]{2,1,0:T(8,128)(2,1)}) custom-call(f32[768,768]{1,0:T(8,128)} %get-tuple-element.99.after_ref, bf16[768,768]{1,0:T(8,128)(2,1)} %get-tuple-element.103.context_ref, bf16[768,768]{1,0:T(8,128)(2,1)} %bitcast.225, ...), custom_call_target="tpu_custom_call" | custom-call | flops 21743271936 | bytes 17694720 | tf_op jit(solution)/shard_map/feed_both/pallas_call | solution.py:426
  193.6 30.7 %cross_backward.1 = (bf16[768,768]{1,0:T(8,128)(2,1)}, bf16[8,768,1024]{2,1,0:T(8,128)(2,1)}, bf16[8,768,1024]{2,1,0:T(8,128)(2,1)}) custom-call(s32[8]{0:T(128)} %lengths.9, bf16[768,768]{1,0:T(8,128)(2,1)} %get-tuple-element.105.grad_ref, bf16[768,768]{1,0:T(8,128)(2,1)} %get-tuple-element.103.context_ref, bf16[768,768]{1,0:T(8,128)(2,1)} %get-tuple-element.100.side_ref, ...), custom_call_target="tpu_custom_call" | custom-call | flops 19327352832 | bytes 62914560 | tf_op jit(solution)/shard_map/cross_backward/pallas_call | solution.py:515
  224.3 13.8 %self_output_backward.1 = (f32[768,768]{1,0:T(8,128)}, bf16[768,768]{1,0:T(8,128)(2,1)}, f32[1,768]{1,0:T(1,128)}, bf16[16,144,256]{2,1,0:T(8,128)(2,1)}, bf16[16,144,256]{2,1,0:T(8,128)(2,1)}) custom-call(s32[32]{0:T(128)} %get-tuple-element.189.owners.refs_0_, bf16[768,768]{1,0:T(8,128)(2,1)} %get-tuple-element.107.grad_side_ref, ...), custom_call_target="tpu_custom_call" | custom-call | flops 3623878656 | bytes 11796480 | tf_op jit(solution)/shard_map/self_output_backward/pallas_call | solution.py:689
  238.1 5.2 %collective-permute-start.14 = (bf16[16,144,256]{2,1,0:T(8,128)(2,1)}, bf16[16,144,256]{2,1,0:T(8,128)(2,1)S(1)}, u32[]{:S(2)}, u32[]{:S(2)}) collective-permute-start(bf16[16,144,256]{2,1,0:T(8,128)(2,1)} %get-tuple-element.124), channel_id=1, source_target_pairs={{0,2},{1,3},{2,0},{3,1},{4,6},{5,7},{6,4},{7,5},{8,10},{9,11},{10,... | collective-permute-start | bytes 3538952 | tf_op jit(solution)/shard_map/ppermute | solution.py:912
  243.3 30.9 %self_backward.1 = (bf16[768,768]{1,0:T(8,128)(2,1)}, bf16[16,240,256]{2,1,0:T(8,128)(2,1)}, bf16[16,240,256]{2,1,0:T(8,128)(2,1)}) custom-call(s32[32]{0:T(128)} %get-tuple-element.189.owners.refs_0_, bf16[768,768]{1,0:T(8,128)(2,1)} %get-tuple-element.112.refs_1_, f32[768,768]{1,0:T(8,128)} %get-tuple-element.113.refs_2_, ...), custom_call_target="tpu_custom_call" | custom-call | flops 14495514624 | bytes 11796480 | tf_op jit(solution)/shard_map/self_backward/pallas_call | solution.py:840
  275.7 3.7 collective-permute-start.17
  279.4 21.4 %memory_weight_grads.1 = (bf16[16,144,256]{2,1,0:T(8,128)(2,1)}, bf16[16,144,256]{2,1,0:T(8,128)(2,1)}) custom-call(s32[8]{0:T(128)} %lengths.9, s32[32]{0:T(128)} %get-tuple-element.189.owners.refs_0_, bf16[8,1024,768]{2,1,0:T(8,128)(2,1)} %memory_ref.3, bf16[8,768,1024]{2,1,0:T(8,128)(2,1)} %get-tuple-element.125.grad_keys_ref, ...), custom_call_target="tpu_custom_call" | custom-call | flops 19327352832 | bytes 37748736 | tf_op jit(solution)/shard_map/memory_weight_grads/pallas_call | solution.py:587
  300.8 4.6 %collective-permute-start.19 = (bf16[16,144,256]{2,1,0:T(8,128)(2,1)}, bf16[16,144,256]{2,1,0:T(8,128)(2,1)S(1)}, u32[]{:S(2)}, u32[]{:S(2)}) collective-permute-start(bf16[16,144,256]{2,1,0:T(8,128)(2,1)} %get-tuple-element.136), channel_id=1, source_target_pairs={{0,2},{1,3},{2,0},{3,1},{4,6},{5,7},{6,4},{7,5},{8,10},{9,11},{10,... | collective-permute-start | bytes 3538952 | tf_op jit(solution)/shard_map/ppermute | solution.py:912
  305.4 3.0 add_convert_fusion.1
  308.5 1.6 collective-permute-start.20
  310.1 2.4 collective-permute-start.21
  312.4 20.7 %memory_grad.1 = bf16[8,1024,768]{2,1,0:T(8,128)(2,1)} custom-call(s32[8]{0:T(128)} %lengths.9, bf16[8,768,1024]{2,1,0:T(8,128)(2,1)} %get-tuple-element.125.grad_keys_ref, bf16[8,768,1024]{2,1,0:T(8,128)(2,1)} %get-tuple-element.126.grad_values_ref, bf16[768,1536]{1,0:T(8,128)(2,1)} %get-tuple-element.135.weight_ref), custom_call_target="tpu_custom_call" | custom-call | flops 19327352832 | bytes 37748736 | tf_op jit(solution)/shard_map/memory_grad/pallas_call | solution.py:637
  334.5 4.7 %collective-permute-done.21 = bf16[4,240,256]{2,1,0:T(8,128)(2,1)S(1)} collective-permute-done((bf16[4,240,256]{2,1,0:T(8,128)(2,1)}, bf16[4,240,256]{2,1,0:T(8,128)(2,1)S(1)}, u32[]{:S(2)}, u32[]{:S(2)}) %collective-permute-start.21) | collective-permute-done | bytes 491552 | tf_op jit(solution)/shard_map/ppermute | solution.py:912
  339.6 5.4 %collective-permute-start.23 = (bf16[384,256]{1,0:T(8,128)(2,1)S(1)}, bf16[384,256]{1,0:T(8,128)(2,1)S(1)}, u32[]{:S(2)}, u32[]{:S(2)}) collective-permute-start(bf16[384,256]{1,0:T(8,128)(2,1)S(1)} %get-tuple-element.165), channel_id=1, source_target_pairs={{0,8},{1,9},{2,10},{3,11},{4,12},{5,13},{6,14},{7,15},{8,0},{9,1},... | collective-permute-start | bytes 589832 | tf_op jit(solution)/shard_map/ppermute | solution.py:912
  347.0 5.6 %collective-permute-done.23 = bf16[384,256]{1,0:T(8,128)(2,1)S(1)} collective-permute-done((bf16[384,256]{1,0:T(8,128)(2,1)S(1)}, bf16[384,256]{1,0:T(8,128)(2,1)S(1)}, u32[]{:S(2)}, u32[]{:S(2)}) %collective-permute-start.23) | collective-permute-done | bytes 196640 | tf_op jit(solution)/shard_map/ppermute | solution.py:912
  352.6 9.9 %collective-permute-done.24 = bf16[384,256]{1,0:T(8,128)(2,1)S(1)} collective-permute-done((bf16[384,256]{1,0:T(8,128)(2,1)S(1)}, bf16[384,256]{1,0:T(8,128)(2,1)S(1)}, u32[]{:S(2)}, u32[]{:S(2)}) %collective-permute-start.24) | collective-permute-done | bytes 196640 | tf_op jit(solution)/shard_map/ppermute | solution.py:912
  362.5 7.0 %collective-permute-done.25 = bf16[384,256]{1,0:T(8,128)(2,1)S(1)} collective-permute-done((bf16[384,256]{1,0:T(8,128)(2,1)S(1)}, bf16[384,256]{1,0:T(8,128)(2,1)S(1)}, u32[]{:S(2)}, u32[]{:S(2)}) %collective-permute-start.25) | collective-permute-done | bytes 196640 | tf_op jit(solution)/shard_map/ppermute | solution.py:912
  369.9 1.9 collective-permute-start.30
  (179 shorter events, 41.9 us)
Async XLA Ops:
  7.3 147.7 %all-gather.3.cloned.1.call-start = ((), (), s32[]{:S(2)}) async-start(), calls=%async_computation.2 | async-start | bytes 10948608 | tf_op jit(solution)/shard_map/all_gather | solution.py:896
  11.7 367.8 %reduce-scatter.2.cloned.1.call-start = ((), (), s32[]{:S(2)}) async-start(), calls=%async_computation.1 | async-start | bytes 10948608 | tf_op jit(solution)/shard_map/reduce_scatter | solution.py:902
  12.0 8.0 %collective-permute-start.1 = (bf16[160,256]{1,0:T(8,128)(2,1)S(1)}, bf16[160,256]{1,0:T(8,128)(2,1)S(1)}, u32[]{:S(2)}, u32[]{:S(2)}) collective-permute-start(bf16[160,256]{1,0:T(8,128)(2,1)S(1)} %get-tuple-element.185), channel_id=1, source_target_pairs={{0,16},{1,17},{2,18},{3,19},{4,20},{5,21},{6,22},{7,23},{8,24},{9,... | collective-permute-start | bytes 245768 | tf_op jit(solution)/shard_map/ppermute | solution.py:912
  14.7 6.9 %collective-permute-start.2 = (bf16[160,256]{1,0:T(8,128)(2,1)S(1)}, bf16[160,256]{1,0:T(8,128)(2,1)S(1)}, u32[]{:S(2)}, u32[]{:S(2)}) collective-permute-start(bf16[160,256]{1,0:T(8,128)(2,1)S(1)} %get-tuple-element.185), channel_id=1, source_target_pairs={{0,24},{1,25},{2,26},{3,27},{4,28},{5,29},{6,30},{7,31},{8,16},{9,... | collective-permute-start | bytes 245768 | tf_op jit(solution)/shard_map/ppermute | solution.py:912
  14.7 7.2 %collective-permute-start = (bf16[160,256]{1,0:T(8,128)(2,1)S(1)}, bf16[160,256]{1,0:T(8,128)(2,1)S(1)}, u32[]{:S(2)}, u32[]{:S(2)}) collective-permute-start(bf16[160,256]{1,0:T(8,128)(2,1)S(1)} %get-tuple-element.185), channel_id=1, source_target_pairs={{0,8},{1,9},{2,10},{3,11},{4,12},{5,13},{6,14},{7,15},{8,0},{9,1},... | collective-permute-start | bytes 245768 | tf_op jit(solution)/shard_map/ppermute | solution.py:912
  16.8 11.8 %collective-permute-start.6 = (bf16[360,256]{1,0:T(8,128)(2,1)S(1)}, bf16[360,256]{1,0:T(8,128)(2,1)S(1)}, u32[]{:S(2)}, u32[]{:S(2)}) collective-permute-start(bf16[360,256]{1,0:T(8,128)(2,1)S(1)} %constant_dynamic-update-slice_fusion), channel_id=1, source_target_pairs={{0,8},{1,9},{2,10},{3,11},{4,12},{5,13},{6,14},{7,15},{8,0},{9,1},... | collective-permute-start | bytes 552968 | tf_op jit(solution)/shard_map/ppermute | solution.py:912
  22.0 26.2 %collective-permute-start.3 = (bf16[4,160,256]{2,1,0:T(8,128)(2,1)S(1)}, bf16[4,160,256]{2,1,0:T(8,128)(2,1)S(1)}, u32[]{:S(2)}, u32[]{:S(2)}) collective-permute-start(bf16[4,160,256]{2,1,0:T(8,128)(2,1)S(1)} %pad_maximum_fusion.2), channel_id=1, source_target_pairs={{0,1},{1,0},{2,3},{3,2},{4,5},{5,4},{6,7},{7,6},{8,9},{9,8},{10,11... | collective-permute-start | bytes 983048 | tf_op jit(solution)/shard_map/ppermute | solution.py:912
  23.5 24.7 %collective-permute-start.4 = (bf16[4,160,256]{2,1,0:T(8,128)(2,1)S(1)}, bf16[4,160,256]{2,1,0:T(8,128)(2,1)S(1)}, u32[]{:S(2)}, u32[]{:S(2)}) collective-permute-start(bf16[4,160,256]{2,1,0:T(8,128)(2,1)S(1)} %pad_maximum_fusion.2), channel_id=1, source_target_pairs={{0,4},{1,5},{2,6},{3,7},{4,0},{5,1},{6,2},{7,3},{8,12},{9,13},{10,... | collective-permute-start | bytes 983048 | tf_op jit(solution)/shard_map/ppermute | solution.py:912
  25.1 23.1 %collective-permute-start.5 = (bf16[4,160,256]{2,1,0:T(8,128)(2,1)S(1)}, bf16[4,160,256]{2,1,0:T(8,128)(2,1)S(1)}, u32[]{:S(2)}, u32[]{:S(2)}) collective-permute-start(bf16[4,160,256]{2,1,0:T(8,128)(2,1)S(1)} %pad_maximum_fusion.2), channel_id=1, source_target_pairs={{0,5},{1,4},{2,7},{3,6},{4,1},{5,0},{6,3},{7,2},{8,13},{9,12},{10,... | collective-permute-start | bytes 983048 | tf_op jit(solution)/shard_map/ppermute | solution.py:912
  25.5 18.1 %collective-permute-start.7 = (bf16[360,256]{1,0:T(8,128)(2,1)S(1)}, bf16[360,256]{1,0:T(8,128)(2,1)S(1)}, u32[]{:S(2)}, u32[]{:S(2)}) collective-permute-start(bf16[360,256]{1,0:T(8,128)(2,1)S(1)} %constant_dynamic-update-slice_fusion), channel_id=1, source_target_pairs={{0,16},{1,17},{2,18},{3,19},{4,20},{5,21},{6,22},{7,23},{8,24},{9,... | collective-permute-start | bytes 552968 | tf_op jit(solution)/shard_map/ppermute | solution.py:912
  28.6 19.6 %collective-permute-start.8 = (bf16[360,256]{1,0:T(8,128)(2,1)S(1)}, bf16[360,256]{1,0:T(8,128)(2,1)S(1)}, u32[]{:S(2)}, u32[]{:S(2)}) collective-permute-start(bf16[360,256]{1,0:T(8,128)(2,1)S(1)} %constant_dynamic-update-slice_fusion), channel_id=1, source_target_pairs={{0,24},{1,25},{2,26},{3,27},{4,28},{5,29},{6,30},{7,31},{8,16},{9,... | collective-permute-start | bytes 552968 | tf_op jit(solution)/shard_map/ppermute | solution.py:912
  51.8 40.1 %collective-permute-start.10 = (bf16[4,360,256]{2,1,0:T(8,128)(2,1)S(1)}, bf16[4,360,256]{2,1,0:T(8,128)(2,1)S(1)}, u32[]{:S(2)}, u32[]{:S(2)}) collective-permute-start(bf16[4,360,256]{2,1,0:T(8,128)(2,1)S(1)} %pad_maximum_fusion), channel_id=1, source_target_pairs={{0,4},{1,5},{2,6},{3,7},{4,0},{5,1},{6,2},{7,3},{8,12},{9,13},{10,... | collective-permute-start | bytes 2211848 | tf_op jit(solution)/shard_map/ppermute | solution.py:912
  53.4 38.5 %collective-permute-start.11 = (bf16[4,360,256]{2,1,0:T(8,128)(2,1)S(1)}, bf16[4,360,256]{2,1,0:T(8,128)(2,1)S(1)}, u32[]{:S(2)}, u32[]{:S(2)}) collective-permute-start(bf16[4,360,256]{2,1,0:T(8,128)(2,1)S(1)} %pad_maximum_fusion), channel_id=1, source_target_pairs={{0,5},{1,4},{2,7},{3,6},{4,1},{5,0},{6,3},{7,2},{8,13},{9,12},{10,... | collective-permute-start | bytes 2211848 | tf_op jit(solution)/shard_map/ppermute | solution.py:912
  54.8 46.7 %collective-permute-start.9 = (bf16[4,360,256]{2,1,0:T(8,128)(2,1)S(1)}, bf16[4,360,256]{2,1,0:T(8,128)(2,1)S(1)}, u32[]{:S(2)}, u32[]{:S(2)}) collective-permute-start(bf16[4,360,256]{2,1,0:T(8,128)(2,1)S(1)} %pad_maximum_fusion), channel_id=1, source_target_pairs={{0,1},{1,0},{2,3},{3,2},{4,5},{5,4},{6,7},{7,6},{8,9},{9,8},{10,11... | collective-permute-start | bytes 2211848 | tf_op jit(solution)/shard_map/ppermute | solution.py:912
  238.1 36.1 %collective-permute-start.14 = (bf16[16,144,256]{2,1,0:T(8,128)(2,1)}, bf16[16,144,256]{2,1,0:T(8,128)(2,1)S(1)}, u32[]{:S(2)}, u32[]{:S(2)}) collective-permute-start(bf16[16,144,256]{2,1,0:T(8,128)(2,1)} %get-tuple-element.124), channel_id=1, source_target_pairs={{0,2},{1,3},{2,0},{3,1},{4,6},{5,7},{6,4},{7,5},{8,10},{9,11},{10,... | collective-permute-start | bytes 3538952 | tf_op jit(solution)/shard_map/ppermute | solution.py:912
  274.2 31.3 %collective-permute-start.15 = (bf16[16,240,256]{2,1,0:T(8,128)(2,1)}, bf16[16,240,256]{2,1,0:T(8,128)(2,1)}, u32[]{:S(2)}, u32[]{:S(2)}) collective-permute-start(bf16[16,240,256]{2,1,0:T(8,128)(2,1)} %get-tuple-element.130), channel_id=1, source_target_pairs={{0,2},{1,3},{2,0},{3,1},{4,6},{5,7},{6,4},{7,5},{8,10},{9,11},{10,... | collective-permute-start | bytes 5898248 | tf_op jit(solution)/shard_map/ppermute | solution.py:912
  275.3 33.1 %collective-permute-start.16 = (bf16[4,144,256]{2,1,0:T(8,128)(2,1)}, bf16[4,144,256]{2,1,0:T(8,128)(2,1)}, u32[]{:S(2)}, u32[]{:S(2)}) collective-permute-start(bf16[4,144,256]{2,1,0:T(8,128)(2,1)} %get-tuple-element.132), channel_id=1, source_target_pairs={{0,1},{1,0},{2,3},{3,2},{4,5},{5,4},{6,7},{7,6},{8,9},{9,8},{10,11... | collective-permute-start | bytes 884744 | tf_op jit(solution)/shard_map/ppermute | solution.py:912
  275.7 32.7 %collective-permute-start.17 = (bf16[4,144,256]{2,1,0:T(8,128)(2,1)}, bf16[4,144,256]{2,1,0:T(8,128)(2,1)}, u32[]{:S(2)}, u32[]{:S(2)}) collective-permute-start(bf16[4,144,256]{2,1,0:T(8,128)(2,1)} %get-tuple-element.133), channel_id=1, source_target_pairs={{0,4},{1,5},{2,6},{3,7},{4,0},{5,1},{6,2},{7,3},{8,12},{9,13},{10,... | collective-permute-start | bytes 884744 | tf_op jit(solution)/shard_map/ppermute | solution.py:912
  279.4 29.0 %collective-permute-start.18 = (bf16[4,144,256]{2,1,0:T(8,128)(2,1)}, bf16[4,144,256]{2,1,0:T(8,128)(2,1)}, u32[]{:S(2)}, u32[]{:S(2)}) collective-permute-start(bf16[4,144,256]{2,1,0:T(8,128)(2,1)} %get-tuple-element.134), channel_id=1, source_target_pairs={{0,5},{1,4},{2,7},{3,6},{4,1},{5,0},{6,3},{7,2},{8,13},{9,12},{10,... | collective-permute-start | bytes 884744 | tf_op jit(solution)/shard_map/ppermute | solution.py:912
  300.8 33.7 %collective-permute-start.19 = (bf16[16,144,256]{2,1,0:T(8,128)(2,1)}, bf16[16,144,256]{2,1,0:T(8,128)(2,1)S(1)}, u32[]{:S(2)}, u32[]{:S(2)}) collective-permute-start(bf16[16,144,256]{2,1,0:T(8,128)(2,1)} %get-tuple-element.136), channel_id=1, source_target_pairs={{0,2},{1,3},{2,0},{3,1},{4,6},{5,7},{6,4},{7,5},{8,10},{9,11},{10,... | collective-permute-start | bytes 3538952 | tf_op jit(solution)/shard_map/ppermute | solution.py:912
  308.5 26.0 %collective-permute-start.20 = (bf16[4,240,256]{2,1,0:T(8,128)(2,1)}, bf16[4,240,256]{2,1,0:T(8,128)(2,1)S(1)}, u32[]{:S(2)}, u32[]{:S(2)}) collective-permute-start(bf16[4,240,256]{2,1,0:T(8,128)(2,1)} %get-tuple-element.139), channel_id=1, source_target_pairs={{0,1},{1,0},{2,3},{3,2},{4,5},{5,4},{6,7},{7,6},{8,9},{9,8},{10,11... | collective-permute-start | bytes 1474568 | tf_op jit(solution)/shard_map/ppermute | solution.py:912
  310.1 29.2 %collective-permute-start.21 = (bf16[4,240,256]{2,1,0:T(8,128)(2,1)}, bf16[4,240,256]{2,1,0:T(8,128)(2,1)S(1)}, u32[]{:S(2)}, u32[]{:S(2)}) collective-permute-start(bf16[4,240,256]{2,1,0:T(8,128)(2,1)} %get-tuple-element.140), channel_id=1, source_target_pairs={{0,4},{1,5},{2,6},{3,7},{4,0},{5,1},{6,2},{7,3},{8,12},{9,13},{10,... | collective-permute-start | bytes 1474568 | tf_op jit(solution)/shard_map/ppermute | solution.py:912
  312.4 26.8 %collective-permute-start.22 = (bf16[4,240,256]{2,1,0:T(8,128)(2,1)}, bf16[4,240,256]{2,1,0:T(8,128)(2,1)S(1)}, u32[]{:S(2)}, u32[]{:S(2)}) collective-permute-start(bf16[4,240,256]{2,1,0:T(8,128)(2,1)} %get-tuple-element.141), channel_id=1, source_target_pairs={{0,5},{1,4},{2,7},{3,6},{4,1},{5,0},{6,3},{7,2},{8,13},{9,12},{10,... | collective-permute-start | bytes 1474568 | tf_op jit(solution)/shard_map/ppermute | solution.py:912
  339.6 13.0 %collective-permute-start.23 = (bf16[384,256]{1,0:T(8,128)(2,1)S(1)}, bf16[384,256]{1,0:T(8,128)(2,1)S(1)}, u32[]{:S(2)}, u32[]{:S(2)}) collective-permute-start(bf16[384,256]{1,0:T(8,128)(2,1)S(1)} %get-tuple-element.165), channel_id=1, source_target_pairs={{0,8},{1,9},{2,10},{3,11},{4,12},{5,13},{6,14},{7,15},{8,0},{9,1},... | collective-permute-start | bytes 589832 | tf_op jit(solution)/shard_map/ppermute | solution.py:912
  345.0 17.5 %collective-permute-start.24 = (bf16[384,256]{1,0:T(8,128)(2,1)S(1)}, bf16[384,256]{1,0:T(8,128)(2,1)S(1)}, u32[]{:S(2)}, u32[]{:S(2)}) collective-permute-start(bf16[384,256]{1,0:T(8,128)(2,1)S(1)} %get-tuple-element.167), channel_id=1, source_target_pairs={{0,16},{1,17},{2,18},{3,19},{4,20},{5,21},{6,22},{7,23},{8,24},{9,... | collective-permute-start | bytes 589832 | tf_op jit(solution)/shard_map/ppermute | solution.py:912
  345.0 24.5 %collective-permute-start.25 = (bf16[384,256]{1,0:T(8,128)(2,1)S(1)}, bf16[384,256]{1,0:T(8,128)(2,1)S(1)}, u32[]{:S(2)}, u32[]{:S(2)}) collective-permute-start(bf16[384,256]{1,0:T(8,128)(2,1)S(1)} %get-tuple-element.166), channel_id=1, source_target_pairs={{0,24},{1,25},{2,26},{3,27},{4,28},{5,29},{6,30},{7,31},{8,16},{9,... | collective-permute-start | bytes 589832 | tf_op jit(solution)/shard_map/ppermute | solution.py:912
  346.8 22.8 %collective-permute-start.26 = (bf16[4,144,256]{2,1,0:T(8,128)(2,1)S(1)}, bf16[4,144,256]{2,1,0:T(8,128)(2,1)S(1)}, u32[]{:S(2)}, u32[]{:S(2)}) collective-permute-start(bf16[4,144,256]{2,1,0:T(8,128)(2,1)S(1)} %get-tuple-element.158), channel_id=1, source_target_pairs={{0,1},{1,0},{2,3},{3,2},{4,5},{5,4},{6,7},{7,6},{8,9},{9,8},{10,11... | collective-permute-start | bytes 884744 | tf_op jit(solution)/shard_map/ppermute | solution.py:912
  346.9 22.7 %collective-permute-start.27 = (bf16[4,144,256]{2,1,0:T(8,128)(2,1)S(1)}, bf16[4,144,256]{2,1,0:T(8,128)(2,1)S(1)}, u32[]{:S(2)}, u32[]{:S(2)}) collective-permute-start(bf16[4,144,256]{2,1,0:T(8,128)(2,1)S(1)} %get-tuple-element.160), channel_id=1, source_target_pairs={{0,4},{1,5},{2,6},{3,7},{4,0},{5,1},{6,2},{7,3},{8,12},{9,13},{10,... | collective-permute-start | bytes 884744 | tf_op jit(solution)/shard_map/ppermute | solution.py:912
  352.6 17.0 %collective-permute-start.28 = (bf16[4,144,256]{2,1,0:T(8,128)(2,1)S(1)}, bf16[4,144,256]{2,1,0:T(8,128)(2,1)S(1)}, u32[]{:S(2)}, u32[]{:S(2)}) collective-permute-start(bf16[4,144,256]{2,1,0:T(8,128)(2,1)S(1)} %get-tuple-element.159), channel_id=1, source_target_pairs={{0,5},{1,4},{2,7},{3,6},{4,1},{5,0},{6,3},{7,2},{8,13},{9,12},{10,... | collective-permute-start | bytes 884744 | tf_op jit(solution)/shard_map/ppermute | solution.py:912
  369.9 8.2 %collective-permute-start.29 = (bf16[144,256]{1,0:T(8,128)(2,1)S(1)}, bf16[144,256]{1,0:T(8,128)(2,1)S(1)}, u32[]{:S(2)}, u32[]{:S(2)}) collective-permute-start(bf16[144,256]{1,0:T(8,128)(2,1)S(1)} %get-tuple-element.179), channel_id=1, source_target_pairs={{0,8},{1,9},{2,10},{3,11},{4,12},{5,13},{6,14},{7,15},{8,0},{9,1},... | collective-permute-start | bytes 221192 | tf_op jit(solution)/shard_map/ppermute | solution.py:912
  369.9 8.2 %collective-permute-start.30 = (bf16[144,256]{1,0:T(8,128)(2,1)S(1)}, bf16[144,256]{1,0:T(8,128)(2,1)S(1)}, u32[]{:S(2)}, u32[]{:S(2)}) collective-permute-start(bf16[144,256]{1,0:T(8,128)(2,1)S(1)} %get-tuple-element.181), channel_id=1, source_target_pairs={{0,16},{1,17},{2,18},{3,19},{4,20},{5,21},{6,22},{7,23},{8,24},{9,... | collective-permute-start | bytes 221192 | tf_op jit(solution)/shard_map/ppermute | solution.py:912
  371.9 6.2 %collective-permute-start.31 = (bf16[144,256]{1,0:T(8,128)(2,1)S(1)}, bf16[144,256]{1,0:T(8,128)(2,1)S(1)}, u32[]{:S(2)}, u32[]{:S(2)}) collective-permute-start(bf16[144,256]{1,0:T(8,128)(2,1)S(1)} %get-tuple-element.180), channel_id=1, source_target_pairs={{0,24},{1,25},{2,26},{3,27},{4,28},{5,29},{6,30},{7,31},{8,16},{9,... | collective-permute-start | bytes 221192 | tf_op jit(solution)/shard_map/ppermute | solution.py:912
  (19 other events, 249.9 us)
Sparse Core Ops, SparseCore 0:
  11.8 114.2 all-gather.2
  193.1 175.9 reduce-scatter.1

commit v4 on v3

--- a/solution.py
+++ b/solution.py
@@ -61,27 +61,26 @@
     return total
 
 
-def assemble(owners, near_ref, far_ref, weight_ref):
-    half = near_ref.shape[0]
-    for offset, packed_ref in ((0, near_ref), (half, far_ref)):
-
-        def place(pair, carry):
-            slot = (pair >> 2) * 8 + (pair & 3)
-            owner = owners[offset + slot]
-            odd = owner & 1
+def assemble(owners, block_refs, weight_ref):
+    slots = block_refs[0].shape[0]
+    for first in range(0, len(block_refs), 2):
+        even_ref, odd_ref = block_refs[first : first + 2]
+
+        def place(slot, carry):
+            owner = owners[first * slots + slot]
+            swap = (owner & 1) == 1
             rows = pl.ds(pl.multiple_of((owner >> 1) * (2 * group_rows), 16), 2 * group_rows)
             for t in range(weight_ref.shape[1] // lane_tile):
                 part = slice(t * group_rows, (t + 1) * group_rows)
-                weight_ref[rows, t * lane_tile : (t + 1) * lane_tile] = jnp.concatenate(
-                    [
-                        packed_ref[slot + 4 * odd, part, :],
-                        packed_ref[slot + 4 - 4 * odd, part, :],
-                    ],
-                    axis=0,
+                cols = slice(t * lane_tile, (t + 1) * lane_tile)
+                one = even_ref[slot, part, :]
+                two = odd_ref[slot, part, :]
+                weight_ref[rows, cols] = jnp.concatenate(
+                    [jnp.where(swap, two, one), jnp.where(swap, one, two)], axis=0
                 )
             return carry
 
-        lax.fori_loop(0, half // 2, place, 0)
+        lax.fori_loop(0, slots, place, 0)
 
 
 def put_slots(owners, keep_ref, send_ref, stage_ref, extra=None):
@@ -119,15 +118,15 @@
     return grad_values, grad_gain
 
 
-def memory_kernel(
-    lengths, owners, memory_ref, near_ref, far_ref, keys_ref, values_ref, weight_ref
-):
+def memory_kernel(lengths, owners, memory_ref, *refs):
+    block_refs = refs[:-3]
+    keys_ref, values_ref, weight_ref = refs[-3:]
     seq = pl.program_id(0)
     memory_len = memory_ref.shape[1]
 
     @pl.when(seq == 0)
     def _():
-        assemble(owners, near_ref, far_ref, weight_ref)
+        assemble(owners, block_refs, weight_ref)
 
     def fill(count):
         rows = memory_ref[0, :count, :]
@@ -146,7 +145,7 @@
         fill(memory_len // 2)
 
 
-def project_memory(mem_lengths, owners, memory, near, far):
+def project_memory(mem_lengths, owners, memory, blocks):
     batch, memory_len, width = memory.shape
     block = pl.BlockSpec((1, memory_len, width), lambda b, n, s: (b, 0, 0))
     return pl.pallas_call(
@@ -156,13 +155,13 @@
         grid_spec=pltpu.PrefetchScalarGridSpec(
             num_scalar_prefetch=2,
             grid=(batch,),
-            in_specs=[block] + [pl.BlockSpec(near.shape, lambda b, n, s: (0, 0, 0))] * 2,
+            in_specs=[block] + [pl.BlockSpec(blocks[0].shape, lambda b, n, s: (0, 0, 0))] * len(blocks),
             out_specs=[block, block, pl.BlockSpec((width, 2 * width), lambda b, n, s: (0, 0))],
         ),
         compiler_params=params(),
         cost_estimate=cost(4 * memory.size * width, 6 * memory.size),
         name="memory_project",
-    )(mem_lengths, owners, memory, near, far)
+    )(mem_lengths, owners, memory, *blocks)
 
 
 def stacked_pair(rows, half, pad):
@@ -182,36 +181,29 @@
     return parts
 
 
-def self_forward_kernel(
+def self_attend_kernel(
     target_len,
+    block_refs,
     owners,
     targets_ref,
-    near_ref,
-    far_ref,
     bias_ref,
     gain_self_ref,
-    gain_cross_ref,
     normed_one_ref,
     queries_ref,
     keys_ref,
     values_ref,
     context_ref,
-    after_ref,
-    normed_two_ref,
-    side_ref,
     weight_ref,
 ):
     width = targets_ref.shape[1]
-
-    def weight(index):
-        return weight_ref[:, index * width : (index + 1) * width]
-
-    assemble(owners, near_ref, far_ref, weight_ref)
+    assemble(owners, block_refs, weight_ref)
     inputs = targets_ref[...].astype(f32)
     normed_one = (inputs * norm_scale(inputs) * gain_self_ref[...]).astype(bf16)
     normed_one_ref[...] = normed_one
     for index, out_ref in ((0, queries_ref), (1, keys_ref), (2, values_ref)):
-        out_ref[...] = dot(normed_one, weight(index)).astype(bf16)
+        out_ref[...] = dot(
+            normed_one, weight_ref[:, index * width : (index + 1) * width]
+        ).astype(bf16)
     half = lane_halves(target_len)
     pad = pair_width - target_len
     pairs = bias_ref.shape[0]
@@ -233,31 +225,69 @@
         return carry
 
     lax.fori_loop(0, targets_ref.shape[0] // target_len, attend, 0)
-    after = inputs + dot(context_ref[...], weight(3))
+
+
+def self_attend(target_len, owners, targets, bias, gain_self, blocks):
+    width = targets.shape[1]
+    whole = pl.BlockSpec(memory_space=pltpu.VMEM)
+    low = jax.ShapeDtypeStruct(targets.shape, bf16)
+
+    def body(*refs):
+        stop = 4 + len(blocks)
+        self_attend_kernel(target_len, refs[4:stop], *refs[:4], *refs[stop:])
+
+    return pl.pallas_call(
+        body,
+        out_shape=[low] * 5 + [jax.ShapeDtypeStruct((width, 3 * width), bf16)],
+        in_specs=[pl.BlockSpec(memory_space=pltpu.SMEM)] + [whole] * (3 + len(blocks)),
+        compiler_params=params(),
+        cost_estimate=cost(16 * targets.size * width, 12 * targets.size),
+        name="self_attend",
+    )(owners, targets, bias, gain_self, *blocks)
+
+
+def self_project_kernel(
+    block_refs,
+    owners,
+    targets_ref,
+    context_ref,
+    gain_cross_ref,
+    after_ref,
+    normed_two_ref,
+    side_ref,
+    weight_ref,
+):
+    width = targets_ref.shape[1]
+    assemble(owners, block_refs, weight_ref)
+    after = targets_ref[...].astype(f32) + dot(context_ref[...], weight_ref[:, :width])
     after_ref[...] = after
     normed_two = (after * norm_scale(after) * gain_cross_ref[...]).astype(bf16)
     normed_two_ref[...] = normed_two
-    side_ref[...] = dot(normed_two, weight(4)).astype(bf16)
-
-
-def self_forward(target_len, owners, targets, near, far, bias, gain_self, gain_cross):
+    side_ref[...] = dot(normed_two, weight_ref[:, width:]).astype(bf16)
+
+
+def self_project(owners, targets, context, gain_cross, blocks):
     width = targets.shape[1]
     whole = pl.BlockSpec(memory_space=pltpu.VMEM)
     low = jax.ShapeDtypeStruct(targets.shape, bf16)
-    wide = jax.ShapeDtypeStruct(targets.shape, f32)
 
     def body(*refs):
-        self_forward_kernel(target_len, *refs)
+        stop = 4 + len(blocks)
+        self_project_kernel(refs[4:stop], *refs[:4], *refs[stop:])
 
     return pl.pallas_call(
         body,
-        out_shape=[low, low, low, low, low, wide, low, low]
-        + [jax.ShapeDtypeStruct((width, 5 * width), bf16)],
-        in_specs=[pl.BlockSpec(memory_space=pltpu.SMEM)] + [whole] * 6,
+        out_shape=[
+            jax.ShapeDtypeStruct(targets.shape, f32),
+            low,
+            low,
+            jax.ShapeDtypeStruct((width, 2 * width), bf16),
+        ],
+        in_specs=[pl.BlockSpec(memory_space=pltpu.SMEM)] + [whole] * (3 + len(blocks)),
         compiler_params=params(),
-        cost_estimate=cost(20 * targets.size * targets.shape[1], 16 * targets.size),
-        name="self_forward",
-    )(owners, targets, near, far, bias, gain_self, gain_cross)
+        cost_estimate=cost(4 * targets.size * width, 12 * targets.size),
+        name="self_project",
+    )(owners, targets, context, gain_cross, *blocks)
 
 
 def masked_stack(rows, half):
@@ -668,7 +698,7 @@
 ):
     width = after_ref.shape[1]
     grad_side = grad_side_ref[...]
-    grad_normed = dot(grad_side, weight_ref[:, 4 * width :], NT)
+    grad_normed = dot(grad_side, weight_ref[:, width:], NT)
     grad_in, grad_gain = norm_pullback(after_ref[...], gain_cross_ref[...], grad_normed)
     grad_gain_ref[...] = grad_gain
     grad_total = grad_after_ref[...] + grad_in
@@ -676,7 +706,7 @@
     low = grad_total.astype(bf16)
     stage_ref[:, :width] = dot(context_ref[...], low, TN)
     stage_ref[:, width:] = dot(normed_two_ref[...], grad_side, TN)
-    grad_context_ref[...] = dot(low, weight_ref[:, 3 * width : 4 * width], NT).astype(bf16)
+    grad_context_ref[...] = dot(low, weight_ref[:, :width], NT).astype(bf16)
     put_slots(owners, keep_ref, send_ref, stage_ref)
 
 
@@ -931,8 +961,7 @@
 
 
 def core_gather(blocks):
-    plane = jnp.concatenate(blocks)
-    return plane, exchange(plane, core_step)
+    return list(blocks) + [exchange(block, core_step) for block in blocks]
 
 
 def tree_sum(parts):
@@ -1001,19 +1030,25 @@
     feed_shapes = [(width, feed_width), (width, feed_width), (feed_width, width)]
 
     own_gains = jnp.stack([gain_self, gain_cross, gain_feed])
-    self_shards = [self_query, self_key, self_value, self_output, cross_query]
+    output_shards = [self_output, cross_query]
+    self_shards = [self_query, self_key, self_value]
     if direct:
         slots, owners = slot_tables(lax.axis_index(axes))
         extra = jnp.pad(own_gains.reshape(1, -1), ((0, 15), (0, lane_tile - own_gains.size)))
-        memory_blocks = plane_gather(
-            line_gather(jnp.concatenate([pack(cross_key), pack(cross_value), extra], axis=0))
+        self_line = line_gather(
+            jnp.concatenate([pack(shard) for shard in output_shards + self_shards], axis=0)
         )
-        self_line = line_gather(jnp.concatenate([pack(shard) for shard in self_shards], axis=0))
+        memory_line = line_gather(
+            jnp.concatenate([pack(cross_key), pack(cross_value), extra], axis=0)
+        )
+        gate_weight, memory_line = lax.optimization_barrier((gate_weight, memory_line))
+        memory_blocks = plane_gather(memory_line)
         memory_blocks, self_line = lax.optimization_barrier((memory_blocks, self_line))
-        memory_near, memory_far = core_gather(memory_blocks)
-        self_blocks = plane_gather(self_line)
+        memory_blocks = core_gather(memory_blocks)
+        output_line = [part[: 6 * group_rows] for part in self_line]
+        self_blocks = plane_gather([part[6 * group_rows :] for part in self_line])
         hot = (slots[:, None] == jnp.arange(groups)[None, :]).astype(bf16)
-        small = [part[:, -16, : own_gains.size] for part in (memory_near, memory_far)]
+        small = [part[:, -16, : own_gains.size] for part in memory_blocks]
         gains = (
             dot(hot, jnp.concatenate(small)).reshape(groups, 3, group_rows).transpose(1, 0, 2)
         ).reshape(3, width)
@@ -1023,10 +1058,11 @@
         def halves(shards):
             packed = gather(shards, [square] * len(shards), groups, devices)
             packed = jnp.take(packed, owners, axis=0)
-            return packed[: groups // 2], packed[groups // 2 :]
-
-        memory_near, memory_far = halves([cross_key, cross_value])
-        self_near, self_far = halves(self_shards)
+            return [packed[4 * b : 4 * b + 4] for b in range(8)]
+
+        memory_blocks = halves([cross_key, cross_value])
+        self_blocks = halves(self_shards)
+        output_blocks = halves(output_shards)
         gains = lax.all_gather(own_gains, axes, axis=1, tiled=True).astype(f32)
     packed_feed = gather(
         [gate_weight, up_weight, down_weight, cross_output],
@@ -1059,23 +1095,22 @@
     cot_rows = cotangent.reshape(row_count, width)
 
     mem_keys, mem_values, memory_weight = project_memory(
-        mem_lengths, owners, memory, memory_near, memory_far
+        mem_lengths, owners, memory, memory_blocks
     )
     if direct:
-        self_blocks, memory_weight = lax.optimization_barrier((self_blocks, memory_weight))
-        self_near, self_far = core_gather(self_blocks)
-    (
-        normed_one,
-        queries,
-        key_rows,
-        value_rows,
-        self_context,
-        after_self,
-        normed_two,
-        side,
-        self_weight,
-    ) = self_forward(
-        target_len, owners, target_rows, self_near, self_far, bias, gains[0:1], gains[1:2]
+        received, output_line, memory_weight = lax.optimization_barrier(
+            (self_blocks[1:], output_line, memory_weight)
+        )
+        self_blocks = core_gather(self_blocks[:1] + received)
+        output_blocks = plane_gather(output_line)
+    normed_one, queries, key_rows, value_rows, self_context, self_weight = self_attend(
+        target_len, owners, target_rows, bias, gains[0:1], self_blocks
+    )
+    if direct:
+        received, self_context = lax.optimization_barrier((output_blocks[1:], self_context))
+        output_blocks = core_gather(output_blocks[:1] + received)
+    after_self, normed_two, side, output_weight = self_project(
+        owners, target_rows, self_context, gains[1:2], output_blocks
     )
     cross_context, weights = cross_forward(mem_lengths, side, mem_keys, mem_values, head_count)
     outputs, grad_after_cross, grad_context, grad_gain_feed, feed_grads = feed_both(
@@ -1095,7 +1130,7 @@
             grad_after_cross,
             normed_two,
             self_context,
-            self_weight,
+            output_weight,
             gains[1:2],
         )
     )

time: 399 us -> 394 us (0.987)
  waiting for transfers between devices: 74.6 us -> 54.2 us
  Pallas kernels: 220 us -> 237 us
    ppermute x32 -> x45, waiting for transfers between devices: 74.6 us -> 54.2 us  [exchange(): return lax.ppermute(values, axes, [(i, i ^ step) for i in range(32)])]
    pallas_call x1 -> x2, Pallas kernels: 18.8 us -> 21.5 us  [the longest x1 15 us: self_attend(): pl.pallas_call(body, out_shape=[low] * 5 + [jax.ShapeDtypeStruct((width,...]
    unnamed x54 -> x90, local copies, waits for them, and re-layouts: 11.2 us -> 9.07 us
    ppermute x32 -> x45, starting transfers between devices: 46.3 us -> 45.8 us  [exchange(): return lax.ppermute(values, axes, [(i, i ^ step) for i in range(32)])]
  transfers between devices with their start and end apart: 34 -> 47, of which waited for: 12 -> 12; matrix products, arithmetic and copies ran while one was open for 7% -> 6% of each run, Pallas kernels for 47% -> 51%
where the time goes in v4:
time: 394 us; the launch traced here: 387 us
  Pallas kernels  237 us (60%)
  waiting for transfers between devices  54.2 us (14%)
  starting transfers between devices  45.9 us (12%)
  local copies, waits for them, and re-layouts  23.8 us (6%)
  between operations  15.4 us (4%)
  other arithmetic  9.95 us (3%)
    ppermute x45, waiting for transfers between devices, exchange(): return lax.ppermute(values, axes, [(i, i ^ step) for i in range(32)])  54.2 us
    ppermute x45, starting transfers between devices, exchange(): return lax.ppermute(values, axes, [(i, i ^ step) for i in range(32)])  45.8 us
    pallas_call x1, Pallas kernels, feed_both(): pl.pallas_call(feed_kernel, out_shape=[jax.ShapeDtypeStruct((rows, width)...  38 us
    pallas_call x1, Pallas kernels, cross_backward(): pl.pallas_call(cross_backward_kernel, out_shape=[jax.ShapeDtypeStruct(sid...  32.4 us
    pallas_call x1, Pallas kernels, self_backward(): pl.pallas_call(body, out_shape=[jax.ShapeDtypeStruct((rows, width), bf16)...  30.2 us
    pallas_call x1, Pallas kernels, cross_forward(): pl.pallas_call(cross_forward_kernel, out_shape=[jax.ShapeDtypeStruct(side...  28.1 us
    pallas_call x1, Pallas kernels, memory_weight_grads(): pl.pallas_call(memory_weight_kernel, out_shape=[jax.ShapeDtypeStruct(half...  24.9 us
    pallas_call x1, Pallas kernels, project_memory(): pl.pallas_call(memory_kernel, out_shape=[jax.ShapeDtypeStruct(memory.shap...  24.7 us
  transfers between devices with their start and end apart: 47, of which 12 were waited for; matrix products, arithmetic and copies ran while one was open for 6% of the time, Pallas kernels for 51%

profile of v4, /device:TPU:8, one launch (start us, length us, event | category | flops | bytes accessed | tf_op | source)
XLA Modules:
  0.0 386.5 jit_solution(8800438734287174184)
XLA Ops:
  9.8 3.0 collective-permute-start.1
  15.2 3.4 collective-permute-done.1
  18.7 1.8 collective-permute-done.2
  22.3 2.4 collective-permute-start.7
  31.0 9.2 %collective-permute-done.7 = bf16[360,256]{1,0:T(8,128)(2,1)S(1)} collective-permute-done((bf16[360,256]{1,0:T(8,128)(2,1)S(1)}, bf16[360,256]{1,0:T(8,128)(2,1)S(1)}, u32[]{:S(2)}, u32[]{:S(2)}) %collective-permute-start.7) | collective-permute-done | bytes 184352 | tf_op jit(solution)/shard_map/ppermute | solution.py:942
  40.2 5.9 %collective-permute-done.8 = bf16[360,256]{1,0:T(8,128)(2,1)S(1)} collective-permute-done((bf16[360,256]{1,0:T(8,128)(2,1)S(1)}, bf16[360,256]{1,0:T(8,128)(2,1)S(1)}, u32[]{:S(2)}, u32[]{:S(2)}) %collective-permute-start.8) | collective-permute-done | bytes 184352 | tf_op jit(solution)/shard_map/ppermute | solution.py:942
  47.4 2.6 collective-permute-start.10
  50.1 1.6 collective-permute-start.11
  52.6 24.7 %memory_project.1 = (bf16[8,1024,768]{2,1,0:T(8,128)(2,1)}, bf16[8,1024,768]{2,1,0:T(8,128)(2,1)}, bf16[768,1536]{1,0:T(8,128)(2,1)}) custom-call(s32[8]{0:T(128)} %lengths.9, s32[32]{0:T(128)} %fusion.27.owners.refs_0_, bf16[8,1024,768]{2,1,0:T(8,128)(2,1)} %memory_ref.3, bf16[4,160,256]{2,1,0:T(8,128)(2,1)} %copy-done.6, bf16[4,160,256]{2,1,0:T(8,128)(2,1)} %copy-done.19, ...), custom_call_target="tpu_custom_call" | custom-call | flops 19327352832 | bytes 37748736 | tf_op jit(solution)/shard_map/memory_project/pallas_call | solution.py:151
  82.6 1.7 collective-permute-start.16
  84.3 3.5 collective-permute-start.17
  88.6 15.0 %self_attend.1 = (bf16[768,768]{1,0:T(8,128)(2,1)}, bf16[768,768]{1,0:T(8,128)(2,1)}, bf16[768,768]{1,0:T(8,128)(2,1)}, bf16[768,768]{1,0:T(8,128)(2,1)}, bf16[7...) custom-call(s32[32]{0:T(128)} %fusion.27.owners.refs_0_, bf16[768,768]{1,0:T(8,128)(2,1)} %bitcast.251, ...), custom_call_target="tpu_custom_call" | custom-call | flops 7247757312 | bytes 7077888 | tf_op jit(solution)/shard_map/self_attend/pallas_call | solution.py:239
  103.6 3.4 collective-permute-done.17.refs_6_
  107.1 4.8 %collective-permute-done.18.refs_7_ = bf16[4,144,256]{2,1,0:T(8,128)(2,1)S(1)} collective-permute-done((bf16[4,144,256]{2,1,0:T(8,128)(2,1)S(1)}, bf16[4,144,256]{2,1,0:T(8,128)(2,1)S(1)}, u32[]{:S(2)}, u32[]{:S(2)}) %collective-permute-start.18) | collective-permute-done | bytes 294944 | tf_op jit(solution)/shard_map/ppermute | solution.py:942
  115.7 6.5 %self_project.1 = (f32[768,768]{1,0:T(8,128)}, bf16[768,768]{1,0:T(8,128)(2,1)}, bf16[768,768]{1,0:T(8,128)(2,1)}, bf16[768,1536]{1,0:T(8,128)(2,1)}) custom-call(s32[32]{0:T(128)} %fusion.27.owners.refs_0_, bf16[768,768]{1,0:T(8,128)(2,1)} %bitcast.252, bf16[768,768]{1,0:T(8,128)(2,1)} %get-tuple-element.120.refs_2_.context_ref, ...), custom_call_target="tpu_custom_call" | custom-call | flops 1811939328 | bytes 7077888 | tf_op jit(solution)/shard_map/self_project/pallas_call | solution.py:278
  122.2 28.1 %cross_forward.1 = (bf16[768,768]{1,0:T(8,128)(2,1)}, bf16[8,1152,1024]{2,1,0:T(8,128)(2,1)}) custom-call(s32[8]{0:T(128)} %lengths.9, bf16[768,768]{1,0:T(8,128)(2,1)} %get-tuple-element.125.side_ref, bf16[8,1024,768]{2,1,0:T(8,128)(2,1)} %get-tuple-element.126.keys_ref, bf16[8,1024,768]{2,1,0:T(8,128)(2,1)} %get-tuple-element.127.values_ref), custom_call_target="tpu_custom_call" | custom-call | flops 9663676416 | bytes 37748736 | tf_op jit(solution)/shard_map/cross_forward/pallas_call | solution.py:333
  150.2 38.0 %feed_both.1 = (bf16[768,768]{1,0:T(8,128)(2,1)}, f32[768,768]{1,0:T(8,128)}, bf16[768,768]{1,0:T(8,128)(2,1)}, f32[1,768]{1,0:T(1,128)}, bf16[32,648,256]{2,1,0:T(8,128)(2,1)}) custom-call(f32[768,768]{1,0:T(8,128)} %get-tuple-element.124.after_ref, bf16[768,768]{1,0:T(8,128)(2,1)} %get-tuple-element.128.context_ref, bf16[768,768]{1,0:T(8,128)(2,1)} %bitcast.250, ...), custom_call_target="tpu_custom_call" | custom-call | flops 21743271936 | bytes 17694720 | tf_op jit(solution)/shard_map/feed_both/pallas_call | solution.py:456
  188.9 32.4 %cross_backward.1 = (bf16[768,768]{1,0:T(8,128)(2,1)}, bf16[8,768,1024]{2,1,0:T(8,128)(2,1)}, bf16[8,768,1024]{2,1,0:T(8,128)(2,1)}) custom-call(s32[8]{0:T(128)} %lengths.9, bf16[768,768]{1,0:T(8,128)(2,1)} %get-tuple-element.131.grad_ref, bf16[768,768]{1,0:T(8,128)(2,1)} %get-tuple-element.128.context_ref, bf16[768,768]{1,0:T(8,128)(2,1)} %get-tuple-element.125.side_ref, ...), custom_call_target="tpu_custom_call" | custom-call | flops 19327352832 | bytes 62914560 | tf_op jit(solution)/shard_map/cross_backward/pallas_call | solution.py:545
  221.2 12.6 %self_output_backward.1 = (f32[768,768]{1,0:T(8,128)}, bf16[768,768]{1,0:T(8,128)(2,1)}, f32[1,768]{1,0:T(1,128)}, bf16[16,144,256]{2,1,0:T(8,128)(2,1)}, bf16[16,144,256]{2,1,0:T(8,128)(2,1)}) custom-call(s32[32]{0:T(128)} %fusion.27.owners.refs_0_, bf16[768,768]{1,0:T(8,128)(2,1)} %get-tuple-element.133.grad_side_ref, ...), custom_call_target="tpu_custom_call" | custom-call | flops 3623878656 | bytes 11796480 | tf_op jit(solution)/shard_map/self_output_backward/pallas_call | solution.py:719
  234.9 30.2 %self_backward.1 = (bf16[768,768]{1,0:T(8,128)(2,1)}, bf16[16,240,256]{2,1,0:T(8,128)(2,1)}, bf16[16,240,256]{2,1,0:T(8,128)(2,1)}) custom-call(s32[32]{0:T(128)} %fusion.27.owners.refs_0_, bf16[768,768]{1,0:T(8,128)(2,1)} %get-tuple-element.137.refs_1_, f32[768,768]{1,0:T(8,128)} %get-tuple-element.138.refs_2_, ...), custom_call_target="tpu_custom_call" | custom-call | flops 14495514624 | bytes 11796480 | tf_op jit(solution)/shard_map/self_backward/pallas_call | solution.py:870
  266.2 1.8 collective-permute-start.29
  268.0 3.1 collective-permute-start.30
  271.2 24.9 %memory_weight_grads.1 = (bf16[16,144,256]{2,1,0:T(8,128)(2,1)}, bf16[16,144,256]{2,1,0:T(8,128)(2,1)}) custom-call(s32[8]{0:T(128)} %lengths.9, s32[32]{0:T(128)} %fusion.27.owners.refs_0_, bf16[8,1024,768]{2,1,0:T(8,128)(2,1)} %memory_ref.3, bf16[8,768,1024]{2,1,0:T(8,128)(2,1)} %get-tuple-element.151.grad_keys_ref, ...), custom_call_target="tpu_custom_call" | custom-call | flops 19327352832 | bytes 37748736 | tf_op jit(solution)/shard_map/memory_weight_grads/pallas_call | solution.py:617
  296.1 3.0 add_convert_fusion.1
  299.7 5.9 %collective-permute-start.34 = (bf16[4,240,256]{2,1,0:T(8,128)(2,1)}, bf16[4,240,256]{2,1,0:T(8,128)(2,1)}, u32[]{:S(2)}, u32[]{:S(2)}) collective-permute-start(bf16[4,240,256]{2,1,0:T(8,128)(2,1)} %get-tuple-element.166), channel_id=1, source_target_pairs={{0,4},{1,5},{2,6},{3,7},{4,0},{5,1},{6,2},{7,3},{8,12},{9,13},{10,... | collective-permute-start | bytes 1474568 | tf_op jit(solution)/shard_map/ppermute | solution.py:942
  305.6 24.3 %memory_grad.1 = bf16[8,1024,768]{2,1,0:T(8,128)(2,1)} custom-call(s32[8]{0:T(128)} %lengths.9, bf16[8,768,1024]{2,1,0:T(8,128)(2,1)} %get-tuple-element.151.grad_keys_ref, bf16[8,768,1024]{2,1,0:T(8,128)(2,1)} %get-tuple-element.152.grad_values_ref, bf16[768,1536]{1,0:T(8,128)(2,1)} %get-tuple-element.161.weight_ref), custom_call_target="tpu_custom_call" | custom-call | flops 19327352832 | bytes 37748736 | tf_op jit(solution)/shard_map/memory_grad/pallas_call | solution.py:667
  332.0 5.7 %collective-permute-start.40 = (bf16[4,144,256]{2,1,0:T(8,128)(2,1)S(1)}, bf16[4,144,256]{2,1,0:T(8,128)(2,1)S(1)}, u32[]{:S(2)}, u32[]{:S(2)}) collective-permute-start(bf16[4,144,256]{2,1,0:T(8,128)(2,1)S(1)} %get-tuple-element.186), channel_id=1, source_target_pairs={{0,4},{1,5},{2,6},{3,7},{4,0},{5,1},{6,2},{7,3},{8,12},{9,13},{10,... | collective-permute-start | bytes 884744 | tf_op jit(solution)/shard_map/ppermute | solution.py:942
  339.5 2.1 collective-permute-done.39
  342.9 5.3 %collective-permute-done.40 = bf16[4,144,256]{2,1,0:T(8,128)(2,1)S(1)} collective-permute-done((bf16[4,144,256]{2,1,0:T(8,128)(2,1)S(1)}, bf16[4,144,256]{2,1,0:T(8,128)(2,1)S(1)}, u32[]{:S(2)}, u32[]{:S(2)}) %collective-permute-start.40) | collective-permute-done | bytes 294944 | tf_op jit(solution)/shard_map/ppermute | solution.py:942
  348.6 3.4 collective-permute-start.44
  352.0 5.3 %collective-permute-done.37 = bf16[384,256]{1,0:T(8,128)(2,1)S(1)} collective-permute-done((bf16[384,256]{1,0:T(8,128)(2,1)S(1)}, bf16[384,256]{1,0:T(8,128)(2,1)S(1)}, u32[]{:S(2)}, u32[]{:S(2)}) %collective-permute-start.37) | collective-permute-done | bytes 196640 | tf_op jit(solution)/shard_map/ppermute | solution.py:942
  357.3 11.7 %collective-permute-done.38 = bf16[384,256]{1,0:T(8,128)(2,1)S(1)} collective-permute-done((bf16[384,256]{1,0:T(8,128)(2,1)S(1)}, bf16[384,256]{1,0:T(8,128)(2,1)S(1)}, u32[]{:S(2)}, u32[]{:S(2)}) %collective-permute-start.38) | collective-permute-done | bytes 196640 | tf_op jit(solution)/shard_map/ppermute | solution.py:942
  (258 shorter events, 43.7 us)
Async XLA Ops:
  7.2 143.0 %all-gather.3.cloned.1.call-start = ((), (), s32[]{:S(2)}) async-start(), calls=%async_computation.2 | async-start | bytes 10948608 | tf_op jit(solution)/shard_map/all_gather | solution.py:926
  21.2 354.1 %reduce-scatter.2.cloned.1.call-start = ((), (), s32[]{:S(2)}) async-start(), calls=%async_computation.1 | async-start | bytes 10948608 | tf_op jit(solution)/shard_map/reduce_scatter | solution.py:932
  22.3 17.9 %collective-permute-start.7 = (bf16[360,256]{1,0:T(8,128)(2,1)S(1)}, bf16[360,256]{1,0:T(8,128)(2,1)S(1)}, u32[]{:S(2)}, u32[]{:S(2)}) collective-permute-start(bf16[360,256]{1,0:T(8,128)(2,1)S(1)} %constant_dynamic-update-slice_fusion), channel_id=1, source_target_pairs={{0,16},{1,17},{2,18},{3,19},{4,20},{5,21},{6,22},{7,23},{8,24},{9,... | collective-permute-start | bytes 552968 | tf_op jit(solution)/shard_map/ppermute | solution.py:942
  24.8 21.3 %collective-permute-start.3 = (bf16[4,160,256]{2,1,0:T(8,128)(2,1)S(1)}, bf16[4,160,256]{2,1,0:T(8,128)(2,1)S(1)}, u32[]{:S(2)}, u32[]{:S(2)}) collective-permute-start(bf16[4,160,256]{2,1,0:T(8,128)(2,1)S(1)} %pad_maximum_fusion.2.refs_0_), channel_id=1, source_target_pairs={{0,1},{1,0},{2,3},{3,2},{4,5},{5,4},{6,7},{7,6},{8,9},{9,8},{10,11... | collective-permute-start | bytes 983048 | tf_op jit(solution)/shard_map/ppermute | solution.py:942
  26.4 19.8 %collective-permute-start.4 = (bf16[4,160,256]{2,1,0:T(8,128)(2,1)S(1)}, bf16[4,160,256]{2,1,0:T(8,128)(2,1)S(1)}, u32[]{:S(2)}, u32[]{:S(2)}) collective-permute-start(bf16[4,160,256]{2,1,0:T(8,128)(2,1)S(1)} %pad_maximum_fusion.2.refs_0_), channel_id=1, source_target_pairs={{0,4},{1,5},{2,6},{3,7},{4,0},{5,1},{6,2},{7,3},{8,12},{9,13},{10,... | collective-permute-start | bytes 983048 | tf_op jit(solution)/shard_map/ppermute | solution.py:942
  27.9 18.3 %collective-permute-start.5 = (bf16[4,160,256]{2,1,0:T(8,128)(2,1)S(1)}, bf16[4,160,256]{2,1,0:T(8,128)(2,1)S(1)}, u32[]{:S(2)}, u32[]{:S(2)}) collective-permute-start(bf16[4,160,256]{2,1,0:T(8,128)(2,1)S(1)} %pad_maximum_fusion.2.refs_0_), channel_id=1, source_target_pairs={{0,5},{1,4},{2,7},{3,6},{4,1},{5,0},{6,3},{7,2},{8,13},{9,12},{10,... | collective-permute-start | bytes 983048 | tf_op jit(solution)/shard_map/ppermute | solution.py:942
  29.9 16.2 %collective-permute-start.8 = (bf16[360,256]{1,0:T(8,128)(2,1)S(1)}, bf16[360,256]{1,0:T(8,128)(2,1)S(1)}, u32[]{:S(2)}, u32[]{:S(2)}) collective-permute-start(bf16[360,256]{1,0:T(8,128)(2,1)S(1)} %constant_dynamic-update-slice_fusion), channel_id=1, source_target_pairs={{0,24},{1,25},{2,26},{3,27},{4,28},{5,29},{6,30},{7,31},{8,16},{9,... | collective-permute-start | bytes 552968 | tf_op jit(solution)/shard_map/ppermute | solution.py:942
  47.4 32.8 %collective-permute-start.10 = (bf16[4,216,256]{2,1,0:T(8,128)(2,1)S(1)}, bf16[4,216,256]{2,1,0:T(8,128)(2,1)}, u32[]{:S(2)}, u32[]{:S(2)}) collective-permute-start(bf16[4,216,256]{2,1,0:T(8,128)(2,1)S(1)} %pad_maximum_fusion.refs_4_), channel_id=1, source_target_pairs={{0,4},{1,5},{2,6},{3,7},{4,0},{5,1},{6,2},{7,3},{8,12},{9,13},{10,... | collective-permute-start | bytes 1327112 | tf_op jit(solution)/shard_map/ppermute | solution.py:942
  50.1 30.1 %collective-permute-start.11 = (bf16[4,216,256]{2,1,0:T(8,128)(2,1)S(1)}, bf16[4,216,256]{2,1,0:T(8,128)(2,1)S(1)}, u32[]{:S(2)}, u32[]{:S(2)}) collective-permute-start(bf16[4,216,256]{2,1,0:T(8,128)(2,1)S(1)} %pad_maximum_fusion.refs_4_), channel_id=1, source_target_pairs={{0,5},{1,4},{2,7},{3,6},{4,1},{5,0},{6,3},{7,2},{8,13},{9,12},{10,... | collective-permute-start | bytes 1327112 | tf_op jit(solution)/shard_map/ppermute | solution.py:942
  51.8 29.2 %collective-permute-start.9 = (bf16[4,216,256]{2,1,0:T(8,128)(2,1)S(1)}, bf16[4,216,256]{2,1,0:T(8,128)(2,1)S(1)}, u32[]{:S(2)}, u32[]{:S(2)}) collective-permute-start(bf16[4,216,256]{2,1,0:T(8,128)(2,1)S(1)} %pad_maximum_fusion.refs_4_), channel_id=1, source_target_pairs={{0,1},{1,0},{2,3},{3,2},{4,5},{5,4},{6,7},{7,6},{8,9},{9,8},{10,11... | collective-permute-start | bytes 1327112 | tf_op jit(solution)/shard_map/ppermute | solution.py:942
  51.9 32.4 %collective-permute-start.19 = (bf16[4,216,256]{2,1,0:T(8,128)(2,1)S(1)}, bf16[4,216,256]{2,1,0:T(8,128)(2,1)}, u32[]{:S(2)}, u32[]{:S(2)}) collective-permute-start(bf16[4,216,256]{2,1,0:T(8,128)(2,1)S(1)} %pad_maximum_fusion.refs_4_), channel_id=1, source_target_pairs={{0,2},{1,3},{2,0},{3,1},{4,6},{5,7},{6,4},{7,5},{8,10},{9,11},{10,... | collective-permute-start | bytes 1327112 | tf_op jit(solution)/shard_map/ppermute | solution.py:942
  82.6 21.0 %collective-permute-start.16 = (bf16[4,144,256]{2,1,0:T(8,128)(2,1)S(1)}, bf16[4,144,256]{2,1,0:T(8,128)(2,1)S(1)}, u32[]{:S(2)}, u32[]{:S(2)}) collective-permute-start(bf16[4,144,256]{2,1,0:T(8,128)(2,1)S(1)} %pad_maximum_fusion.3.refs_4_), channel_id=1, source_target_pairs={{0,1},{1,0},{2,3},{3,2},{4,5},{5,4},{6,7},{7,6},{8,9},{9,8},{10,11... | collective-permute-start | bytes 884744 | tf_op jit(solution)/shard_map/ppermute | solution.py:942
  84.3 22.8 %collective-permute-start.17 = (bf16[4,144,256]{2,1,0:T(8,128)(2,1)S(1)}, bf16[4,144,256]{2,1,0:T(8,128)(2,1)S(1)}, u32[]{:S(2)}, u32[]{:S(2)}) collective-permute-start(bf16[4,144,256]{2,1,0:T(8,128)(2,1)S(1)} %pad_maximum_fusion.3.refs_4_), channel_id=1, source_target_pairs={{0,4},{1,5},{2,6},{3,7},{4,0},{5,1},{6,2},{7,3},{8,12},{9,13},{10,... | collective-permute-start | bytes 884744 | tf_op jit(solution)/shard_map/ppermute | solution.py:942
  87.8 24.1 %collective-permute-start.18 = (bf16[4,144,256]{2,1,0:T(8,128)(2,1)S(1)}, bf16[4,144,256]{2,1,0:T(8,128)(2,1)S(1)}, u32[]{:S(2)}, u32[]{:S(2)}) collective-permute-start(bf16[4,144,256]{2,1,0:T(8,128)(2,1)S(1)} %pad_maximum_fusion.3.refs_4_), channel_id=1, source_target_pairs={{0,5},{1,4},{2,7},{3,6},{4,1},{5,0},{6,3},{7,2},{8,13},{9,12},{10,... | collective-permute-start | bytes 884744 | tf_op jit(solution)/shard_map/ppermute | solution.py:942
  87.8 26.1 %collective-permute-start.23 = (bf16[4,144,256]{2,1,0:T(8,128)(2,1)S(1)}, bf16[4,144,256]{2,1,0:T(8,128)(2,1)S(1)}, u32[]{:S(2)}, u32[]{:S(2)}) collective-permute-start(bf16[4,144,256]{2,1,0:T(8,128)(2,1)S(1)} %pad_maximum_fusion.3.refs_4_), channel_id=1, source_target_pairs={{0,2},{1,3},{2,0},{3,1},{4,6},{5,7},{6,4},{7,5},{8,10},{9,11},{10,... | collective-permute-start | bytes 884744 | tf_op jit(solution)/shard_map/ppermute | solution.py:942
  233.9 31.3 %collective-permute-start.27 = (bf16[16,144,256]{2,1,0:T(8,128)(2,1)}, bf16[16,144,256]{2,1,0:T(8,128)(2,1)S(1)}, u32[]{:S(2)}, u32[]{:S(2)}) collective-permute-start(bf16[16,144,256]{2,1,0:T(8,128)(2,1)} %get-tuple-element.150), channel_id=1, source_target_pairs={{0,2},{1,3},{2,0},{3,1},{4,6},{5,7},{6,4},{7,5},{8,10},{9,11},{10,... | collective-permute-start | bytes 3538952 | tf_op jit(solution)/shard_map/ppermute | solution.py:942
  265.1 31.0 %collective-permute-start.28 = (bf16[16,240,256]{2,1,0:T(8,128)(2,1)}, bf16[16,240,256]{2,1,0:T(8,128)(2,1)}, u32[]{:S(2)}, u32[]{:S(2)}) collective-permute-start(bf16[16,240,256]{2,1,0:T(8,128)(2,1)} %get-tuple-element.156), channel_id=1, source_target_pairs={{0,2},{1,3},{2,0},{3,1},{4,6},{5,7},{6,4},{7,5},{8,10},{9,11},{10,... | collective-permute-start | bytes 5898248 | tf_op jit(solution)/shard_map/ppermute | solution.py:942
  266.2 32.9 %collective-permute-start.29 = (bf16[4,144,256]{2,1,0:T(8,128)(2,1)}, bf16[4,144,256]{2,1,0:T(8,128)(2,1)}, u32[]{:S(2)}, u32[]{:S(2)}) collective-permute-start(bf16[4,144,256]{2,1,0:T(8,128)(2,1)} %get-tuple-element.158), channel_id=1, source_target_pairs={{0,1},{1,0},{2,3},{3,2},{4,5},{5,4},{6,7},{7,6},{8,9},{9,8},{10,11... | collective-permute-start | bytes 884744 | tf_op jit(solution)/shard_map/ppermute | solution.py:942
  268.0 31.1 %collective-permute-start.30 = (bf16[4,144,256]{2,1,0:T(8,128)(2,1)}, bf16[4,144,256]{2,1,0:T(8,128)(2,1)}, u32[]{:S(2)}, u32[]{:S(2)}) collective-permute-start(bf16[4,144,256]{2,1,0:T(8,128)(2,1)} %get-tuple-element.159), channel_id=1, source_target_pairs={{0,4},{1,5},{2,6},{3,7},{4,0},{5,1},{6,2},{7,3},{8,12},{9,13},{10,... | collective-permute-start | bytes 884744 | tf_op jit(solution)/shard_map/ppermute | solution.py:942
  271.2 28.0 %collective-permute-start.31 = (bf16[4,144,256]{2,1,0:T(8,128)(2,1)}, bf16[4,144,256]{2,1,0:T(8,128)(2,1)}, u32[]{:S(2)}, u32[]{:S(2)}) collective-permute-start(bf16[4,144,256]{2,1,0:T(8,128)(2,1)} %get-tuple-element.160), channel_id=1, source_target_pairs={{0,5},{1,4},{2,7},{3,6},{4,1},{5,0},{6,3},{7,2},{8,13},{9,12},{10,... | collective-permute-start | bytes 884744 | tf_op jit(solution)/shard_map/ppermute | solution.py:942
  296.1 35.2 %collective-permute-start.32 = (bf16[16,144,256]{2,1,0:T(8,128)(2,1)}, bf16[16,144,256]{2,1,0:T(8,128)(2,1)S(1)}, u32[]{:S(2)}, u32[]{:S(2)}) collective-permute-start(bf16[16,144,256]{2,1,0:T(8,128)(2,1)} %get-tuple-element.162), channel_id=1, source_target_pairs={{0,2},{1,3},{2,0},{3,1},{4,6},{5,7},{6,4},{7,5},{8,10},{9,11},{10,... | collective-permute-start | bytes 3538952 | tf_op jit(solution)/shard_map/ppermute | solution.py:942
  299.2 38.5 %collective-permute-start.33 = (bf16[4,240,256]{2,1,0:T(8,128)(2,1)}, bf16[4,240,256]{2,1,0:T(8,128)(2,1)}, u32[]{:S(2)}, u32[]{:S(2)}) collective-permute-start(bf16[4,240,256]{2,1,0:T(8,128)(2,1)} %get-tuple-element.165), channel_id=1, source_target_pairs={{0,1},{1,0},{2,3},{3,2},{4,5},{5,4},{6,7},{7,6},{8,9},{9,8},{10,11... | collective-permute-start | bytes 1474568 | tf_op jit(solution)/shard_map/ppermute | solution.py:942
  299.7 38.0 %collective-permute-start.34 = (bf16[4,240,256]{2,1,0:T(8,128)(2,1)}, bf16[4,240,256]{2,1,0:T(8,128)(2,1)}, u32[]{:S(2)}, u32[]{:S(2)}) collective-permute-start(bf16[4,240,256]{2,1,0:T(8,128)(2,1)} %get-tuple-element.166), channel_id=1, source_target_pairs={{0,4},{1,5},{2,6},{3,7},{4,0},{5,1},{6,2},{7,3},{8,12},{9,13},{10,... | collective-permute-start | bytes 1474568 | tf_op jit(solution)/shard_map/ppermute | solution.py:942
  305.6 32.1 %collective-permute-start.35 = (bf16[4,240,256]{2,1,0:T(8,128)(2,1)}, bf16[4,240,256]{2,1,0:T(8,128)(2,1)}, u32[]{:S(2)}, u32[]{:S(2)}) collective-permute-start(bf16[4,240,256]{2,1,0:T(8,128)(2,1)} %get-tuple-element.167), channel_id=1, source_target_pairs={{0,5},{1,4},{2,7},{3,6},{4,1},{5,0},{6,3},{7,2},{8,13},{9,12},{10,... | collective-permute-start | bytes 1474568 | tf_op jit(solution)/shard_map/ppermute | solution.py:942
  331.6 9.9 %collective-permute-start.39 = (bf16[4,144,256]{2,1,0:T(8,128)(2,1)S(1)}, bf16[4,144,256]{2,1,0:T(8,128)(2,1)S(1)}, u32[]{:S(2)}, u32[]{:S(2)}) collective-permute-start(bf16[4,144,256]{2,1,0:T(8,128)(2,1)S(1)} %get-tuple-element.184), channel_id=1, source_target_pairs={{0,1},{1,0},{2,3},{3,2},{4,5},{5,4},{6,7},{7,6},{8,9},{9,8},{10,11... | collective-permute-start | bytes 884744 | tf_op jit(solution)/shard_map/ppermute | solution.py:942
  332.0 16.2 %collective-permute-start.40 = (bf16[4,144,256]{2,1,0:T(8,128)(2,1)S(1)}, bf16[4,144,256]{2,1,0:T(8,128)(2,1)S(1)}, u32[]{:S(2)}, u32[]{:S(2)}) collective-permute-start(bf16[4,144,256]{2,1,0:T(8,128)(2,1)S(1)} %get-tuple-element.186), channel_id=1, source_target_pairs={{0,4},{1,5},{2,6},{3,7},{4,0},{5,1},{6,2},{7,3},{8,12},{9,13},{10,... | collective-permute-start | bytes 884744 | tf_op jit(solution)/shard_map/ppermute | solution.py:942
  337.7 10.6 %collective-permute-start.41 = (bf16[4,144,256]{2,1,0:T(8,128)(2,1)S(1)}, bf16[4,144,256]{2,1,0:T(8,128)(2,1)S(1)}, u32[]{:S(2)}, u32[]{:S(2)}) collective-permute-start(bf16[4,144,256]{2,1,0:T(8,128)(2,1)S(1)} %get-tuple-element.185), channel_id=1, source_target_pairs={{0,5},{1,4},{2,7},{3,6},{4,1},{5,0},{6,3},{7,2},{8,13},{9,12},{10,... | collective-permute-start | bytes 884744 | tf_op jit(solution)/shard_map/ppermute | solution.py:942
  339.4 17.8 %collective-permute-start.37 = (bf16[384,256]{1,0:T(8,128)(2,1)S(1)}, bf16[384,256]{1,0:T(8,128)(2,1)S(1)}, u32[]{:S(2)}, u32[]{:S(2)}) collective-permute-start(bf16[384,256]{1,0:T(8,128)(2,1)S(1)} %get-tuple-element.193), channel_id=1, source_target_pairs={{0,16},{1,17},{2,18},{3,19},{4,20},{5,21},{6,22},{7,23},{8,24},{9,... | collective-permute-start | bytes 589832 | tf_op jit(solution)/shard_map/ppermute | solution.py:942
  341.6 27.4 %collective-permute-start.38 = (bf16[384,256]{1,0:T(8,128)(2,1)S(1)}, bf16[384,256]{1,0:T(8,128)(2,1)S(1)}, u32[]{:S(2)}, u32[]{:S(2)}) collective-permute-start(bf16[384,256]{1,0:T(8,128)(2,1)S(1)} %get-tuple-element.192), channel_id=1, source_target_pairs={{0,24},{1,25},{2,26},{3,27},{4,28},{5,29},{6,30},{7,31},{8,16},{9,... | collective-permute-start | bytes 589832 | tf_op jit(solution)/shard_map/ppermute | solution.py:942
  348.5 25.4 %collective-permute-start.42 = (bf16[144,256]{1,0:T(8,128)(2,1)S(1)}, bf16[144,256]{1,0:T(8,128)(2,1)S(1)}, u32[]{:S(2)}, u32[]{:S(2)}) collective-permute-start(bf16[144,256]{1,0:T(8,128)(2,1)S(1)} %get-tuple-element.205), channel_id=1, source_target_pairs={{0,8},{1,9},{2,10},{3,11},{4,12},{5,13},{6,14},{7,15},{8,0},{9,1},... | collective-permute-start | bytes 221192 | tf_op jit(solution)/shard_map/ppermute | solution.py:942
  348.5 25.3 %collective-permute-start.43 = (bf16[144,256]{1,0:T(8,128)(2,1)S(1)}, bf16[144,256]{1,0:T(8,128)(2,1)S(1)}, u32[]{:S(2)}, u32[]{:S(2)}) collective-permute-start(bf16[144,256]{1,0:T(8,128)(2,1)S(1)} %get-tuple-element.207), channel_id=1, source_target_pairs={{0,16},{1,17},{2,18},{3,19},{4,20},{5,21},{6,22},{7,23},{8,24},{9,... | collective-permute-start | bytes 221192 | tf_op jit(solution)/shard_map/ppermute | solution.py:942
  348.6 25.2 %collective-permute-start.44 = (bf16[144,256]{1,0:T(8,128)(2,1)S(1)}, bf16[144,256]{1,0:T(8,128)(2,1)S(1)}, u32[]{:S(2)}, u32[]{:S(2)}) collective-permute-start(bf16[144,256]{1,0:T(8,128)(2,1)S(1)} %get-tuple-element.206), channel_id=1, source_target_pairs={{0,24},{1,25},{2,26},{3,27},{4,28},{5,29},{6,30},{7,31},{8,16},{9,... | collective-permute-start | bytes 221192 | tf_op jit(solution)/shard_map/ppermute | solution.py:942
  (54 other events, 495.5 us)
Sparse Core Ops, SparseCore 0:
  21.4 109.1 all-gather.2
  188.4 181.3 reduce-scatter.1

commit v5 on v4

--- a/solution.py
+++ b/solution.py
@@ -301,11 +301,19 @@
     memory_len = keys_ref.shape[1]
     half = lane_halves(target_len)
 
+    pairs = width // pair_width
+    columns = [slice(p * pair_width, (p + 1) * pair_width) for p in range(pairs)]
+
     def attend(count):
-        for p in range(width // pair_width):
-            cols = slice(p * pair_width, (p + 1) * pair_width)
-            stack = masked_stack(side_ref[:, cols], half)
-            scores = dot(stack, keys_ref[0, :count, cols], NT)
+        def pair_scores(p):
+            stack = masked_stack(side_ref[:, columns[p]], half)
+            return dot(stack, keys_ref[0, :count, columns[p]], NT)
+
+        coming = pair_scores(0)
+        for p, cols in enumerate(columns):
+            scores = coming
+            if p + 1 < pairs:
+                coming = pair_scores(p + 1)
             terms = jnp.exp(scores - jnp.max(scores, axis=-1, keepdims=True))
             scale = 1.0 / jnp.sum(terms, axis=-1, keepdims=True)
             weights = (terms * scale).astype(bf16)
@@ -509,23 +517,31 @@
     memory_len = keys_ref.shape[1]
     half = lane_halves(target_len)
 
+    pairs = width // pair_width
+    columns = [slice(p * pair_width, (p + 1) * pair_width) for p in range(pairs)]
+
     def attend(count):
-        for p in range(width // pair_width):
-            cols = slice(p * pair_width, (p + 1) * pair_width)
-            grad_rows = grad_ref[:, cols]
-            grad_stack = masked_stack(grad_rows, half)
+        def pair_start(p):
+            cols = columns[p]
+            grad_stack = masked_stack(grad_ref[:, cols], half)
+            return grad_stack, dot(grad_stack, values_ref[0, :count, cols], NT)
+
+        coming = pair_start(0)
+        for p, cols in enumerate(columns):
+            grad_stack, grad_probs = coming
+            weights = weights_ref[0, 2 * target_len * p : 2 * target_len * (p + 1), :count]
+            if p + 1 < pairs:
+                coming = pair_start(p + 1)
             query_stack = masked_stack(side_ref[:, cols], half)
-            product = grad_rows.astype(f32) * context_ref[:, cols].astype(f32)
+            product = grad_ref[:, cols].astype(f32) * context_ref[:, cols].astype(f32)
             inner = jnp.sum(masked_stack(product, half), axis=-1, keepdims=True)
-            weights = weights_ref[0, 2 * target_len * p : 2 * target_len * (p + 1), :count]
-            grad_probs = dot(grad_stack, values_ref[0, :count, cols], NT)
             grad_scores = (weights.astype(f32) * (grad_probs - inner)).astype(bf16)
+            grad_values_ref[0, cols, :count] = dot(grad_stack, weights, TN).astype(bf16)
             both = dot(grad_scores, keys_ref[0, :count, cols])
             grad_side_ref[:, cols] = jnp.where(half, both[:target_len], both[target_len:]).astype(
                 bf16
             )
             grad_keys_ref[0, cols, :count] = dot(query_stack, grad_scores, TN).astype(bf16)
-            grad_values_ref[0, cols, :count] = dot(grad_stack, weights, TN).astype(bf16)
 
     @pl.when(lengths[seq] > memory_len // 2)
     def _():

time: 394 us -> 386 us (0.980)
  waiting for transfers between devices: 54.2 us -> 49.6 us
  Pallas kernels: 237 us -> 233 us
    ppermute x45, waiting for transfers between devices: 54.2 us -> 49 us  [exchange(): return lax.ppermute(values, axes, [(i, i ^ step) for i in range(32)])]
    pallas_call x1, Pallas kernels: 28.1 us -> 23.1 us  [cross_forward(): pl.pallas_call(cross_forward_kernel, out_shape=[jax.ShapeDtypeStruct(side...]
  transfers between devices with their start and end apart: 47 -> 47, of which waited for: 12 -> 13; matrix products, arithmetic and copies ran while one was open for 6% -> 6% of each run, Pallas kernels for 51% -> 51%
where the time goes in v5:
time: 386 us; the launch traced here: 379 us
  Pallas kernels  233 us (60%)
  waiting for transfers between devices  49.6 us (13%)
  starting transfers between devices  47.5 us (12%)
  local copies, waits for them, and re-layouts  23.1 us (6%)
  between operations  15.4 us (4%)
  other arithmetic  10 us (3%)
    ppermute x45, waiting for transfers between devices, exchange(): return lax.ppermute(values, axes, [(i, i ^ step) for i in range(32)])  49 us
    ppermute x45, starting transfers between devices, exchange(): return lax.ppermute(values, axes, [(i, i ^ step) for i in range(32)])  47.4 us
    pallas_call x1, Pallas kernels, feed_both(): pl.pallas_call(feed_kernel, out_shape=[jax.ShapeDtypeStruct((rows, width)...  38.1 us
    pallas_call x1, Pallas kernels, cross_backward(): pl.pallas_call(cross_backward_kernel, out_shape=[jax.ShapeDtypeStruct(sid...  31.1 us
    pallas_call x1, Pallas kernels, self_backward(): pl.pallas_call(body, out_shape=[jax.ShapeDtypeStruct((rows, width), bf16)...  30.2 us
    pallas_call x1, Pallas kernels, memory_weight_grads(): pl.pallas_call(memory_weight_kernel, out_shape=[jax.ShapeDtypeStruct(half...  25.2 us
    pallas_call x1, Pallas kernels, project_memory(): pl.pallas_call(memory_kernel, out_shape=[jax.ShapeDtypeStruct(memory.shap...  25.1 us
    pallas_call x1, Pallas kernels, memory_gradient(): pl.pallas_call(memory_grad_kernel, out_shape=jax.ShapeDtypeStruct((batch,...  24.5 us
  transfers between devices with their start and end apart: 47, of which 13 were waited for; matrix products, arithmetic and copies ran while one was open for 6% of the time, Pallas kernels for 51%

profile of v5, /device:TPU:8, one launch (start us, length us, event | category | flops | bytes accessed | tf_op | source)
XLA Modules:
  0.0 378.8 jit_solution(1354398026835962756)
XLA Ops:
  9.8 3.0 collective-permute-start.1
  15.2 3.4 collective-permute-done.1
  18.7 1.8 collective-permute-done.2
  22.3 2.4 collective-permute-start.7
  31.0 9.2 %collective-permute-done.7 = bf16[360,256]{1,0:T(8,128)(2,1)S(1)} collective-permute-done((bf16[360,256]{1,0:T(8,128)(2,1)S(1)}, bf16[360,256]{1,0:T(8,128)(2,1)S(1)}, u32[]{:S(2)}, u32[]{:S(2)}) %collective-permute-start.7) | collective-permute-done | bytes 184352 | tf_op jit(solution)/shard_map/ppermute | solution.py:958
  40.2 5.9 %collective-permute-done.8 = bf16[360,256]{1,0:T(8,128)(2,1)S(1)} collective-permute-done((bf16[360,256]{1,0:T(8,128)(2,1)S(1)}, bf16[360,256]{1,0:T(8,128)(2,1)S(1)}, u32[]{:S(2)}, u32[]{:S(2)}) %collective-permute-start.8) | collective-permute-done | bytes 184352 | tf_op jit(solution)/shard_map/ppermute | solution.py:958
  47.4 2.6 collective-permute-start.10
  50.1 1.6 collective-permute-start.11
  52.6 25.1 %memory_project.1 = (bf16[8,1024,768]{2,1,0:T(8,128)(2,1)}, bf16[8,1024,768]{2,1,0:T(8,128)(2,1)}, bf16[768,1536]{1,0:T(8,128)(2,1)}) custom-call(s32[8]{0:T(128)} %lengths.9, s32[32]{0:T(128)} %fusion.27.owners.refs_0_, bf16[8,1024,768]{2,1,0:T(8,128)(2,1)} %memory_ref.3, bf16[4,160,256]{2,1,0:T(8,128)(2,1)} %copy-done.6, bf16[4,160,256]{2,1,0:T(8,128)(2,1)} %copy-done.19, ...), custom_call_target="tpu_custom_call" | custom-call | flops 19327352832 | bytes 37748736 | tf_op jit(solution)/shard_map/memory_project/pallas_call | solution.py:151
  82.6 2.8 collective-permute-start.16
  87.0 16.3 %self_attend.1 = (bf16[768,768]{1,0:T(8,128)(2,1)}, bf16[768,768]{1,0:T(8,128)(2,1)}, bf16[768,768]{1,0:T(8,128)(2,1)}, bf16[768,768]{1,0:T(8,128)(2,1)}, bf16[7...) custom-call(s32[32]{0:T(128)} %fusion.27.owners.refs_0_, bf16[768,768]{1,0:T(8,128)(2,1)} %bitcast.251, ...), custom_call_target="tpu_custom_call" | custom-call | flops 7247757312 | bytes 7077888 | tf_op jit(solution)/shard_map/self_attend/pallas_call | solution.py:239
  103.3 7.0 %collective-permute-done.18.refs_7_ = bf16[4,144,256]{2,1,0:T(8,128)(2,1)S(1)} collective-permute-done((bf16[4,144,256]{2,1,0:T(8,128)(2,1)S(1)}, bf16[4,144,256]{2,1,0:T(8,128)(2,1)S(1)}, u32[]{:S(2)}, u32[]{:S(2)}) %collective-permute-start.18) | collective-permute-done | bytes 294944 | tf_op jit(solution)/shard_map/ppermute | solution.py:958
  114.1 6.4 %self_project.1 = (f32[768,768]{1,0:T(8,128)}, bf16[768,768]{1,0:T(8,128)(2,1)}, bf16[768,768]{1,0:T(8,128)(2,1)}, bf16[768,1536]{1,0:T(8,128)(2,1)}) custom-call(s32[32]{0:T(128)} %fusion.27.owners.refs_0_, bf16[768,768]{1,0:T(8,128)(2,1)} %bitcast.252, bf16[768,768]{1,0:T(8,128)(2,1)} %get-tuple-element.120.refs_2_.context_ref, ...), custom_call_target="tpu_custom_call" | custom-call | flops 1811939328 | bytes 7077888 | tf_op jit(solution)/shard_map/self_project/pallas_call | solution.py:278
  120.5 23.1 %cross_forward.1 = (bf16[768,768]{1,0:T(8,128)(2,1)}, bf16[8,1152,1024]{2,1,0:T(8,128)(2,1)}) custom-call(s32[8]{0:T(128)} %lengths.9, bf16[768,768]{1,0:T(8,128)(2,1)} %get-tuple-element.125.side_ref, bf16[8,1024,768]{2,1,0:T(8,128)(2,1)} %get-tuple-element.126.keys_ref, bf16[8,1024,768]{2,1,0:T(8,128)(2,1)} %get-tuple-element.127.values_ref), custom_call_target="tpu_custom_call" | custom-call | flops 9663676416 | bytes 37748736 | tf_op jit(solution)/shard_map/cross_forward/pallas_call | solution.py:341
  143.6 38.1 %feed_both.1 = (bf16[768,768]{1,0:T(8,128)(2,1)}, f32[768,768]{1,0:T(8,128)}, bf16[768,768]{1,0:T(8,128)(2,1)}, f32[1,768]{1,0:T(1,128)}, bf16[32,648,256]{2,1,0:T(8,128)(2,1)}) custom-call(f32[768,768]{1,0:T(8,128)} %get-tuple-element.124.after_ref, bf16[768,768]{1,0:T(8,128)(2,1)} %get-tuple-element.128.context_ref, bf16[768,768]{1,0:T(8,128)(2,1)} %bitcast.250, ...), custom_call_target="tpu_custom_call" | custom-call | flops 21743271936 | bytes 17694720 | tf_op jit(solution)/shard_map/feed_both/pallas_call | solution.py:464
  182.4 31.1 %cross_backward.1 = (bf16[768,768]{1,0:T(8,128)(2,1)}, bf16[8,768,1024]{2,1,0:T(8,128)(2,1)}, bf16[8,768,1024]{2,1,0:T(8,128)(2,1)}) custom-call(s32[8]{0:T(128)} %lengths.9, bf16[768,768]{1,0:T(8,128)(2,1)} %get-tuple-element.131.grad_ref, bf16[768,768]{1,0:T(8,128)(2,1)} %get-tuple-element.128.context_ref, bf16[768,768]{1,0:T(8,128)(2,1)} %get-tuple-element.125.side_ref, ...), custom_call_target="tpu_custom_call" | custom-call | flops 19327352832 | bytes 62914560 | tf_op jit(solution)/shard_map/cross_backward/pallas_call | solution.py:561
  213.5 12.6 %self_output_backward.1 = (f32[768,768]{1,0:T(8,128)}, bf16[768,768]{1,0:T(8,128)(2,1)}, f32[1,768]{1,0:T(1,128)}, bf16[16,144,256]{2,1,0:T(8,128)(2,1)}, bf16[16,144,256]{2,1,0:T(8,128)(2,1)}) custom-call(s32[32]{0:T(128)} %fusion.27.owners.refs_0_, bf16[768,768]{1,0:T(8,128)(2,1)} %get-tuple-element.133.grad_side_ref, ...), custom_call_target="tpu_custom_call" | custom-call | flops 3623878656 | bytes 11796480 | tf_op jit(solution)/shard_map/self_output_backward/pallas_call | solution.py:735
  226.1 30.2 %self_backward.1 = (bf16[768,768]{1,0:T(8,128)(2,1)}, bf16[16,240,256]{2,1,0:T(8,128)(2,1)}, bf16[16,240,256]{2,1,0:T(8,128)(2,1)}) custom-call(s32[32]{0:T(128)} %fusion.27.owners.refs_0_, bf16[768,768]{1,0:T(8,128)(2,1)} %get-tuple-element.137.refs_1_, f32[768,768]{1,0:T(8,128)} %get-tuple-element.138.refs_2_, ...), custom_call_target="tpu_custom_call" | custom-call | flops 14495514624 | bytes 11796480 | tf_op jit(solution)/shard_map/self_backward/pallas_call | solution.py:886
  257.8 3.5 collective-permute-start.29
  262.8 25.2 %memory_weight_grads.1 = (bf16[16,144,256]{2,1,0:T(8,128)(2,1)}, bf16[16,144,256]{2,1,0:T(8,128)(2,1)}) custom-call(s32[8]{0:T(128)} %lengths.9, s32[32]{0:T(128)} %fusion.27.owners.refs_0_, bf16[8,1024,768]{2,1,0:T(8,128)(2,1)} %memory_ref.3, bf16[8,768,1024]{2,1,0:T(8,128)(2,1)} %get-tuple-element.151.grad_keys_ref, ...), custom_call_target="tpu_custom_call" | custom-call | flops 19327352832 | bytes 37748736 | tf_op jit(solution)/shard_map/memory_weight_grads/pallas_call | solution.py:633
  288.1 3.1 add_convert_fusion.1
  291.2 3.2 collective-permute-start.33
  295.9 24.5 %memory_grad.1 = bf16[8,1024,768]{2,1,0:T(8,128)(2,1)} custom-call(s32[8]{0:T(128)} %lengths.9, bf16[8,768,1024]{2,1,0:T(8,128)(2,1)} %get-tuple-element.151.grad_keys_ref, bf16[8,768,1024]{2,1,0:T(8,128)(2,1)} %get-tuple-element.152.grad_values_ref, bf16[768,1536]{1,0:T(8,128)(2,1)} %get-tuple-element.161.weight_ref), custom_call_target="tpu_custom_call" | custom-call | flops 19327352832 | bytes 37748736 | tf_op jit(solution)/shard_map/memory_grad/pallas_call | solution.py:683
  322.2 3.2 collective-permute-start.39
  327.7 1.6 add_convert_fusion
  329.5 4.6 %collective-permute-start.37 = (bf16[384,256]{1,0:T(8,128)(2,1)S(1)}, bf16[384,256]{1,0:T(8,128)(2,1)S(1)}, u32[]{:S(2)}, u32[]{:S(2)}) collective-permute-start(bf16[384,256]{1,0:T(8,128)(2,1)S(1)} %get-tuple-element.193), channel_id=1, source_target_pairs={{0,16},{1,17},{2,18},{3,19},{4,20},{5,21},{6,22},{7,23},{8,24},{9,... | collective-permute-start | bytes 589832 | tf_op jit(solution)/shard_map/ppermute | solution.py:958
  334.0 6.5 %collective-permute-done.40 = bf16[4,144,256]{2,1,0:T(8,128)(2,1)S(1)} collective-permute-done((bf16[4,144,256]{2,1,0:T(8,128)(2,1)S(1)}, bf16[4,144,256]{2,1,0:T(8,128)(2,1)S(1)}, u32[]{:S(2)}, u32[]{:S(2)}) %collective-permute-start.40) | collective-permute-done | bytes 294944 | tf_op jit(solution)/shard_map/ppermute | solution.py:958
  340.9 4.4 %collective-permute-start.43 = (bf16[144,256]{1,0:T(8,128)(2,1)S(1)}, bf16[144,256]{1,0:T(8,128)(2,1)S(1)}, u32[]{:S(2)}, u32[]{:S(2)}) collective-permute-start(bf16[144,256]{1,0:T(8,128)(2,1)S(1)} %get-tuple-element.207), channel_id=1, source_target_pairs={{0,16},{1,17},{2,18},{3,19},{4,20},{5,21},{6,22},{7,23},{8,24},{9,... | collective-permute-start | bytes 221192 | tf_op jit(solution)/shard_map/ppermute | solution.py:958
  345.3 1.6 collective-permute-done.36
  346.9 1.9 collective-permute-start.44
  348.8 10.2 %collective-permute-done.38 = bf16[384,256]{1,0:T(8,128)(2,1)S(1)} collective-permute-done((bf16[384,256]{1,0:T(8,128)(2,1)S(1)}, bf16[384,256]{1,0:T(8,128)(2,1)S(1)}, u32[]{:S(2)}, u32[]{:S(2)}) %collective-permute-start.38) | collective-permute-done | bytes 196640 | tf_op jit(solution)/shard_map/ppermute | solution.py:958
  363.8 1.8 collective-permute-done.44
  (258 shorter events, 45.5 us)
Async XLA Ops:
  7.2 136.4 %all-gather.3.cloned.1.call-start = ((), (), s32[]{:S(2)}) async-start(), calls=%async_computation.2 | async-start | bytes 10948608 | tf_op jit(solution)/shard_map/all_gather | solution.py:942
  21.2 346.4 %reduce-scatter.2.cloned.1.call-start = ((), (), s32[]{:S(2)}) async-start(), calls=%async_computation.1 | async-start | bytes 10948608 | tf_op jit(solution)/shard_map/reduce_scatter | solution.py:948
  22.3 17.9 %collective-permute-start.7 = (bf16[360,256]{1,0:T(8,128)(2,1)S(1)}, bf16[360,256]{1,0:T(8,128)(2,1)S(1)}, u32[]{:S(2)}, u32[]{:S(2)}) collective-permute-start(bf16[360,256]{1,0:T(8,128)(2,1)S(1)} %constant_dynamic-update-slice_fusion), channel_id=1, source_target_pairs={{0,16},{1,17},{2,18},{3,19},{4,20},{5,21},{6,22},{7,23},{8,24},{9,... | collective-permute-start | bytes 552968 | tf_op jit(solution)/shard_map/ppermute | solution.py:958
  24.8 21.3 %collective-permute-start.3 = (bf16[4,160,256]{2,1,0:T(8,128)(2,1)S(1)}, bf16[4,160,256]{2,1,0:T(8,128)(2,1)S(1)}, u32[]{:S(2)}, u32[]{:S(2)}) collective-permute-start(bf16[4,160,256]{2,1,0:T(8,128)(2,1)S(1)} %pad_maximum_fusion.2.refs_0_), channel_id=1, source_target_pairs={{0,1},{1,0},{2,3},{3,2},{4,5},{5,4},{6,7},{7,6},{8,9},{9,8},{10,11... | collective-permute-start | bytes 983048 | tf_op jit(solution)/shard_map/ppermute | solution.py:958
  26.4 19.8 %collective-permute-start.4 = (bf16[4,160,256]{2,1,0:T(8,128)(2,1)S(1)}, bf16[4,160,256]{2,1,0:T(8,128)(2,1)S(1)}, u32[]{:S(2)}, u32[]{:S(2)}) collective-permute-start(bf16[4,160,256]{2,1,0:T(8,128)(2,1)S(1)} %pad_maximum_fusion.2.refs_0_), channel_id=1, source_target_pairs={{0,4},{1,5},{2,6},{3,7},{4,0},{5,1},{6,2},{7,3},{8,12},{9,13},{10,... | collective-permute-start | bytes 983048 | tf_op jit(solution)/shard_map/ppermute | solution.py:958
  27.9 18.3 %collective-permute-start.5 = (bf16[4,160,256]{2,1,0:T(8,128)(2,1)S(1)}, bf16[4,160,256]{2,1,0:T(8,128)(2,1)S(1)}, u32[]{:S(2)}, u32[]{:S(2)}) collective-permute-start(bf16[4,160,256]{2,1,0:T(8,128)(2,1)S(1)} %pad_maximum_fusion.2.refs_0_), channel_id=1, source_target_pairs={{0,5},{1,4},{2,7},{3,6},{4,1},{5,0},{6,3},{7,2},{8,13},{9,12},{10,... | collective-permute-start | bytes 983048 | tf_op jit(solution)/shard_map/ppermute | solution.py:958
  29.9 16.2 %collective-permute-start.8 = (bf16[360,256]{1,0:T(8,128)(2,1)S(1)}, bf16[360,256]{1,0:T(8,128)(2,1)S(1)}, u32[]{:S(2)}, u32[]{:S(2)}) collective-permute-start(bf16[360,256]{1,0:T(8,128)(2,1)S(1)} %constant_dynamic-update-slice_fusion), channel_id=1, source_target_pairs={{0,24},{1,25},{2,26},{3,27},{4,28},{5,29},{6,30},{7,31},{8,16},{9,... | collective-permute-start | bytes 552968 | tf_op jit(solution)/shard_map/ppermute | solution.py:958
  47.4 33.2 %collective-permute-start.10 = (bf16[4,216,256]{2,1,0:T(8,128)(2,1)S(1)}, bf16[4,216,256]{2,1,0:T(8,128)(2,1)}, u32[]{:S(2)}, u32[]{:S(2)}) collective-permute-start(bf16[4,216,256]{2,1,0:T(8,128)(2,1)S(1)} %pad_maximum_fusion.refs_4_), channel_id=1, source_target_pairs={{0,4},{1,5},{2,6},{3,7},{4,0},{5,1},{6,2},{7,3},{8,12},{9,13},{10,... | collective-permute-start | bytes 1327112 | tf_op jit(solution)/shard_map/ppermute | solution.py:958
  50.1 30.5 %collective-permute-start.11 = (bf16[4,216,256]{2,1,0:T(8,128)(2,1)S(1)}, bf16[4,216,256]{2,1,0:T(8,128)(2,1)S(1)}, u32[]{:S(2)}, u32[]{:S(2)}) collective-permute-start(bf16[4,216,256]{2,1,0:T(8,128)(2,1)S(1)} %pad_maximum_fusion.refs_4_), channel_id=1, source_target_pairs={{0,5},{1,4},{2,7},{3,6},{4,1},{5,0},{6,3},{7,2},{8,13},{9,12},{10,... | collective-permute-start | bytes 1327112 | tf_op jit(solution)/shard_map/ppermute | solution.py:958
  51.8 29.2 %collective-permute-start.9 = (bf16[4,216,256]{2,1,0:T(8,128)(2,1)S(1)}, bf16[4,216,256]{2,1,0:T(8,128)(2,1)S(1)}, u32[]{:S(2)}, u32[]{:S(2)}) collective-permute-start(bf16[4,216,256]{2,1,0:T(8,128)(2,1)S(1)} %pad_maximum_fusion.refs_4_), channel_id=1, source_target_pairs={{0,1},{1,0},{2,3},{3,2},{4,5},{5,4},{6,7},{7,6},{8,9},{9,8},{10,11... | collective-permute-start | bytes 1327112 | tf_op jit(solution)/shard_map/ppermute | solution.py:958
  51.9 33.5 %collective-permute-start.19 = (bf16[4,216,256]{2,1,0:T(8,128)(2,1)S(1)}, bf16[4,216,256]{2,1,0:T(8,128)(2,1)}, u32[]{:S(2)}, u32[]{:S(2)}) collective-permute-start(bf16[4,216,256]{2,1,0:T(8,128)(2,1)S(1)} %pad_maximum_fusion.refs_4_), channel_id=1, source_target_pairs={{0,2},{1,3},{2,0},{3,1},{4,6},{5,7},{6,4},{7,5},{8,10},{9,11},{10,... | collective-permute-start | bytes 1327112 | tf_op jit(solution)/shard_map/ppermute | solution.py:958
  82.6 20.7 %collective-permute-start.16 = (bf16[4,144,256]{2,1,0:T(8,128)(2,1)S(1)}, bf16[4,144,256]{2,1,0:T(8,128)(2,1)S(1)}, u32[]{:S(2)}, u32[]{:S(2)}) collective-permute-start(bf16[4,144,256]{2,1,0:T(8,128)(2,1)S(1)} %pad_maximum_fusion.3.refs_4_), channel_id=1, source_target_pairs={{0,1},{1,0},{2,3},{3,2},{4,5},{5,4},{6,7},{7,6},{8,9},{9,8},{10,11... | collective-permute-start | bytes 884744 | tf_op jit(solution)/shard_map/ppermute | solution.py:958
  85.4 17.9 %collective-permute-start.17 = (bf16[4,144,256]{2,1,0:T(8,128)(2,1)S(1)}, bf16[4,144,256]{2,1,0:T(8,128)(2,1)S(1)}, u32[]{:S(2)}, u32[]{:S(2)}) collective-permute-start(bf16[4,144,256]{2,1,0:T(8,128)(2,1)S(1)} %pad_maximum_fusion.3.refs_4_), channel_id=1, source_target_pairs={{0,4},{1,5},{2,6},{3,7},{4,0},{5,1},{6,2},{7,3},{8,12},{9,13},{10,... | collective-permute-start | bytes 884744 | tf_op jit(solution)/shard_map/ppermute | solution.py:958
  85.7 24.6 %collective-permute-start.18 = (bf16[4,144,256]{2,1,0:T(8,128)(2,1)S(1)}, bf16[4,144,256]{2,1,0:T(8,128)(2,1)S(1)}, u32[]{:S(2)}, u32[]{:S(2)}) collective-permute-start(bf16[4,144,256]{2,1,0:T(8,128)(2,1)S(1)} %pad_maximum_fusion.3.refs_4_), channel_id=1, source_target_pairs={{0,5},{1,4},{2,7},{3,6},{4,1},{5,0},{6,3},{7,2},{8,13},{9,12},{10,... | collective-permute-start | bytes 884744 | tf_op jit(solution)/shard_map/ppermute | solution.py:958
  87.0 25.4 %collective-permute-start.23 = (bf16[4,144,256]{2,1,0:T(8,128)(2,1)S(1)}, bf16[4,144,256]{2,1,0:T(8,128)(2,1)S(1)}, u32[]{:S(2)}, u32[]{:S(2)}) collective-permute-start(bf16[4,144,256]{2,1,0:T(8,128)(2,1)S(1)} %pad_maximum_fusion.3.refs_4_), channel_id=1, source_target_pairs={{0,2},{1,3},{2,0},{3,1},{4,6},{5,7},{6,4},{7,5},{8,10},{9,11},{10,... | collective-permute-start | bytes 884744 | tf_op jit(solution)/shard_map/ppermute | solution.py:958
  226.1 30.6 %collective-permute-start.27 = (bf16[16,144,256]{2,1,0:T(8,128)(2,1)}, bf16[16,144,256]{2,1,0:T(8,128)(2,1)S(1)}, u32[]{:S(2)}, u32[]{:S(2)}) collective-permute-start(bf16[16,144,256]{2,1,0:T(8,128)(2,1)} %get-tuple-element.150), channel_id=1, source_target_pairs={{0,2},{1,3},{2,0},{3,1},{4,6},{5,7},{6,4},{7,5},{8,10},{9,11},{10,... | collective-permute-start | bytes 3538952 | tf_op jit(solution)/shard_map/ppermute | solution.py:958
  256.2 31.8 %collective-permute-start.28 = (bf16[16,240,256]{2,1,0:T(8,128)(2,1)}, bf16[16,240,256]{2,1,0:T(8,128)(2,1)}, u32[]{:S(2)}, u32[]{:S(2)}) collective-permute-start(bf16[16,240,256]{2,1,0:T(8,128)(2,1)} %get-tuple-element.156), channel_id=1, source_target_pairs={{0,2},{1,3},{2,0},{3,1},{4,6},{5,7},{6,4},{7,5},{8,10},{9,11},{10,... | collective-permute-start | bytes 5898248 | tf_op jit(solution)/shard_map/ppermute | solution.py:958
  257.8 33.4 %collective-permute-start.29 = (bf16[4,144,256]{2,1,0:T(8,128)(2,1)}, bf16[4,144,256]{2,1,0:T(8,128)(2,1)}, u32[]{:S(2)}, u32[]{:S(2)}) collective-permute-start(bf16[4,144,256]{2,1,0:T(8,128)(2,1)} %get-tuple-element.158), channel_id=1, source_target_pairs={{0,1},{1,0},{2,3},{3,2},{4,5},{5,4},{6,7},{7,6},{8,9},{9,8},{10,11... | collective-permute-start | bytes 884744 | tf_op jit(solution)/shard_map/ppermute | solution.py:958
  261.4 29.8 %collective-permute-start.30 = (bf16[4,144,256]{2,1,0:T(8,128)(2,1)}, bf16[4,144,256]{2,1,0:T(8,128)(2,1)}, u32[]{:S(2)}, u32[]{:S(2)}) collective-permute-start(bf16[4,144,256]{2,1,0:T(8,128)(2,1)} %get-tuple-element.159), channel_id=1, source_target_pairs={{0,4},{1,5},{2,6},{3,7},{4,0},{5,1},{6,2},{7,3},{8,12},{9,13},{10,... | collective-permute-start | bytes 884744 | tf_op jit(solution)/shard_map/ppermute | solution.py:958
  261.4 29.8 %collective-permute-start.31 = (bf16[4,144,256]{2,1,0:T(8,128)(2,1)}, bf16[4,144,256]{2,1,0:T(8,128)(2,1)}, u32[]{:S(2)}, u32[]{:S(2)}) collective-permute-start(bf16[4,144,256]{2,1,0:T(8,128)(2,1)} %get-tuple-element.160), channel_id=1, source_target_pairs={{0,5},{1,4},{2,7},{3,6},{4,1},{5,0},{6,3},{7,2},{8,13},{9,12},{10,... | collective-permute-start | bytes 884744 | tf_op jit(solution)/shard_map/ppermute | solution.py:958
  288.1 33.8 %collective-permute-start.32 = (bf16[16,144,256]{2,1,0:T(8,128)(2,1)}, bf16[16,144,256]{2,1,0:T(8,128)(2,1)S(1)}, u32[]{:S(2)}, u32[]{:S(2)}) collective-permute-start(bf16[16,144,256]{2,1,0:T(8,128)(2,1)} %get-tuple-element.162), channel_id=1, source_target_pairs={{0,2},{1,3},{2,0},{3,1},{4,6},{5,7},{6,4},{7,5},{8,10},{9,11},{10,... | collective-permute-start | bytes 3538952 | tf_op jit(solution)/shard_map/ppermute | solution.py:958
  291.2 34.2 %collective-permute-start.33 = (bf16[4,240,256]{2,1,0:T(8,128)(2,1)}, bf16[4,240,256]{2,1,0:T(8,128)(2,1)}, u32[]{:S(2)}, u32[]{:S(2)}) collective-permute-start(bf16[4,240,256]{2,1,0:T(8,128)(2,1)} %get-tuple-element.165), channel_id=1, source_target_pairs={{0,1},{1,0},{2,3},{3,2},{4,5},{5,4},{6,7},{7,6},{8,9},{9,8},{10,11... | collective-permute-start | bytes 1474568 | tf_op jit(solution)/shard_map/ppermute | solution.py:958
  294.4 33.4 %collective-permute-start.34 = (bf16[4,240,256]{2,1,0:T(8,128)(2,1)}, bf16[4,240,256]{2,1,0:T(8,128)(2,1)}, u32[]{:S(2)}, u32[]{:S(2)}) collective-permute-start(bf16[4,240,256]{2,1,0:T(8,128)(2,1)} %get-tuple-element.166), channel_id=1, source_target_pairs={{0,4},{1,5},{2,6},{3,7},{4,0},{5,1},{6,2},{7,3},{8,12},{9,13},{10,... | collective-permute-start | bytes 1474568 | tf_op jit(solution)/shard_map/ppermute | solution.py:958
  294.4 33.4 %collective-permute-start.35 = (bf16[4,240,256]{2,1,0:T(8,128)(2,1)}, bf16[4,240,256]{2,1,0:T(8,128)(2,1)}, u32[]{:S(2)}, u32[]{:S(2)}) collective-permute-start(bf16[4,240,256]{2,1,0:T(8,128)(2,1)} %get-tuple-element.167), channel_id=1, source_target_pairs={{0,5},{1,4},{2,7},{3,6},{4,1},{5,0},{6,3},{7,2},{8,13},{9,12},{10,... | collective-permute-start | bytes 1474568 | tf_op jit(solution)/shard_map/ppermute | solution.py:958
  325.4 15.2 %collective-permute-start.40 = (bf16[4,144,256]{2,1,0:T(8,128)(2,1)S(1)}, bf16[4,144,256]{2,1,0:T(8,128)(2,1)S(1)}, u32[]{:S(2)}, u32[]{:S(2)}) collective-permute-start(bf16[4,144,256]{2,1,0:T(8,128)(2,1)S(1)} %get-tuple-element.186), channel_id=1, source_target_pairs={{0,4},{1,5},{2,6},{3,7},{4,0},{5,1},{6,2},{7,3},{8,12},{9,13},{10,... | collective-permute-start | bytes 884744 | tf_op jit(solution)/shard_map/ppermute | solution.py:958
  325.4 15.2 %collective-permute-start.41 = (bf16[4,144,256]{2,1,0:T(8,128)(2,1)S(1)}, bf16[4,144,256]{2,1,0:T(8,128)(2,1)S(1)}, u32[]{:S(2)}, u32[]{:S(2)}) collective-permute-start(bf16[4,144,256]{2,1,0:T(8,128)(2,1)S(1)} %get-tuple-element.185), channel_id=1, source_target_pairs={{0,5},{1,4},{2,7},{3,6},{4,1},{5,0},{6,3},{7,2},{8,13},{9,12},{10,... | collective-permute-start | bytes 884744 | tf_op jit(solution)/shard_map/ppermute | solution.py:958
  329.4 17.5 %collective-permute-start.36 = (bf16[384,256]{1,0:T(8,128)(2,1)S(1)}, bf16[384,256]{1,0:T(8,128)(2,1)S(1)}, u32[]{:S(2)}, u32[]{:S(2)}) collective-permute-start(bf16[384,256]{1,0:T(8,128)(2,1)S(1)} %get-tuple-element.191), channel_id=1, source_target_pairs={{0,8},{1,9},{2,10},{3,11},{4,12},{5,13},{6,14},{7,15},{8,0},{9,1},... | collective-permute-start | bytes 589832 | tf_op jit(solution)/shard_map/ppermute | solution.py:958
  329.5 19.3 %collective-permute-start.37 = (bf16[384,256]{1,0:T(8,128)(2,1)S(1)}, bf16[384,256]{1,0:T(8,128)(2,1)S(1)}, u32[]{:S(2)}, u32[]{:S(2)}) collective-permute-start(bf16[384,256]{1,0:T(8,128)(2,1)S(1)} %get-tuple-element.193), channel_id=1, source_target_pairs={{0,16},{1,17},{2,18},{3,19},{4,20},{5,21},{6,22},{7,23},{8,24},{9,... | collective-permute-start | bytes 589832 | tf_op jit(solution)/shard_map/ppermute | solution.py:958
  334.0 25.0 %collective-permute-start.38 = (bf16[384,256]{1,0:T(8,128)(2,1)S(1)}, bf16[384,256]{1,0:T(8,128)(2,1)S(1)}, u32[]{:S(2)}, u32[]{:S(2)}) collective-permute-start(bf16[384,256]{1,0:T(8,128)(2,1)S(1)} %get-tuple-element.192), channel_id=1, source_target_pairs={{0,24},{1,25},{2,26},{3,27},{4,28},{5,29},{6,30},{7,31},{8,16},{9,... | collective-permute-start | bytes 589832 | tf_op jit(solution)/shard_map/ppermute | solution.py:958
  340.8 23.0 %collective-permute-start.42 = (bf16[144,256]{1,0:T(8,128)(2,1)S(1)}, bf16[144,256]{1,0:T(8,128)(2,1)S(1)}, u32[]{:S(2)}, u32[]{:S(2)}) collective-permute-start(bf16[144,256]{1,0:T(8,128)(2,1)S(1)} %get-tuple-element.205), channel_id=1, source_target_pairs={{0,8},{1,9},{2,10},{3,11},{4,12},{5,13},{6,14},{7,15},{8,0},{9,1},... | collective-permute-start | bytes 221192 | tf_op jit(solution)/shard_map/ppermute | solution.py:958
  340.9 23.0 %collective-permute-start.43 = (bf16[144,256]{1,0:T(8,128)(2,1)S(1)}, bf16[144,256]{1,0:T(8,128)(2,1)S(1)}, u32[]{:S(2)}, u32[]{:S(2)}) collective-permute-start(bf16[144,256]{1,0:T(8,128)(2,1)S(1)} %get-tuple-element.207), channel_id=1, source_target_pairs={{0,16},{1,17},{2,18},{3,19},{4,20},{5,21},{6,22},{7,23},{8,24},{9,... | collective-permute-start | bytes 221192 | tf_op jit(solution)/shard_map/ppermute | solution.py:958
  346.9 18.8 %collective-permute-start.44 = (bf16[144,256]{1,0:T(8,128)(2,1)S(1)}, bf16[144,256]{1,0:T(8,128)(2,1)S(1)}, u32[]{:S(2)}, u32[]{:S(2)}) collective-permute-start(bf16[144,256]{1,0:T(8,128)(2,1)S(1)} %get-tuple-element.206), channel_id=1, source_target_pairs={{0,24},{1,25},{2,26},{3,27},{4,28},{5,29},{6,30},{7,31},{8,16},{9,... | collective-permute-start | bytes 221192 | tf_op jit(solution)/shard_map/ppermute | solution.py:958
  (54 other events, 494.1 us)
Sparse Core Ops, SparseCore 0:
  21.4 108.8 all-gather.2
  181.9 185.6 reduce-scatter.1

commit v6 on v5

--- a/solution.py
+++ b/solution.py
@@ -27,8 +27,8 @@
     return lax.dot_general(left_side, right_side, dims, preferred_element_type=f32)
 
 
-def params():
-    return pltpu.CompilerParams(vmem_limit_bytes=60 * 1024 * 1024)
+def params(mebibytes=40):
+    return pltpu.CompilerParams(vmem_limit_bytes=mebibytes * 1024 * 1024)
 
 
 def cost(flops, size, exps=0):
@@ -494,7 +494,7 @@
             pltpu.VMEM((rows, width), f32),
             pltpu.VMEM((rows, width), f32),
         ],
-        compiler_params=params(),
+        compiler_params=params(60),
         cost_estimate=cost(18 * rows * width * steps * lane_tile, 30 * rows * width),
         name="feed_both",
     )(after_self, context, cotangent, gain, packed_feed, packed_feed, packed_feed, packed_feed)

time: 386 us -> 389 us (level)
  waiting for transfers between devices: 49.6 us -> 68.8 us
  Pallas kernels: 233 us -> 216 us
  local copies, waits for them, and re-layouts: 23.1 us -> 38.1 us
  starting transfers between devices: 47.5 us -> 40 us
  other arithmetic: 10 us -> 4.55 us
    unnamed x90 -> x96, local copies, waits for them, and re-layouts: 8.42 us -> 24.6 us
    reduce_scatter x1, waiting for transfers between devices: 0.55 us -> 11.9 us  [scatter(): share = lax.psum_scatter(packed, axes, scatter_dimension=0, tiled=False)]
    ppermute x45, waiting for transfers between devices: 49 us -> 56.8 us  [exchange(): return lax.ppermute(values, axes, [(i, i ^ step) for i in range(32)])]
    ppermute x45, starting transfers between devices: 47.4 us -> 40 us  [exchange(): return lax.ppermute(values, axes, [(i, i ^ step) for i in range(32)])]
    pallas_call x1, Pallas kernels: 12.6 us -> 7.8 us  [self_output_backward(): pl.pallas_call(self_output_kernel, out_shape=[jax.ShapeDtypeStruct((rows,...]
    pallas_call x1, Pallas kernels: 30.2 us -> 25.9 us  [self_backward(): pl.pallas_call(body, out_shape=[jax.ShapeDtypeStruct((rows, width), bf16)...]
    pallas_call x1, Pallas kernels: 16.3 us -> 12.1 us  [self_attend(): pl.pallas_call(body, out_shape=[low] * 5 + [jax.ShapeDtypeStruct((width,...]
  transfers between devices with their start and end apart: 47 -> 47, of which waited for: 13 -> 14; matrix products, arithmetic and copies ran while one was open for 6% -> 5% of each run, Pallas kernels for 51% -> 46%
where the time goes in v6:
time: 389 us; the launch traced here: 384 us
  Pallas kernels  216 us (56%)
  waiting for transfers between devices  68.8 us (18%)
  starting transfers between devices  40 us (10%)
  local copies, waits for them, and re-layouts  38.1 us (10%)
  between operations  15.3 us (4%)
  other arithmetic  4.55 us (1%)
    ppermute x45, waiting for transfers between devices, exchange(): return lax.ppermute(values, axes, [(i, i ^ step) for i in range(32)])  56.8 us
    ppermute x45, starting transfers between devices, exchange(): return lax.ppermute(values, axes, [(i, i ^ step) for i in range(32)])  40 us
    pallas_call x1, Pallas kernels, feed_both(): pl.pallas_call(feed_kernel, out_shape=[jax.ShapeDtypeStruct((rows, width)...  38.1 us
    pallas_call x1, Pallas kernels, cross_backward(): pl.pallas_call(cross_backward_kernel, out_shape=[jax.ShapeDtypeStruct(sid...  31.7 us
    pallas_call x1, Pallas kernels, self_backward(): pl.pallas_call(body, out_shape=[jax.ShapeDtypeStruct((rows, width), bf16)...  25.9 us
    pallas_call x1, Pallas kernels, memory_weight_grads(): pl.pallas_call(memory_weight_kernel, out_shape=[jax.ShapeDtypeStruct(half...  24.7 us
    unnamed x96, local copies, waits for them, and re-layouts  24.6 us
    pallas_call x1, Pallas kernels, project_memory(): pl.pallas_call(memory_kernel, out_shape=[jax.ShapeDtypeStruct(memory.shap...  24.4 us
  transfers between devices with their start and end apart: 47, of which 14 were waited for; matrix products, arithmetic and copies ran while one was open for 5% of the time, Pallas kernels for 46%

profile of v6, /device:TPU:8, one launch (start us, length us, event | category | flops | bytes accessed | tf_op | source)
XLA Modules:
  0.0 383.7 jit_solution(2051650941328832381)
XLA Ops:
  9.8 3.0 collective-permute-start.1
  15.2 3.4 collective-permute-done.1
  18.7 1.8 collective-permute-done.2
  22.3 2.4 collective-permute-start.7
  24.8 1.6 collective-permute-start.3
  30.7 10.4 %collective-permute-done.7 = bf16[360,256]{1,0:T(8,128)(2,1)} collective-permute-done((bf16[360,256]{1,0:T(8,128)(2,1)S(1)}, bf16[360,256]{1,0:T(8,128)(2,1)}, u32[]{:S(2)}, u32[]{:S(2)}) %collective-permute-start.7) | collective-permute-done | bytes 184352 | tf_op jit(solution)/shard_map/ppermute | solution.py:958
  41.1 5.0 %collective-permute-done.8 = bf16[360,256]{1,0:T(8,128)(2,1)S(1)} collective-permute-done((bf16[360,256]{1,0:T(8,128)(2,1)S(1)}, bf16[360,256]{1,0:T(8,128)(2,1)S(1)}, u32[]{:S(2)}, u32[]{:S(2)}) %collective-permute-start.8) | collective-permute-done | bytes 184352 | tf_op jit(solution)/shard_map/ppermute | solution.py:958
  51.8 2.6 collective-permute-start.10
  54.4 1.6 collective-permute-start.11
  56.2 24.4 %memory_project.1 = (bf16[8,1024,768]{2,1,0:T(8,128)(2,1)}, bf16[8,1024,768]{2,1,0:T(8,128)(2,1)}, bf16[768,1536]{1,0:T(8,128)(2,1)S(1)}) custom-call(s32[8]{0:T(128)S(1)} %copy-done.3, s32[32]{0:T(128)S(1)} %fusion.27.owners.refs_0_, bf16[8,1024,768]{2,1,0:T(8,128)(2,1)} %memory_ref.3, bf16[4,160,256]{2,1,0:T(8,128)(2,1)S(1)} %pad_maximum_fusion.2.refs_0_, ...), custom_call_target="tpu_custom_call" | custom-call | flops 19327352832 | bytes 37748736 | tf_op jit(solution)/shard_map/memory_project/pallas_call | solution.py:151
  82.1 2.6 collective-permute-done.9.refs_5_
  90.3 12.1 %self_attend.1 = (bf16[768,768]{1,0:T(8,128)(2,1)S(1)}, bf16[768,768]{1,0:T(8,128)(2,1)S(1)}, bf16[768,768]{1,0:T(8,128)(2,1)S(1)}, bf16[768,768]{1,0:T(8,128)(2...) custom-call(s32[32]{0:T(128)S(1)} %fusion.27.owners.refs_0_, bf16[768,768]{1,0:T(8,128)(2,1)S(1)} %bitcast.175, ...), custom_call_target="tpu_custom_call" | custom-call | flops 7247757312 | bytes 7077888 | tf_op jit(solution)/shard_map/self_attend/pallas_call | solution.py:239
  107.6 8.6 %collective-permute-done.18.refs_7_ = bf16[4,144,256]{2,1,0:T(8,128)(2,1)} collective-permute-done((bf16[4,144,256]{2,1,0:T(8,128)(2,1)S(1)}, bf16[4,144,256]{2,1,0:T(8,128)(2,1)}, u32[]{:S(2)}, u32[]{:S(2)}) %collective-permute-start.18) | collective-permute-done | bytes 294944 | tf_op jit(solution)/shard_map/ppermute | solution.py:958
  120.2 4.3 %self_project.1 = (f32[768,768]{1,0:T(8,128)S(1)}, bf16[768,768]{1,0:T(8,128)(2,1)S(1)}, bf16[768,768]{1,0:T(8,128)(2,1)S(1)}, bf16[768,1536]{1,0:T(8,128)(2,1)S(1)}) custom-call(s32[32]{0:T(128)S(1)} %fusion.27.owners.refs_0_, bf16[768,768]{1,0:T(8,128)(2,1)S(1)} %bitcast.176, bf16[768,768]{1,0:T(8,128)(2,1)S(1)} %copy-done.9, ...), custom_call_target="tpu_custom_call" | custom-call | flops 1811939328 | bytes 7077888 | tf_op jit(solution)/shard_map/self_project/pallas_call | solution.py:278
  128.3 23.1 %cross_forward.1 = (bf16[768,768]{1,0:T(8,128)(2,1)S(1)}, bf16[8,1152,1024]{2,1,0:T(8,128)(2,1)}) custom-call(s32[8]{0:T(128)S(1)} %copy-done.3, bf16[768,768]{1,0:T(8,128)(2,1)S(1)} %get-tuple-element.125.side_ref, bf16[8,1024,768]{2,1,0:T(8,128)(2,1)} %get-tuple-element.126.keys_ref, bf16[8,1024,768]{2,1,0:T(8,128)(2,1)} %get-tuple-element.127.values_ref), custom_call_target="tpu_custom_call" | custom-call | flops 9663676416 | bytes 37748736 | tf_op jit(solution)/shard_map/cross_forward/pallas_call | solution.py:341
  153.5 38.1 %feed_both.1 = (bf16[768,768]{1,0:T(8,128)(2,1)}, f32[768,768]{1,0:T(8,128)}, bf16[768,768]{1,0:T(8,128)(2,1)}, f32[1,768]{1,0:T(1,128)}, bf16[32,648,256]{2,1,0:T(8,128)(2,1)}) custom-call(f32[768,768]{1,0:T(8,128)} %copy-done.4, bf16[768,768]{1,0:T(8,128)(2,1)} %copy-done.15, bf16[768,768]{1,0:T(8,128)(2,1)} %bitcast.253, f32[1,768]{1,0:T(1,128)} %slice.249.gain_ref, ...), custom_call_target="tpu_custom_call" | custom-call | flops 21743271936 | bytes 17694720 | tf_op jit(solution)/shard_map/feed_both/pallas_call | solution.py:464
  196.2 31.7 %cross_backward.1 = (bf16[768,768]{1,0:T(8,128)(2,1)S(1)}, bf16[8,768,1024]{2,1,0:T(8,128)(2,1)}, bf16[8,768,1024]{2,1,0:T(8,128)(2,1)}) custom-call(s32[8]{0:T(128)S(1)} %copy-done.3, bf16[768,768]{1,0:T(8,128)(2,1)S(1)} %copy-done.27, bf16[768,768]{1,0:T(8,128)(2,1)S(1)} %copy-done.16, bf16[768,768]{1,0:T(8,128)(2,1)S(1)} %copy-done.14, ...), custom_call_target="tpu_custom_call" | custom-call | flops 19327352832 | bytes 62914560 | tf_op jit(solution)/shard_map/cross_backward/pallas_call | solution.py:561
  228.1 7.8 %self_output_backward.1 = (f32[768,768]{1,0:T(8,128)S(1)}, bf16[768,768]{1,0:T(8,128)(2,1)S(1)}, f32[1,768]{1,0:T(1,128)S(1)}, bf16[16,144,256]{2,1,0:T(8,128)(2,1)S(1)}, bf16[16,144,256]{2,1,0:T(8,128)(2,1)S(1)}) custom-call(s32[32]{0:T(128)S(1)} %fusion.27.owners.refs_0_, bf16[768,768]{1,0:T(8,128)(2,1)S(1)} %get-tuple-element.133.grad_side_ref, ...), custom_call_target="tpu_custom_call" | custom-call | flops 3623878656 | bytes 11796480 | tf_op jit(solution)/shard_map/self_output_backward/pallas_call | solution.py:735
  236.0 25.9 %self_backward.1 = (bf16[768,768]{1,0:T(8,128)(2,1)}, bf16[16,240,256]{2,1,0:T(8,128)(2,1)S(1)}, bf16[16,240,256]{2,1,0:T(8,128)(2,1)S(1)}) custom-call(s32[32]{0:T(128)S(1)} %fusion.27.owners.refs_0_, bf16[768,768]{1,0:T(8,128)(2,1)S(1)} %get-tuple-element.137.refs_1_, f32[768,768]{1,0:T(8,128)S(1)} %get-tuple-element.138.refs_2_, ...), custom_call_target="tpu_custom_call" | custom-call | flops 14495514624 | bytes 11796480 | tf_op jit(solution)/shard_map/self_backward/pallas_call | solution.py:886
  262.7 2.8 collective-permute-start.29
  267.1 24.7 %memory_weight_grads.1 = (bf16[16,144,256]{2,1,0:T(8,128)(2,1)S(1)}, bf16[16,144,256]{2,1,0:T(8,128)(2,1)S(1)}) custom-call(s32[8]{0:T(128)S(1)} %copy-done.3, s32[32]{0:T(128)S(1)} %fusion.27.owners.refs_0_, bf16[8,1024,768]{2,1,0:T(8,128)(2,1)} %memory_ref.3, bf16[8,768,1024]{2,1,0:T(8,128)(2,1)} %get-tuple-element.151.grad_keys_ref, ...), custom_call_target="tpu_custom_call" | custom-call | flops 19327352832 | bytes 37748736 | tf_op jit(solution)/shard_map/memory_weight_grads/pallas_call | solution.py:633
  292.5 1.8 collective-permute-start.33
  294.3 1.7 collective-permute-start.35
  296.0 24.3 %memory_grad.1 = bf16[8,1024,768]{2,1,0:T(8,128)(2,1)} custom-call(s32[8]{0:T(128)S(1)} %copy-done.3, bf16[8,768,1024]{2,1,0:T(8,128)(2,1)} %get-tuple-element.151.grad_keys_ref, bf16[8,768,1024]{2,1,0:T(8,128)(2,1)} %get-tuple-element.152.grad_values_ref, bf16[768,1536]{1,0:T(8,128)(2,1)S(1)} %copy-done.26), custom_call_target="tpu_custom_call" | custom-call | flops 19327352832 | bytes 37748736 | tf_op jit(solution)/shard_map/memory_grad/pallas_call | solution.py:683
  320.7 1.7 collective-permute-start.39
  322.4 1.8 collective-permute-start.41
  324.7 2.0 collective-permute-start.37
  326.7 3.9 %collective-permute-done.39 = bf16[4,144,256]{2,1,0:T(8,128)(2,1)S(1)} collective-permute-done((bf16[4,144,256]{2,1,0:T(8,128)(2,1)S(1)}, bf16[4,144,256]{2,1,0:T(8,128)(2,1)S(1)}, u32[]{:S(2)}, u32[]{:S(2)}) %collective-permute-start.39) | collective-permute-done | bytes 294944 | tf_op jit(solution)/shard_map/ppermute | solution.py:958
  331.2 9.1 %collective-permute-done.40 = bf16[4,144,256]{2,1,0:T(8,128)(2,1)S(1)} collective-permute-done((bf16[4,144,256]{2,1,0:T(8,128)(2,1)S(1)}, bf16[4,144,256]{2,1,0:T(8,128)(2,1)S(1)}, u32[]{:S(2)}, u32[]{:S(2)}) %collective-permute-start.40) | collective-permute-done | bytes 294944 | tf_op jit(solution)/shard_map/ppermute | solution.py:958
  340.6 2.1 collective-permute-start.43
  344.1 10.4 %collective-permute-done.38 = bf16[384,256]{1,0:T(8,128)(2,1)S(1)} collective-permute-done((bf16[384,256]{1,0:T(8,128)(2,1)S(1)}, bf16[384,256]{1,0:T(8,128)(2,1)S(1)}, u32[]{:S(2)}, u32[]{:S(2)}) %collective-permute-start.38) | collective-permute-done | bytes 196640 | tf_op jit(solution)/shard_map/ppermute | solution.py:958
  360.8 11.9 %reduce-scatter.2.cloned.1.call-done = bf16[1,648,256]{2,1,0:T(8,128)(2,1)} async-done(((bf16[32,648,256]{2,1,0:T(8,128)(2,1)}), bf16[1,648,256]{2,1,0:T(8,128)(2,1)}) %reduce-scatter.2.cloned.1.call-update) | async-done | bytes 331792 | tf_op jit(solution)/shard_map/reduce_scatter | solution.py:948
  (261 shorter events, 59.6 us)
Async XLA Ops:
  7.2 146.3 %all-gather.3.cloned.1.call-start = ((), (), s32[]{:S(2)}) async-start(), calls=%async_computation.2 | async-start | bytes 10948608 | tf_op jit(solution)/shard_map/all_gather | solution.py:942
  21.2 351.4 %reduce-scatter.2.cloned.1.call-start = ((), (), s32[]{:S(2)}) async-start(), calls=%async_computation.1 | async-start | bytes 10948608 | tf_op jit(solution)/shard_map/reduce_scatter | solution.py:948
  22.3 18.9 %collective-permute-start.7 = (bf16[360,256]{1,0:T(8,128)(2,1)S(1)}, bf16[360,256]{1,0:T(8,128)(2,1)}, u32[]{:S(2)}, u32[]{:S(2)}) collective-permute-start(bf16[360,256]{1,0:T(8,128)(2,1)S(1)} %constant_dynamic-update-slice_fusion), channel_id=1, source_target_pairs={{0,16},{1,17},{2,18},{3,19},{4,20},{5,21},{6,22},{7,23},{8,24},{9,... | collective-permute-start | bytes 552968 | tf_op jit(solution)/shard_map/ppermute | solution.py:958
  24.8 21.3 %collective-permute-start.3 = (bf16[4,160,256]{2,1,0:T(8,128)(2,1)S(1)}, bf16[4,160,256]{2,1,0:T(8,128)(2,1)S(1)}, u32[]{:S(2)}, u32[]{:S(2)}) collective-permute-start(bf16[4,160,256]{2,1,0:T(8,128)(2,1)S(1)} %pad_maximum_fusion.2.refs_0_), channel_id=1, source_target_pairs={{0,1},{1,0},{2,3},{3,2},{4,5},{5,4},{6,7},{7,6},{8,9},{9,8},{10,11... | collective-permute-start | bytes 983048 | tf_op jit(solution)/shard_map/ppermute | solution.py:958
  26.3 19.8 %collective-permute-start.4 = (bf16[4,160,256]{2,1,0:T(8,128)(2,1)S(1)}, bf16[4,160,256]{2,1,0:T(8,128)(2,1)S(1)}, u32[]{:S(2)}, u32[]{:S(2)}) collective-permute-start(bf16[4,160,256]{2,1,0:T(8,128)(2,1)S(1)} %pad_maximum_fusion.2.refs_0_), channel_id=1, source_target_pairs={{0,4},{1,5},{2,6},{3,7},{4,0},{5,1},{6,2},{7,3},{8,12},{9,13},{10,... | collective-permute-start | bytes 983048 | tf_op jit(solution)/shard_map/ppermute | solution.py:958
  27.9 18.3 %collective-permute-start.5 = (bf16[4,160,256]{2,1,0:T(8,128)(2,1)S(1)}, bf16[4,160,256]{2,1,0:T(8,128)(2,1)S(1)}, u32[]{:S(2)}, u32[]{:S(2)}) collective-permute-start(bf16[4,160,256]{2,1,0:T(8,128)(2,1)S(1)} %pad_maximum_fusion.2.refs_0_), channel_id=1, source_target_pairs={{0,5},{1,4},{2,7},{3,6},{4,1},{5,0},{6,3},{7,2},{8,13},{9,12},{10,... | collective-permute-start | bytes 983048 | tf_op jit(solution)/shard_map/ppermute | solution.py:958
  29.2 16.9 %collective-permute-start.8 = (bf16[360,256]{1,0:T(8,128)(2,1)S(1)}, bf16[360,256]{1,0:T(8,128)(2,1)S(1)}, u32[]{:S(2)}, u32[]{:S(2)}) collective-permute-start(bf16[360,256]{1,0:T(8,128)(2,1)S(1)} %constant_dynamic-update-slice_fusion), channel_id=1, source_target_pairs={{0,24},{1,25},{2,26},{3,27},{4,28},{5,29},{6,30},{7,31},{8,16},{9,... | collective-permute-start | bytes 552968 | tf_op jit(solution)/shard_map/ppermute | solution.py:958
  51.8 30.4 %collective-permute-start.10 = (bf16[4,216,256]{2,1,0:T(8,128)(2,1)S(1)}, bf16[4,216,256]{2,1,0:T(8,128)(2,1)}, u32[]{:S(2)}, u32[]{:S(2)}) collective-permute-start(bf16[4,216,256]{2,1,0:T(8,128)(2,1)S(1)} %pad_maximum_fusion.refs_4_), channel_id=1, source_target_pairs={{0,4},{1,5},{2,6},{3,7},{4,0},{5,1},{6,2},{7,3},{8,12},{9,13},{10,... | collective-permute-start | bytes 1327112 | tf_op jit(solution)/shard_map/ppermute | solution.py:958
  54.4 27.7 %collective-permute-start.11 = (bf16[4,216,256]{2,1,0:T(8,128)(2,1)S(1)}, bf16[4,216,256]{2,1,0:T(8,128)(2,1)}, u32[]{:S(2)}, u32[]{:S(2)}) collective-permute-start(bf16[4,216,256]{2,1,0:T(8,128)(2,1)S(1)} %pad_maximum_fusion.refs_4_), channel_id=1, source_target_pairs={{0,5},{1,4},{2,7},{3,6},{4,1},{5,0},{6,3},{7,2},{8,13},{9,12},{10,... | collective-permute-start | bytes 1327112 | tf_op jit(solution)/shard_map/ppermute | solution.py:958
  56.0 28.7 %collective-permute-start.9 = (bf16[4,216,256]{2,1,0:T(8,128)(2,1)S(1)}, bf16[4,216,256]{2,1,0:T(8,128)(2,1)}, u32[]{:S(2)}, u32[]{:S(2)}) collective-permute-start(bf16[4,216,256]{2,1,0:T(8,128)(2,1)S(1)} %pad_maximum_fusion.refs_4_), channel_id=1, source_target_pairs={{0,1},{1,0},{2,3},{3,2},{4,5},{5,4},{6,7},{7,6},{8,9},{9,8},{10,11... | collective-permute-start | bytes 1327112 | tf_op jit(solution)/shard_map/ppermute | solution.py:958
  56.1 31.2 %collective-permute-start.19 = (bf16[4,216,256]{2,1,0:T(8,128)(2,1)S(1)}, bf16[4,216,256]{2,1,0:T(8,128)(2,1)}, u32[]{:S(2)}, u32[]{:S(2)}) collective-permute-start(bf16[4,216,256]{2,1,0:T(8,128)(2,1)S(1)} %pad_maximum_fusion.refs_4_), channel_id=1, source_target_pairs={{0,2},{1,3},{2,0},{3,1},{4,6},{5,7},{6,4},{7,5},{8,10},{9,11},{10,... | collective-permute-start | bytes 1327112 | tf_op jit(solution)/shard_map/ppermute | solution.py:958
  86.7 20.9 %collective-permute-start.16 = (bf16[4,144,256]{2,1,0:T(8,128)(2,1)S(1)}, bf16[4,144,256]{2,1,0:T(8,128)(2,1)}, u32[]{:S(2)}, u32[]{:S(2)}) collective-permute-start(bf16[4,144,256]{2,1,0:T(8,128)(2,1)S(1)} %pad_maximum_fusion.3.refs_4_), channel_id=1, source_target_pairs={{0,1},{1,0},{2,3},{3,2},{4,5},{5,4},{6,7},{7,6},{8,9},{9,8},{10,11... | collective-permute-start | bytes 884744 | tf_op jit(solution)/shard_map/ppermute | solution.py:958
  87.3 20.3 %collective-permute-start.17 = (bf16[4,144,256]{2,1,0:T(8,128)(2,1)S(1)}, bf16[4,144,256]{2,1,0:T(8,128)(2,1)}, u32[]{:S(2)}, u32[]{:S(2)}) collective-permute-start(bf16[4,144,256]{2,1,0:T(8,128)(2,1)S(1)} %pad_maximum_fusion.3.refs_4_), channel_id=1, source_target_pairs={{0,4},{1,5},{2,6},{3,7},{4,0},{5,1},{6,2},{7,3},{8,12},{9,13},{10,... | collective-permute-start | bytes 884744 | tf_op jit(solution)/shard_map/ppermute | solution.py:958
  88.8 27.4 %collective-permute-start.18 = (bf16[4,144,256]{2,1,0:T(8,128)(2,1)S(1)}, bf16[4,144,256]{2,1,0:T(8,128)(2,1)}, u32[]{:S(2)}, u32[]{:S(2)}) collective-permute-start(bf16[4,144,256]{2,1,0:T(8,128)(2,1)S(1)} %pad_maximum_fusion.3.refs_4_), channel_id=1, source_target_pairs={{0,5},{1,4},{2,7},{3,6},{4,1},{5,0},{6,3},{7,2},{8,13},{9,12},{10,... | collective-permute-start | bytes 884744 | tf_op jit(solution)/shard_map/ppermute | solution.py:958
  90.2 27.4 %collective-permute-start.23 = (bf16[4,144,256]{2,1,0:T(8,128)(2,1)S(1)}, bf16[4,144,256]{2,1,0:T(8,128)(2,1)}, u32[]{:S(2)}, u32[]{:S(2)}) collective-permute-start(bf16[4,144,256]{2,1,0:T(8,128)(2,1)S(1)} %pad_maximum_fusion.3.refs_4_), channel_id=1, source_target_pairs={{0,2},{1,3},{2,0},{3,1},{4,6},{5,7},{6,4},{7,5},{8,10},{9,11},{10,... | collective-permute-start | bytes 884744 | tf_op jit(solution)/shard_map/ppermute | solution.py:958
  235.9 26.5 %collective-permute-start.27 = (bf16[16,144,256]{2,1,0:T(8,128)(2,1)S(1)}, bf16[16,144,256]{2,1,0:T(8,128)(2,1)S(1)}, u32[]{:S(2)}, u32[]{:S(2)}) collective-permute-start(bf16[16,144,256]{2,1,0:T(8,128)(2,1)S(1)} %get-tuple-element.150), channel_id=1, source_target_pairs={{0,2},{1,3},{2,0},{3,1},{4,6},{5,7},{6,4},{7,5},{8,10},{9,11},{10,... | collective-permute-start | bytes 3538952 | tf_op jit(solution)/shard_map/ppermute | solution.py:958
  261.9 30.0 %collective-permute-start.28 = (bf16[16,240,256]{2,1,0:T(8,128)(2,1)S(1)}, bf16[16,240,256]{2,1,0:T(8,128)(2,1)S(1)}, u32[]{:S(2)}, u32[]{:S(2)}) collective-permute-start(bf16[16,240,256]{2,1,0:T(8,128)(2,1)S(1)} %get-tuple-element.156), channel_id=1, source_target_pairs={{0,2},{1,3},{2,0},{3,1},{4,6},{5,7},{6,4},{7,5},{8,10},{9,11},{10,... | collective-permute-start | bytes 5898248 | tf_op jit(solution)/shard_map/ppermute | solution.py:958
  262.7 29.7 %collective-permute-start.29 = (bf16[4,144,256]{2,1,0:T(8,128)(2,1)S(1)}, bf16[4,144,256]{2,1,0:T(8,128)(2,1)S(1)}, u32[]{:S(2)}, u32[]{:S(2)}) collective-permute-start(bf16[4,144,256]{2,1,0:T(8,128)(2,1)S(1)} %get-tuple-element.158), channel_id=1, source_target_pairs={{0,1},{1,0},{2,3},{3,2},{4,5},{5,4},{6,7},{7,6},{8,9},{9,8},{10,11... | collective-permute-start | bytes 884744 | tf_op jit(solution)/shard_map/ppermute | solution.py:958
  265.5 26.9 %collective-permute-start.30 = (bf16[4,144,256]{2,1,0:T(8,128)(2,1)S(1)}, bf16[4,144,256]{2,1,0:T(8,128)(2,1)S(1)}, u32[]{:S(2)}, u32[]{:S(2)}) collective-permute-start(bf16[4,144,256]{2,1,0:T(8,128)(2,1)S(1)} %get-tuple-element.159), channel_id=1, source_target_pairs={{0,4},{1,5},{2,6},{3,7},{4,0},{5,1},{6,2},{7,3},{8,12},{9,13},{10,... | collective-permute-start | bytes 884744 | tf_op jit(solution)/shard_map/ppermute | solution.py:958
  265.5 26.9 %collective-permute-start.31 = (bf16[4,144,256]{2,1,0:T(8,128)(2,1)S(1)}, bf16[4,144,256]{2,1,0:T(8,128)(2,1)S(1)}, u32[]{:S(2)}, u32[]{:S(2)}) collective-permute-start(bf16[4,144,256]{2,1,0:T(8,128)(2,1)S(1)} %get-tuple-element.160), channel_id=1, source_target_pairs={{0,5},{1,4},{2,7},{3,6},{4,1},{5,0},{6,3},{7,2},{8,13},{9,12},{10,... | collective-permute-start | bytes 884744 | tf_op jit(solution)/shard_map/ppermute | solution.py:958
  291.8 28.7 %collective-permute-start.32 = (bf16[16,144,256]{2,1,0:T(8,128)(2,1)S(1)}, bf16[16,144,256]{2,1,0:T(8,128)(2,1)S(1)}, u32[]{:S(2)}, u32[]{:S(2)}) collective-permute-start(bf16[16,144,256]{2,1,0:T(8,128)(2,1)S(1)} %get-tuple-element.162), channel_id=1, source_target_pairs={{0,2},{1,3},{2,0},{3,1},{4,6},{5,7},{6,4},{7,5},{8,10},{9,11},{10,... | collective-permute-start | bytes 3538952 | tf_op jit(solution)/shard_map/ppermute | solution.py:958
  292.5 29.9 %collective-permute-start.33 = (bf16[4,240,256]{2,1,0:T(8,128)(2,1)S(1)}, bf16[4,240,256]{2,1,0:T(8,128)(2,1)S(1)}, u32[]{:S(2)}, u32[]{:S(2)}) collective-permute-start(bf16[4,240,256]{2,1,0:T(8,128)(2,1)S(1)} %get-tuple-element.165), channel_id=1, source_target_pairs={{0,1},{1,0},{2,3},{3,2},{4,5},{5,4},{6,7},{7,6},{8,9},{9,8},{10,11... | collective-permute-start | bytes 1474568 | tf_op jit(solution)/shard_map/ppermute | solution.py:958
  294.3 30.0 %collective-permute-start.34 = (bf16[4,240,256]{2,1,0:T(8,128)(2,1)S(1)}, bf16[4,240,256]{2,1,0:T(8,128)(2,1)S(1)}, u32[]{:S(2)}, u32[]{:S(2)}) collective-permute-start(bf16[4,240,256]{2,1,0:T(8,128)(2,1)S(1)} %get-tuple-element.166), channel_id=1, source_target_pairs={{0,4},{1,5},{2,6},{3,7},{4,0},{5,1},{6,2},{7,3},{8,12},{9,13},{10,... | collective-permute-start | bytes 1474568 | tf_op jit(solution)/shard_map/ppermute | solution.py:958
  294.3 30.0 %collective-permute-start.35 = (bf16[4,240,256]{2,1,0:T(8,128)(2,1)S(1)}, bf16[4,240,256]{2,1,0:T(8,128)(2,1)S(1)}, u32[]{:S(2)}, u32[]{:S(2)}) collective-permute-start(bf16[4,240,256]{2,1,0:T(8,128)(2,1)S(1)} %get-tuple-element.167), channel_id=1, source_target_pairs={{0,5},{1,4},{2,7},{3,6},{4,1},{5,0},{6,3},{7,2},{8,13},{9,12},{10,... | collective-permute-start | bytes 1474568 | tf_op jit(solution)/shard_map/ppermute | solution.py:958
  322.4 17.9 %collective-permute-start.40 = (bf16[4,144,256]{2,1,0:T(8,128)(2,1)S(1)}, bf16[4,144,256]{2,1,0:T(8,128)(2,1)S(1)}, u32[]{:S(2)}, u32[]{:S(2)}) collective-permute-start(bf16[4,144,256]{2,1,0:T(8,128)(2,1)S(1)} %get-tuple-element.186), channel_id=1, source_target_pairs={{0,4},{1,5},{2,6},{3,7},{4,0},{5,1},{6,2},{7,3},{8,12},{9,13},{10,... | collective-permute-start | bytes 884744 | tf_op jit(solution)/shard_map/ppermute | solution.py:958
  322.4 17.9 %collective-permute-start.41 = (bf16[4,144,256]{2,1,0:T(8,128)(2,1)S(1)}, bf16[4,144,256]{2,1,0:T(8,128)(2,1)S(1)}, u32[]{:S(2)}, u32[]{:S(2)}) collective-permute-start(bf16[4,144,256]{2,1,0:T(8,128)(2,1)S(1)} %get-tuple-element.185), channel_id=1, source_target_pairs={{0,5},{1,4},{2,7},{3,6},{4,1},{5,0},{6,3},{7,2},{8,13},{9,12},{10,... | collective-permute-start | bytes 884744 | tf_op jit(solution)/shard_map/ppermute | solution.py:958
  324.6 18.1 %collective-permute-start.36 = (bf16[384,256]{1,0:T(8,128)(2,1)S(1)}, bf16[384,256]{1,0:T(8,128)(2,1)S(1)}, u32[]{:S(2)}, u32[]{:S(2)}) collective-permute-start(bf16[384,256]{1,0:T(8,128)(2,1)S(1)} %get-tuple-element.191), channel_id=1, source_target_pairs={{0,8},{1,9},{2,10},{3,11},{4,12},{5,13},{6,14},{7,15},{8,0},{9,1},... | collective-permute-start | bytes 589832 | tf_op jit(solution)/shard_map/ppermute | solution.py:958
  324.7 19.4 %collective-permute-start.37 = (bf16[384,256]{1,0:T(8,128)(2,1)S(1)}, bf16[384,256]{1,0:T(8,128)(2,1)S(1)}, u32[]{:S(2)}, u32[]{:S(2)}) collective-permute-start(bf16[384,256]{1,0:T(8,128)(2,1)S(1)} %get-tuple-element.193), channel_id=1, source_target_pairs={{0,16},{1,17},{2,18},{3,19},{4,20},{5,21},{6,22},{7,23},{8,24},{9,... | collective-permute-start | bytes 589832 | tf_op jit(solution)/shard_map/ppermute | solution.py:958
  330.7 23.8 %collective-permute-start.38 = (bf16[384,256]{1,0:T(8,128)(2,1)S(1)}, bf16[384,256]{1,0:T(8,128)(2,1)S(1)}, u32[]{:S(2)}, u32[]{:S(2)}) collective-permute-start(bf16[384,256]{1,0:T(8,128)(2,1)S(1)} %get-tuple-element.192), channel_id=1, source_target_pairs={{0,24},{1,25},{2,26},{3,27},{4,28},{5,29},{6,30},{7,31},{8,16},{9,... | collective-permute-start | bytes 589832 | tf_op jit(solution)/shard_map/ppermute | solution.py:958
  340.5 18.8 %collective-permute-start.42 = (bf16[144,256]{1,0:T(8,128)(2,1)S(1)}, bf16[144,256]{1,0:T(8,128)(2,1)S(1)}, u32[]{:S(2)}, u32[]{:S(2)}) collective-permute-start(bf16[144,256]{1,0:T(8,128)(2,1)S(1)} %get-tuple-element.205), channel_id=1, source_target_pairs={{0,8},{1,9},{2,10},{3,11},{4,12},{5,13},{6,14},{7,15},{8,0},{9,1},... | collective-permute-start | bytes 221192 | tf_op jit(solution)/shard_map/ppermute | solution.py:958
  340.6 18.7 %collective-permute-start.43 = (bf16[144,256]{1,0:T(8,128)(2,1)S(1)}, bf16[144,256]{1,0:T(8,128)(2,1)S(1)}, u32[]{:S(2)}, u32[]{:S(2)}) collective-permute-start(bf16[144,256]{1,0:T(8,128)(2,1)S(1)} %get-tuple-element.207), channel_id=1, source_target_pairs={{0,16},{1,17},{2,18},{3,19},{4,20},{5,21},{6,22},{7,23},{8,24},{9,... | collective-permute-start | bytes 221192 | tf_op jit(solution)/shard_map/ppermute | solution.py:958
  342.7 16.6 %collective-permute-start.44 = (bf16[144,256]{1,0:T(8,128)(2,1)S(1)}, bf16[144,256]{1,0:T(8,128)(2,1)S(1)}, u32[]{:S(2)}, u32[]{:S(2)}) collective-permute-start(bf16[144,256]{1,0:T(8,128)(2,1)S(1)} %get-tuple-element.206), channel_id=1, source_target_pairs={{0,24},{1,25},{2,26},{3,27},{4,28},{5,29},{6,30},{7,31},{8,16},{9,... | collective-permute-start | bytes 221192 | tf_op jit(solution)/shard_map/ppermute | solution.py:958
  (54 other events, 437.9 us)
Sparse Core Ops, SparseCore 0:
  21.4 112.3 all-gather.2
  191.7 180.8 reduce-scatter.1
